TPU v7x, 32 devices: a whole 2x2x4 slice. The times are simulated.
32 devices in a mesh: context: 8 (over y, x, core), tensor: 4 (over z).
Axes of the slice: x: 2, y: 2, z: 4, core: 2. Of those that a mesh axis runs over, the one named last changes fastest.
Arguments:
- inputs: bfloat16 [2048, 8192], P('context', 'tensor'), may hold values from -6 to 6
- step_size: float32 [128, 2048], P('tensor', 'context'), as said below
- decay_rate: float32 [128], P('tensor'), as said below
- skip: float32 [128], P('tensor'), may hold values from 0.5 to 1.5
- b_in: bfloat16 [2048, 128], P('context'), may hold values from -1.796875 to 1.796875
- c_in: bfloat16 [2048, 128], P('context'), may hold values from -1.796875 to 1.796875
- doc_start: int32 [2048], P('context'), may hold values 0 or 1
- cotangent: bfloat16 [2048, 8192], P('context', 'tensor'), may hold values from -6 to 6
Outputs:
- mixed: bfloat16 [2048, 8192], P('context', 'tensor')
- grad_inputs: bfloat16 [2048, 8192], P('context', 'tensor')
- grad_b: bfloat16 [2048, 128], P('context')
- grad_c: bfloat16 [2048, 128], P('context')
Inputs may be any that keep to these rules, and one draw needn't show every extreme that they name: `step_size`: positive. `decay_rate`: positive. `doc_start`: a 1 marks the first token of a document; the state before the first token is zero.
All inputs are finite; a program needn't handle non-finite values. No bound on the sum of `doc_start` on one device may be relied on, other than what follows from the above.
Results may differ from a plain program's by a relative error of at most 0.001.
Values may be sent and summed in bfloat16 or wider, within the bound.
No kernel may reach another device: no remote copies, remote signals or barrier semaphores. Data moves between devices by JAX's collectives and lax.ppermute only.
A program may use at most 128 MiB of HBM per device.

v0:
```python
import jax
import jax.numpy as jnp
from jax import lax
from jax.sharding import PartitionSpec as P

BLOCK = 128


HIGH = lax.Precision.HIGHEST


def entering_2(value, axis, combine, identity, reverse):
    size, index = (lax.axis_size(axis), lax.axis_index(axis))
    everything = jax.tree.map(lambda part: lax.all_gather(part, axis), value)
    start = jax.tree.map(
        lambda part, zero: jnp.broadcast_to(jnp.asarray(zero, part.dtype), part.shape),
        value,
        identity,
    )

    def hop(k, before):
        at = size - 1 - k if reverse else k
        reached = at > index if reverse else at < index
        new = combine(before, jax.tree.map(lambda part: part[at], everything))
        return jax.tree.map(lambda a, b: jnp.where(reached, a, b), new, before)

    return lax.fori_loop(0, size, hop, start)


def contract(spec, *operands):
    return jnp.einsum(spec, *operands, precision=HIGH)


def compose(earlier, later):
    return (earlier[0] * later[0], later[0][:, None, None] * earlier[1] + later[1])


def carry_forward(element, identity):
    return entering_2(element, "context", compose, identity, False)


def carry_backward(element, identity):
    return entering_2(element, "context", compose, identity, True)


def forward_blocks(
    values,
    b_half,
    c_half,
    b_float,
    c_float,
    step_size,
    decay_sum,
    doc_count,
    skip,
    entering,
    block_rows,
):
    head_count = values.shape[0]
    tok_count = values.shape[1]
    carried = entering
    prev_sum = jnp.zeros((head_count,), jnp.float32)
    prev_count = jnp.zeros((), jnp.int32)
    order = jnp.arange(block_rows)
    outputs = []
    saved = []
    for number in range(tok_count // block_rows):
        first_row = number * block_rows
        rows = slice(first_row, first_row + block_rows)
        value_blk = values[:, rows].astype(jnp.float32)
        b_blk = b_float[rows]
        c_blk = c_float[rows]
        step_blk = step_size[:, rows]
        sum_blk = decay_sum[:, rows]
        count_blk = doc_count[rows]
        mask = (order[:, None] >= order[None, :]) & (count_blk[:, None] == count_blk[None, :])
        spread = sum_blk[:, :, None] - sum_blk[:, None, :]
        weights = jnp.where(mask[None], jnp.exp(jnp.minimum(spread, 0.0)), 0.0)
        intersection = jnp.dot(c_half[rows], b_half[rows].T, preferred_element_type=jnp.float32)
        scores = weights * intersection[None] * step_blk[:, None, :]
        carry_keep = (
            jnp.exp(sum_blk - prev_sum[:, None])
            * (count_blk == prev_count).astype(jnp.float32)[None, :]
        )
        result = contract("hts,hsp->htp", scores, value_blk)
        result = result + carry_keep[:, :, None] * contract("tn,hpn->htp", c_blk, carried)
        result = result + skip[:, None, None] * value_blk
        end_weight = (
            jnp.exp(sum_blk[:, -1:] - sum_blk)
            * (count_blk == count_blk[-1]).astype(jnp.float32)[None, :]
            * step_blk
        )
        saved.append((weights, intersection, carry_keep, end_weight, carried))
        carried = carry_keep[:, -1][:, None, None] * carried + contract(
            "hs,hsp,sn->hpn", end_weight, value_blk, b_blk
        )
        prev_sum = sum_blk[:, -1]
        prev_count = count_blk[-1]
        outputs.append(result)
    return (jnp.concatenate(outputs, axis=1), saved)


def backward_blocks(
    values, grads_half, b_float, c_float, step_size, skip, saved, leaving, block_rows
):
    tok_count = values.shape[1]
    arriving = leaving
    grad_vals = []
    grad_bs = []
    grad_cs = []
    for number in reversed(range(tok_count // block_rows)):
        first_row = number * block_rows
        rows = slice(first_row, first_row + block_rows)
        value_half = values[:, rows]
        grad_half = grads_half[:, rows]
        value_blk = value_half.astype(jnp.float32)
        grad_blk = grad_half.astype(jnp.float32)
        b_blk = b_float[rows]
        c_blk = c_float[rows]
        step_blk = step_size[:, rows]
        weights, intersection, carry_keep, end_weight, carried = saved[number]
        scores = weights * intersection[None] * step_blk[:, None, :]
        inner = jnp.einsum(
            "htp,hsp->hts", grad_half, value_half, preferred_element_type=jnp.float32
        )
        common = jnp.sum(weights * inner * step_blk[:, None, :], axis=0)
        grad_c_blk = jnp.dot(common, b_blk, precision=HIGH) + contract(
            "ht,htp,hpn->tn", carry_keep, grad_blk, carried
        )
        grad_b_blk = jnp.dot(common.T, c_blk, precision=HIGH) + contract(
            "hs,hsp,hpn->sn", end_weight, value_blk, arriving
        )
        grad_val_blk = contract("hts,htp->hsp", scores, grad_blk)
        grad_val_blk = grad_val_blk + end_weight[:, :, None] * contract(
            "hpn,sn->hsp", arriving, b_blk
        )
        grad_val_blk = grad_val_blk + skip[:, None, None] * grad_blk
        arriving = carry_keep[:, -1][:, None, None] * arriving + contract(
            "ht,htp,tn->hpn", carry_keep, grad_blk, c_blk
        )
        grad_vals.insert(0, grad_val_blk)
        grad_bs.insert(0, grad_b_blk)
        grad_cs.insert(0, grad_c_blk)
    return (
        jnp.concatenate(grad_vals, axis=1),
        jnp.concatenate(grad_bs, axis=0),
        jnp.concatenate(grad_cs, axis=0),
    )


def shards(inputs, step_size, decay_rate, skip, b_in, c_in, doc_start, cotangent):
    head_count = step_size.shape[0]
    tok_count = step_size.shape[1]
    head_width = inputs.shape[1] // head_count
    state_width = b_in.shape[1]
    block_rows = min(BLOCK, tok_count)
    values = inputs.reshape(tok_count, head_count, head_width).transpose(1, 0, 2)
    grads_half = cotangent.reshape(tok_count, head_count, head_width).transpose(1, 0, 2)
    b_float = b_in.astype(jnp.float32)
    c_float = c_in.astype(jnp.float32)
    log_decay = -step_size * decay_rate[:, None]
    decay_sum = jnp.cumsum(log_decay, axis=1)
    doc_count = jnp.cumsum(doc_start)
    keep_end = (doc_count == doc_count[-1]).astype(jnp.float32)
    end_weight = jnp.exp(decay_sum[:, -1:] - decay_sum) * keep_end[None, :] * step_size
    own_state = jnp.einsum(
        "hs,hsp,sn->hpn", end_weight, values.astype(jnp.float32), b_float, precision=HIGH
    )
    piece_decay = jnp.exp(decay_sum[:, -1]) * (doc_count[-1] == 0).astype(jnp.float32)
    start_weight = jnp.exp(decay_sum) * (doc_count == 0).astype(jnp.float32)[None, :]
    own_grad = jnp.einsum(
        "ht,htp,tn->hpn", start_weight, grads_half.astype(jnp.float32), c_float, precision=HIGH
    )
    identity = (
        jnp.ones((head_count,), jnp.float32),
        jnp.zeros((head_count, head_width, state_width), jnp.float32),
    )
    entering = carry_forward((piece_decay, own_state), identity)[1]
    result, saved = forward_blocks(
        values,
        b_in,
        c_in,
        b_float,
        c_float,
        step_size,
        decay_sum,
        doc_count,
        skip,
        entering,
        block_rows,
    )
    leaving = carry_backward((piece_decay, own_grad), identity)[1]
    grad_vals, grad_b_part, grad_c_part = backward_blocks(
        values, grads_half, b_float, c_float, step_size, skip, saved, leaving, block_rows
    )
    total_b, total_c = lax.psum((grad_b_part, grad_c_part), "tensor")
    grad_b = total_b.astype(jnp.bfloat16)
    grad_c = total_c.astype(jnp.bfloat16)
    mixed = (
        result.transpose(1, 0, 2).reshape(tok_count, head_count * head_width).astype(jnp.bfloat16)
    )
    grad_inputs = (
        grad_vals.transpose(1, 0, 2)
        .reshape(tok_count, head_count * head_width)
        .astype(jnp.bfloat16)
    )
    return (mixed, grad_inputs, grad_b, grad_c)


def solution(mesh):
    in_specs = (
        P("context", "tensor"),
        P("tensor", "context"),
        P("tensor"),
        P("tensor"),
        P("context", None),
        P("context", None),
        P("context"),
        P("context", "tensor"),
    )
    out_specs = (
        P("context", "tensor"),
        P("context", "tensor"),
        P("context", None),
        P("context", None),
    )
    return jax.shard_map(shards, mesh=mesh, in_specs=in_specs, out_specs=out_specs, check_vma=False)
```

profile of v0, /device:TPU:0, one launch (start us, length us, event | category | flops | bytes accessed | tf_op | source)
XLA Modules:
  0.0 193.6 jit_solution(14486047313129698208)
XLA Ops:
  12.1 1.5 copy.26
  14.0 2.1 %fusion.2 = f32[32,64,128]{2,1,0:T(8,128)} fusion(bf16[32,256,64]{1,2,0:T(8,128)(2,1)S(1)} %bitcast.143, f32[32,256]{1,0:T(8,128)S(1)} %get-tuple-element.315, bf16[256,128]{1,0:T(8,128)(2,1)S(1)} %copy-done.9), kind=kOutput, calls=%fused_computation.8 | convolution fusion | flops 806354944 | bytes 2195456 | tf_op jit(solution)/shard_map/ht,htp,tn->hpn/dot_general | solution.py:171
  16.9 2.1 %fusion.7 = f32[32,64,128]{2,1,0:T(8,128)} fusion(bf16[32,256,64]{1,2,0:T(8,128)(2,1)S(1)} %bitcast.153, f32[32,256]{1,0:T(8,128)S(1)} %get-tuple-element.316, bf16[256,128]{1,0:T(8,128)(2,1)S(1)} %copy-done.8), kind=kOutput, calls=%fused_computation.15 | convolution fusion | flops 806354944 | bytes 2195456 | tf_op jit(solution)/shard_map/hs,hsp,sn->hpn/dot_general | solution.py:166
  20.6 15.6 %all-reduce = f32[256]{0:T(256)S(1)} all-reduce(f32[256]{0:T(256)S(1)} %dynamic-update-slice), channel_id=2, replica_groups=mesh['context'=8,'tensor'=4] {'context'}, use_global_device_ids=true, to_apply=%add | all-reduce | flops 256 | bytes 2048
  40.1 2.7 %fusion.10 = f32[32,128,64]{1,2,0:T(8,128)} fusion(f32[32,128]{1,0:T(8,128)S(1)} %get-tuple-element.313, f32[128,128]{1,0:T(8,128)S(1)} %fusion.94, f32[32,128]{1,0:T(8,128)S(1)} %get-tuple-element.312, pred[128,128]{1,0:T(8,128)(4,1)S(1)} %get-tuple-element.328, bf16[32,256,64]{1,2,0:T(8,128)(2,1)S(1)} %bitcast.144), kind=kOutput, calls=%fused_computation.20 | convolution fusion | flops 405274624 | bytes 1703936 | tf_op jit(solution)/shard_map/hts,htp->hsp/dot_general | solution.py:31
  42.8 3.6 %fusion.11 = f32[32,128,64]{1,2,0:T(8,128)} fusion(f32[32,128]{1,0:T(8,128)S(1)} %get-tuple-element.313, f32[128,128]{1,0:T(8,128)S(1)} %fusion.94, f32[32,128]{1,0:T(8,128)S(1)} %get-tuple-element.312, pred[128,128]{1,0:T(8,128)(4,1)S(1)} %get-tuple-element.328, bf16[32,256,64]{1,2,0:T(8,128)(2,1)S(1)} %bitcast.156), kind=kOutput, calls=%fused_computation.21 | convolution fusion | flops 405274624 | bytes 1703936 | tf_op jit(solution)/shard_map/hts,hsp->htp/dot_general | solution.py:31
  46.4 2.7 %fusion.5 = f32[32,128,64]{1,2,0:T(8,128)} fusion(f32[32,128]{1,0:T(8,128)S(1)} %get-tuple-element.314, f32[128,128]{1,0:T(8,128)S(1)} %fusion.90, f32[32,128]{1,0:T(8,128)S(1)} %get-tuple-element.311, pred[128,128]{1,0:T(8,128)(4,1)S(1)} %get-tuple-element.327, bf16[32,256,64]{1,2,0:T(8,128)(2,1)S(1)} %bitcast.145), kind=kOutput, calls=%fused_computation.13 | convolution fusion | flops 405274624 | bytes 1703936 | tf_op jit(solution)/shard_map/hts,htp->hsp/dot_general | solution.py:31
  49.0 3.6 %fusion.6 = f32[32,128,64]{1,2,0:T(8,128)} fusion(f32[32,128]{1,0:T(8,128)S(1)} %get-tuple-element.314, f32[128,128]{1,0:T(8,128)S(1)} %fusion.90, f32[32,128]{1,0:T(8,128)S(1)} %get-tuple-element.311, pred[128,128]{1,0:T(8,128)(4,1)S(1)} %get-tuple-element.327, bf16[32,256,64]{1,2,0:T(8,128)(2,1)S(1)} %bitcast.157), kind=kOutput, calls=%fused_computation.14 | convolution fusion | flops 405274624 | bytes 1703936 | tf_op jit(solution)/shard_map/hts,hsp->htp/dot_general | solution.py:31
  54.9 18.6 %all-gather.8.cloned.1.call-done = f32[256,64,128]{2,1,0:T(8,128)} async-done(((f32[32,64,128]{2,1,0:T(8,128)}), f32[256,64,128]{2,1,0:T(8,128)}) %all-gather.8.cloned.1.call-update) | async-done | bytes 8388624 | tf_op jit(solution)/shard_map/all_gather | solution.py:14
  73.4 17.5 %while.31 = (s32[]{:T(128)}, f32[32,64,128]{2,1,0:T(8,128)S(1)}, s32[]{:T(128)}, f32[8,32]{1,0:T(8,128)}, f32[8,32,64,128]{3,2,1,0:T(8,128)}, /*index=5*/s32[]{:T(128)}, s32[]{:T(128)}, s32[]{:T(128)}, s32[]{:T(128)}) while((s32[]{:T(128)}, f32[32,64,128]{2,1,0:T(8,128)S(1)}, s32[]{:T(128)}, f32[8,32]{1,0:T(8,128)}, ...), condition=%wide.region_7.8_spmd.clone, body=%wide.region_6.7_spmd.clone.sunk | while | flops 1048584 | bytes 3146279 | solution.py:27
  74.1 1.5 fusion.128
  76.3 1.5 fusion.128
  78.5 1.5 fusion.128
  80.7 1.5 fusion.128
  82.9 1.5 fusion.128
  85.2 1.5 fusion.128
  87.3 1.5 fusion.128
  89.5 1.5 fusion.128
  91.0 3.0 %convolution_bitcast_fusion.1 = f32[128,128]{1,0:T(8,128)S(1)} fusion(f32[32,64,128]{2,1,0:T(8,128)S(1)} %get-tuple-element.231, f32[32,128]{1,0:T(8,128)S(1)} %get-tuple-element.307, bf16[32,256,64]{1,2,0:T(8,128)(2,1)} %bitcast.154), kind=kOutput, calls=%fused_computation.59 | convolution fusion | flops 403177472 | bytes 1654784 | tf_op jit(solution)/shard_map/hs,hsp,hpn->sn/dot_general | solution.py:31
  94.7 1.8 fusion.31
  97.0 32.7 %all-gather.6.cloned.1.call-done = f32[256,64,128]{2,1,0:T(8,128)} async-done(((f32[32,64,128]{2,1,0:T(8,128)}), f32[256,64,128]{2,1,0:T(8,128)}) %all-gather.6.cloned.1.call-update) | async-done | bytes 8388624 | tf_op jit(solution)/shard_map/all_gather | solution.py:14
  129.8 17.5 %while.30 = (s32[]{:T(128)}, f32[32,64,128]{2,1,0:T(8,128)S(1)}, s32[]{:T(128)}, f32[8,32]{1,0:T(8,128)}, f32[8,32,64,128]{3,2,1,0:T(8,128)}, /*index=5*/s32[]{:T(128)}, s32[]{:T(128)}) while((s32[]{:T(128)}, f32[32,64,128]{2,1,0:T(8,128)S(1)}, s32[]{:T(128)}, f32[8,32]{1,0:T(8,128)}, f32[8,32,64,128]{3,2,1,0:T(8,128)}, ...), condition=%wide.region_5.6_spmd.clone, body=%wide.region_4.5_spmd.clone.sunk | while | flops 1048580 | bytes 3146217 | solution.py:27
  130.4 1.5 fusion.127
  132.6 1.5 fusion.127
  134.8 1.5 fusion.127
  141.3 1.5 fusion.127
  143.4 1.5 fusion.127
  147.3 1.8 convolution_bitcast_fusion
  149.2 1.8 convolution_add_fusion.1
  152.0 1.8 fusion.30
  157.4 2.0 %fusion.27 = bf16[32,128,64]{1,2,0:T(8,128)(2,1)S(1)} fusion(f32[32,128,64]{1,2,0:T(8,128)} %fusion.11, f32[32,64,128]{2,1,0:T(8,128)S(1)} %get-tuple-element.230, f32[32]{0:T(128)S(1)} %copy-done.24, f32[32,128]{1,0:T(8,128)S(1)} %copy-done.18, bf16[32,256,64]{1,2,0:T(8,128)(2,1)S(1)} %bitcast.161, bf16[256,128]{1,0:T(8,128)(2,1)S(1)} %copy-done.9), kind=kOutput, calls=%fused_computation.51 | convolution fusion | flops 404226048 | bytes 3195392 | tf_op jit(solution)/shard_map/tn,hpn->htp/dot_general | solution.py:31
  161.8 25.0 %all-reduce.3 = (bf16[256,128]{1,0:T(8,128)(2,1)}, bf16[256,128]{1,0:T(8,128)(2,1)}) all-reduce(f32[256,128]{1,0:T(8,128)S(1)} %pad_maximum_fusion.2, f32[256,128]{1,0:T(8,128)S(1)} %pad_maximum_fusion.3), channel_id=1, replica_groups=mesh['context'=8,'tensor'=4] {'tensor'}, use_global_device_ids=true, to_apply=%region_10.11 | all-reduce | flops 65536 | bytes 393216 | tf_op jit(solution)/shard_map/psum | solution.py:196
  (125 shorter events, 35.5 us)
Async XLA Ops:
  7.2 6.7 %copy-start.14 = (f32[32,256]{1,0:T(8,128)S(1)}, f32[32,256]{1,0:T(8,128)}, u32[]{:S(2)}) copy-start(f32[32,256]{1,0:T(8,128)} %param.13) | copy-start | bytes 98308
  7.2 6.8 %copy-start.9 = (bf16[256,128]{1,0:T(8,128)(2,1)S(1)}, bf16[256,128]{1,0:T(8,128)(2,1)}, u32[]{:S(2)}) copy-start(bf16[256,128]{1,0:T(8,128)(2,1)} %param.17) | copy-start | bytes 196612
  7.2 66.3 %all-gather.8.cloned.1.call-start = ((), (), s32[]{:S(2)}) async-start(), calls=%async_computation.1 | async-start | bytes 9437184 | tf_op jit(solution)/shard_map/all_gather | solution.py:14
  13.6 2.6 %copy-start.10 = (bf16[256,2048]{1,0:T(8,128)(2,1)S(1)}, bf16[256,2048]{1,0:T(8,128)(2,1)}, u32[]{:S(2)}) copy-start(bf16[256,2048]{1,0:T(8,128)(2,1)} %param.12) | copy-start | bytes 3145732
  16.1 0.8 copy-start.8
  16.1 113.6 %all-gather.6.cloned.1.call-start = ((), (), s32[]{:S(2)}) async-start(), calls=%async_computation | async-start | bytes 9437184 | tf_op jit(solution)/shard_map/all_gather | solution.py:14
  16.7 2.4 %copy-start = (bf16[256,2048]{0,1:T(8,128)(2,1)}, bf16[256,2048]{0,1:T(8,128)(2,1)S(1)}, u32[]{:S(2)}) copy-start(bf16[256,2048]{0,1:T(8,128)(2,1)S(1)} %copy.25) | copy-start | bytes 3145732
  16.7 2.4 %copy-start.27 = (u32[32]{0:T(128)S(1)}, u32[32]{0:T(128)}, u32[]{:S(2)}) copy-start(u32[32]{0:T(128)} %constant.86) | copy-start | bytes 388
  38.9 52.1 %copy-start.21 = (f32[32,128]{1,0:T(8,128)}, f32[32,128]{1,0:T(8,128)S(1)}, u32[]{:S(2)}) copy-start(f32[32,128]{1,0:T(8,128)S(1)} %get-tuple-element.307) | copy-start | bytes 49156
  38.9 108.4 %copy-start.17 = (f32[32,128]{1,0:T(8,128)}, f32[32,128]{1,0:T(8,128)S(1)}, u32[]{:S(2)}) copy-start(f32[32,128]{1,0:T(8,128)S(1)} %get-tuple-element.310) | copy-start | bytes 49156
  38.9 110.2 %copy-start.15 = (f32[32,128]{1,0:T(8,128)}, f32[32,128]{1,0:T(8,128)S(1)}, u32[]{:S(2)}) copy-start(f32[32,128]{1,0:T(8,128)S(1)} %get-tuple-element.308) | copy-start | bytes 49156
  40.1 2.7 %copy-start.1 = (bf16[256,2048]{0,1:T(8,128)(2,1)S(1)}, bf16[256,2048]{0,1:T(8,128)(2,1)}, u32[]{:S(2)}) copy-start(bf16[256,2048]{0,1:T(8,128)(2,1)} %copy-done) | copy-start | bytes 3145732
  54.8 41.9 %copy-start.19 = (f32[128,128]{1,0:T(8,128)}, f32[128,128]{1,0:T(8,128)S(1)}, u32[]{:S(2)}) copy-start(f32[128,128]{1,0:T(8,128)S(1)} %multiply_reduce_fusion) | copy-start | bytes 196612
  73.4 20.5 %copy-start.26 = (f32[32]{0:T(128)S(1)}, f32[32]{0:T(128)}, u32[]{:S(2)}) copy-start(f32[32]{0:T(128)} %get-tuple-element.325) | copy-start | bytes 388
  91.0 3.7 %copy-start.2 = (bf16[256,2048]{0,1:T(8,128)(2,1)S(1)}, bf16[256,2048]{0,1:T(8,128)(2,1)}, u32[]{:S(2)}) copy-start(bf16[256,2048]{0,1:T(8,128)(2,1)} %copy-done) | copy-start | bytes 3145732
  94.6 1.9 copy-start.4
  129.8 19.4 %copy-start.25 = (f32[32]{0:T(128)S(1)}, f32[32]{0:T(128)}, u32[]{:S(2)}) copy-start(f32[32]{0:T(128)} %get-tuple-element.326) | copy-start | bytes 388
  149.2 4.7 %copy-start.20 = (f32[128,128]{1,0:T(8,128)S(1)}, f32[128,128]{1,0:T(8,128)}, u32[]{:S(2)}) copy-start(f32[128,128]{1,0:T(8,128)} %copy-done.19) | copy-start | bytes 196612
  149.2 5.1 %copy-start.5 = (f32[32,64,128]{2,1,0:T(8,128)S(1)}, f32[32,64,128]{2,1,0:T(8,128)}, u32[]{:S(2)}) copy-start(f32[32,64,128]{2,1,0:T(8,128)} %copy-done.4) | copy-start | bytes 3145732
  149.2 5.1 %copy-start.13 = (f32[32,128,64]{1,2,0:T(8,128)S(1)}, f32[32,128,64]{1,2,0:T(8,128)}, u32[]{:S(2)}) copy-start(f32[32,128,64]{1,2,0:T(8,128)} %fusion.10) | copy-start | bytes 3145732
  149.2 5.1 %copy-start.23 = (f32[32]{0:T(128)S(1)}, f32[32]{0:T(128)}, u32[]{:S(2)}) copy-start(f32[32]{0:T(128)} %param.15) | copy-start | bytes 388
  151.0 1.0 copy-start.6
  152.0 2.3 %copy-start.16 = (f32[32,128]{1,0:T(8,128)S(1)}, f32[32,128]{1,0:T(8,128)}, u32[]{:S(2)}) copy-start(f32[32,128]{1,0:T(8,128)} %copy-done.15) | copy-start | bytes 49156
  153.9 1.2 copy-start.12
  153.9 1.2 copy-start.22
  155.8 1.6 copy-start.3
  155.8 1.6 copy-start.18
  155.8 1.6 copy-start.24
  157.4 2.1 %copy-start.7 = (f32[32,64,128]{2,1,0:T(8,128)S(1)}, f32[32,64,128]{2,1,0:T(8,128)}, u32[]{:S(2)}) copy-start(f32[32,64,128]{2,1,0:T(8,128)} %copy-done.6) | copy-start | bytes 3145732
  157.4 2.1 %copy-start.11 = (f32[32,128,64]{1,2,0:T(8,128)S(1)}, f32[32,128,64]{1,2,0:T(8,128)}, u32[]{:S(2)}) copy-start(f32[32,128,64]{1,2,0:T(8,128)} %fusion.6) | copy-start | bytes 3145732
Sparse Core Ops, SparseCore 0:
  16.2 57.1 all-gather.7
  75.3 54.3 all-gather.5
where the time goes:
time: 195 us; the launch traced here: 194 us
  waiting for transfers between devices  51.4 us (26%)
  blocking collectives  40.6 us (21%)
  matrix products  35.1 us (18%)
  other arithmetic  28.9 us (15%)
  local copies, waits for them, and re-layouts  21.1 us (11%)
  between operations  15.9 us (8%)
    all_gather x2, waiting for transfers between devices, entering_2(): everything = jax.tree.map(lambda part: lax.all_gather(part, axis), value)  51.3 us
    dot_general x14, matrix products, contract(): return jnp.einsum(spec, *operands, precision=HIGH)  27.6 us
    psum x1, blocking collectives, shards(): total_b, total_c = lax.psum((grad_b_part, grad_c_part), 'tensor')  25 us
    select_n x16, other arithmetic, hop(): return jax.tree.map(lambda a, b: jnp.where(reached, a, b), new, before)  23.5 us
    unnamed x1, blocking collectives  15.6 us
    mul x16, local copies, waits for them, and re-layouts, compose(): later[0][:, None, None] * earlier[1] + later[1]  11 us
    unnamed x63, local copies, waits for them, and re-layouts  7.09 us
  transfers between devices with their start and end apart: 2, of which 2 were waited for; matrix products, arithmetic and copies ran while one was open for 23% of the time, Pallas kernels for 0%

commit v1 on v0

v1 whole, which is shorter than its diff:
```python
import functools

import jax
import jax.numpy as jnp
from jax import lax
from jax.experimental import pallas as pl
from jax.experimental.pallas import tpu as pltpu
from jax.sharding import PartitionSpec as P

BLOCK = 128
LANES = 128
F32 = jnp.float32
BF16 = jnp.bfloat16
NEVER = -200.0
MASKED = -1e30
BOUND = 6.0 * 1.796875
META = 8

NN = (((1,), (0,)), ((), ()))
NT = (((1,), (1,)), ((), ()))
TN = (((0,), (0,)), ((), ()))


def dot(a, b, dims):
    return lax.dot_general(a, b, dims, preferred_element_type=F32)


def split2(x):
    hi = x.astype(BF16)
    lo = (x - hi.astype(F32)).astype(BF16)
    return hi, lo


def split3(x):
    hi = x.astype(BF16)
    rest = x - hi.astype(F32)
    mid = rest.astype(BF16)
    lo = (rest - mid.astype(F32)).astype(BF16)
    return hi, mid, lo


def iota(shape, axis):
    return lax.broadcasted_iota(jnp.int32, shape, axis)


def block_sums(step, decay, doc):
    log_decay = -step * decay
    tri = jnp.where(iota((BLOCK, BLOCK), 0) >= iota((BLOCK, BLOCK), 1), 1.0, 0.0).astype(BF16)
    out = []
    for first in range(0, step.shape[1], BLOCK):
        cols = slice(first, first + BLOCK)
        parts = split3(log_decay[:, cols])
        starts = jnp.broadcast_to(doc[:, cols].astype(F32), (16, BLOCK)).astype(BF16)
        down = functools.reduce(jnp.add, [dot(tri, part, NT) for part in parts])
        across = functools.reduce(jnp.add, [dot(part, tri, NT) for part in parts])
        count_down = dot(tri, starts, NT)[:, :1]
        count_across = dot(starts, tri, NT)[:1]
        out.append((down, across, count_down, count_across))
    return out


def edge_weights(step, sums):
    eye = jnp.where(iota((BLOCK, BLOCK), 0) == iota((BLOCK, BLOCK), 1), 1.0, 0.0).astype(BF16)
    blocks = len(sums)
    ends = [s[0][BLOCK - 1 :] for s in sums]
    counts = [s[2][BLOCK - 1 :] for s in sums]
    keep, last = [], []
    for k in range(blocks):
        down, _, count_down, _ = sums[k]
        sum_before = down
        starts_before = count_down
        sum_after = ends[k] - down
        starts_after = counts[k] - count_down
        for j in range(k):
            sum_before = sum_before + ends[j]
            starts_before = starts_before + counts[j]
        for j in range(k + 1, blocks):
            sum_after = sum_after + ends[j]
            starts_after = starts_after + counts[j]
        parts = split3(step[:, k * BLOCK : (k + 1) * BLOCK])
        step_down = functools.reduce(jnp.add, [dot(eye, part, NT) for part in parts])
        keep.append(jnp.where(starts_before == 0.0, jnp.exp(sum_before), 0.0))
        last.append(jnp.where(starts_after == 0.0, jnp.exp(sum_after) * step_down, 0.0))
    total = functools.reduce(jnp.add, ends)
    starts = functools.reduce(jnp.add, counts)
    total = jnp.where(starts == 0.0, jnp.maximum(total, NEVER), NEVER)
    return jnp.concatenate(keep, 0), jnp.concatenate(last, 0), total


def expander(heads, width):
    shape = (heads, heads * width)
    return jnp.where(iota(shape, 0) == iota(shape, 1) // width, 1.0, 0.0).astype(BF16)


def states_kernel(
    group, width, core_ref, x_ref, g_ref, step_ref, decay_ref, doc_ref, b_ref, c_ref,
    mine_ref, send_ref, b_t, c_t, weights, meta,
):
    step_id = pl.program_id(0)
    groups = weights.shape[1]
    half = b_t.shape[0] // 2

    @pl.when(step_id == 0)
    def _():
        swap = core_ref[0] == 1
        for ref, out in ((b_ref, b_t), (c_ref, c_t)):
            turned = ref[...].astype(F32).T
            swapped = jnp.concatenate([turned[half:], turned[:half]], 0)
            out[...] = jnp.where(swap, swapped, turned).astype(BF16)
        step = step_ref[...]
        keep, last, total = edge_weights(step, block_sums(step, decay_ref[...], doc_ref[...]))
        bound_f = BOUND * jnp.sum(last, axis=0, keepdims=True)
        bound_b = BOUND * jnp.sum(keep, axis=0, keepdims=True)
        rows = jnp.concatenate(
            [total, bound_f, bound_b, jnp.zeros((META - 3, total.shape[1]), F32)], 0
        )
        for k in range(groups):
            heads = slice(k * group, (k + 1) * group)
            weights[0, k] = last[:, heads]
            weights[1, k] = keep[:, heads]
            meta[k] = rows[:, heads]

    spread = expander(group, width)
    rows = functools.reduce(jnp.add, [dot(p, spread, NN) for p in split3(meta[step_id])])
    for kind, (ref, turned) in enumerate(((x_ref, b_t), (g_ref, c_t))):
        hi, lo = split2(weights[kind, step_id])
        turned = turned[...]
        for k in range(group * width // LANES):
            lanes = slice(k * LANES, (k + 1) * LANES)
            scale = dot(hi, spread[:, lanes], NN) + dot(lo, spread[:, lanes], NN)
            scaled = split2(ref[:, lanes].astype(F32) * scale)
            state = dot(turned, scaled[0], NN) + dot(turned, scaled[1], NN)
            mine_ref[k, kind * half : (kind + 1) * half] = state[:half]
            send_ref[k, kind * half : (kind + 1) * half] = state[half:]
    for k in range(group * width // LANES):
        lanes = slice(k * LANES, (k + 1) * LANES)
        mine_ref[k, 2 * half :] = rows[:, lanes]
        send_ref[k, 2 * half :] = rows[:, lanes]


def local_kernel(
    group, width, skip_ref, x_ref, g_ref, step_ref, step_blk, decay_ref, doc_ref, b_ref, c_ref,
    mixed_ref, gx_ref, xh_ref, xl_ref, gh_ref, gl_ref, grads_ref,
    weights, down_s, across_s, bias, inter, common,
):
    step_id = pl.program_id(0)
    groups = weights.shape[1]
    pairs = ((0, 0), (1, 0), (1, 1))

    @pl.when(step_id == 0)
    def _():
        step = step_ref[...]
        sums = block_sums(step, decay_ref[...], doc_ref[...])
        keep, last, _ = edge_weights(step, sums)
        for k in range(groups):
            heads = slice(k * group, (k + 1) * group)
            weights[0, k] = last[:, heads]
            weights[1, k] = keep[:, heads]
            for j in range(2):
                down_s[j, k] = sums[j][0][:, heads]
                across_s[j, k] = sums[j][1][heads]
        for n, (t, s) in enumerate(pairs):
            if t == s:
                ok = sums[t][2] == sums[s][3]
                ok = ok & (iota((BLOCK, BLOCK), 0) >= iota((BLOCK, BLOCK), 1))
            else:
                ok = sums[t][2] == sums[s][3] - sums[s][3][:, BLOCK - 1 :]
            bias[n] = jnp.where(ok, 0.0, MASKED)
            inter[n] = dot(
                c_ref[t * BLOCK : (t + 1) * BLOCK], b_ref[s * BLOCK : (s + 1) * BLOCK], NT
            )
        common[...] = jnp.zeros_like(common)

    spread = expander(group, width)
    for ref, high, low, kind in ((x_ref, xh_ref, xl_ref, 0), (g_ref, gh_ref, gl_ref, 1)):
        hi, lo = split2(weights[kind, step_id])
        for k in range(group * width // LANES):
            lanes = slice(k * LANES, (k + 1) * LANES)
            scale = dot(hi, spread[:, lanes], NN) + dot(lo, spread[:, lanes], NN)
            scaled = split2(ref[:, lanes].astype(F32) * scale)
            high[:, lanes] = scaled[0]
            low[:, lanes] = scaled[1]

    down = [down_s[j, step_id] for j in range(2)]
    across = [across_s[j, step_id] for j in range(2)]
    left = iota((BLOCK, LANES), 1) < width
    left2 = iota((2 * BLOCK, LANES), 1) < width
    for k in range(group * width // LANES):
        lanes = slice(k * LANES, (k + 1) * LANES)
        xs = [x_ref[j * BLOCK : (j + 1) * BLOCK, lanes] for j in range(2)]
        gs = [g_ref[j * BLOCK : (j + 1) * BLOCK, lanes] for j in range(2)]
        zero = jnp.zeros_like(gs[0])
        halves = [
            jnp.concatenate([jnp.where(left, v, zero), jnp.where(left, zero, v)], 0) for v in gs
        ]
        inner = [dot(halves[t], xs[s], NT) for t, s in pairs]
        twice_x = [jnp.concatenate([v, v], 0) for v in xs]
        twice_g = [jnp.concatenate([v, v], 0) for v in gs]
        both_x = jnp.concatenate(twice_x, 0)
        both_g = jnp.concatenate(twice_g, 0)
        mixed_parts, gx_parts = [], []
        totals = [None] * 3
        for e in range(2):
            h = 2 * k + e
            parts = []
            for n, (t, s) in enumerate(pairs):
                row = across[s][h : h + 1]
                if t != s:
                    row = row - row[:, BLOCK - 1 :]
                weight = jnp.exp((down[t][:, h : h + 1] + bias[n]) - row)
                weight = weight * step_blk[h : h + 1, s * BLOCK : (s + 1) * BLOCK]
                term = weight * inner[n][e * BLOCK : (e + 1) * BLOCK]
                totals[n] = term if e == 0 else totals[n] + term
                parts.append(split2(weight * inter[n]))
            p00, p10, p11 = parts
            mixed_parts.append(
                (
                    dot(jnp.concatenate(p00, 1), twice_x[0], NN),
                    dot(jnp.concatenate(p10 + p11, 1), both_x, NN),
                )
            )
            gx_parts.append(
                (
                    dot(jnp.concatenate(p00 + p10, 0), both_g, TN),
                    dot(jnp.concatenate(p11, 0), twice_g[1], TN),
                )
            )
        for n in range(3):
            common[n] += totals[n]
        first = step_id * group + 2 * k
        skip = jnp.where(left, skip_ref[first], skip_ref[first + 1])
        for j in range(2):
            rows = slice(j * BLOCK, (j + 1) * BLOCK)
            mixed_ref[rows, lanes] = (
                jnp.where(left, mixed_parts[0][j], mixed_parts[1][j]) + skip * xs[j].astype(F32)
            )
            gx_ref[rows, lanes] = (
                jnp.where(left, gx_parts[0][j], gx_parts[1][j]) + skip * gs[j].astype(F32)
            )

    @pl.when(step_id == pl.num_programs(0) - 1)
    def _():
        c00, c10, c11 = [split2(common[n]) for n in range(3)]
        b0, b1 = b_ref[:BLOCK], b_ref[BLOCK:]
        c0, c1 = c_ref[:BLOCK], c_ref[BLOCK:]
        grads_ref[0, :BLOCK] = sum(dot(v, c0, TN) for v in c00) + sum(dot(v, c1, TN) for v in c10)
        grads_ref[0, BLOCK:] = sum(dot(v, c1, TN) for v in c11)
        grads_ref[1, :BLOCK] = sum(dot(v, b0, NN) for v in c00)
        grads_ref[1, BLOCK:] = sum(dot(v, b0, NN) for v in c10) + sum(dot(v, b1, NN) for v in c11)


def place_state(core, own, other, kind, high, low):
    half = own.shape[2]
    at = pl.multiple_of(core * half, half)
    away = pl.multiple_of((1 - core) * half, half)
    for k in range(own.shape[1]):
        lanes = slice(k * LANES, (k + 1) * LANES)
        hi, lo = split2(own[kind, k])
        high[pl.ds(at, half), lanes] = hi
        low[pl.ds(at, half), lanes] = lo
        hi, lo = split2(other[kind, k])
        high[pl.ds(away, half), lanes] = hi
        low[pl.ds(away, half), lanes] = lo


def grads_kernel(
    parts, core_ref, own_ref, other_ref, xh_ref, xl_ref, gh_ref, gl_ref, local_ref, out_ref,
    high, low, total,
):
    step_id = pl.program_id(0)

    @pl.when(step_id == 0)
    def _():
        total[...] = local_ref[...]

    for slot, kind, vh, vl in ((0, 1, xh_ref, xl_ref), (1, 0, gh_ref, gl_ref)):
        place_state(core_ref[0], own_ref, other_ref, kind, high.at[kind], low.at[kind])
        hi, lo = high[kind], low[kind]
        first = vh[...]
        total[slot] += dot(first, hi, NT) + dot(first, lo, NT) + dot(vl[...], hi, NT)

    @pl.when(step_id == pl.num_programs(0) - 1)
    def _():
        rows = total.shape[1] // parts
        for k in range(parts):
            for slot in range(2):
                out_ref[k, slot] = total[slot, k * rows : (k + 1) * rows]


def outputs_kernel(
    group, width, core_ref, own_ref, other_ref, mixed_ref, gx_ref, step_ref, decay_ref, doc_ref,
    b_ref, c_ref, mixed_out, gx_out, high, low, weights,
):
    step_id = pl.program_id(0)
    groups = weights.shape[1]

    @pl.when(step_id == 0)
    def _():
        step = step_ref[...]
        keep, last, _ = edge_weights(step, block_sums(step, decay_ref[...], doc_ref[...]))
        for k in range(groups):
            heads = slice(k * group, (k + 1) * group)
            weights[0, k] = last[:, heads]
            weights[1, k] = keep[:, heads]

    spread = expander(group, width)
    for kind, weight, proj, base, out in (
        (0, 1, c_ref, mixed_ref, mixed_out),
        (1, 0, b_ref, gx_ref, gx_out),
    ):
        place_state(core_ref[0], own_ref, other_ref, kind, high.at[kind], low.at[kind])
        hi, lo = split2(weights[weight, step_id])
        proj = proj[...]
        for k in range(group * width // LANES):
            lanes = slice(k * LANES, (k + 1) * LANES)
            scale = dot(hi, spread[:, lanes], NN) + dot(lo, spread[:, lanes], NN)
            carried = dot(proj, high[kind, :, lanes], NN) + dot(proj, low[kind, :, lanes], NN)
            out[:, lanes] = (base[:, lanes] + scale * carried).astype(BF16)


def whole(shape):
    return pl.BlockSpec(shape, lambda i: (0,) * len(shape))


SMEM = pl.BlockSpec(memory_space=pltpu.SMEM)
PARAMS = pltpu.CompilerParams(vmem_limit_bytes=48 << 20)


def swap_with(value, axis, mask):
    size = lax.axis_size(axis)
    return lax.ppermute(value, axis, [(i, i ^ mask) for i in range(size)])


def scan_chips(total_f, total_b, total_l, axis):
    size, index = lax.axis_size(axis), lax.axis_index(axis)
    before, after = jnp.zeros_like(total_f), jnp.zeros_like(total_b)
    log_before, log_after = jnp.zeros_like(total_l), jnp.zeros_like(total_l)
    bit = 2
    while bit < size:
        other_f, other_b, other_l = [swap_with(v, axis, bit) for v in (total_f, total_b, total_l)]
        upper = (index & bit) != 0
        before = jnp.where(upper, jnp.exp(log_before) * other_f + before, before)
        after = jnp.where(upper, after, jnp.exp(log_after) * other_b + after)
        log_before = jnp.where(upper, log_before + other_l, log_before)
        log_after = jnp.where(upper, log_after, log_after + other_l)
        scale, other_scale = jnp.exp(total_l), jnp.exp(other_l)
        total_f = jnp.where(upper, scale * other_f + total_f, other_scale * total_f + other_f)
        total_b = jnp.where(upper, other_b + other_scale * total_b, total_b + scale * other_b)
        total_l = jnp.maximum(total_l + other_l, NEVER)
        bit *= 2
    return before, after


def encode(state, bound, log_decay):
    chunks = state.shape[0]
    power = jnp.clip(jnp.ceil(jnp.log2(bound)), -100.0, 120.0)
    data = state * jnp.exp2(14.0 - power)
    first = lax.reduce_precision(log_decay, 5, 10)
    second = lax.reduce_precision(log_decay - first, 5, 10)
    third = lax.reduce_precision(log_decay - first - second, 5, 10)
    rows = [v.reshape(chunks, LANES) for v in (first, second, third, power)]
    return jnp.concatenate([data.reshape(-1, LANES)] + rows, 0).astype(jnp.float16)


def decode(coded, chunks):
    values = coded.astype(F32)
    size = coded.shape[0] - 4 * chunks
    rows = [
        values[size + k * chunks : size + (k + 1) * chunks].reshape(chunks, 1, LANES)
        for k in range(4)
    ]
    state = values[:size].reshape(chunks, -1, LANES) * jnp.exp2(rows[3] - 14.0)
    return state, rows[0] + rows[1] + rows[2]


def meet_chips(total_f, total_b, bound_f, bound_b, total_l, axis):
    index = lax.axis_index(axis)
    chunks = total_f.shape[0]
    x, y = (index >> 1) & 1, (index >> 2) & 1
    near_up, far_up = x == 0, y == 0
    near = encode(
        jnp.where(near_up, total_f, total_b), jnp.where(near_up, bound_f, bound_b), total_l
    )
    far = encode(
        jnp.where(far_up, total_f, total_b), jnp.where(far_up, bound_f, bound_b), total_l
    )
    from_two = swap_with(far, axis, 4)
    from_three = swap_with(far, axis, 6)
    from_one = swap_with(near, axis, 2)
    return from_one, from_two, from_three


def join_chips(arrived, axis, chunks):
    index = lax.axis_index(axis)
    x, y = (index >> 1) & 1, (index >> 2) & 1
    (one, log_one), (two, log_two), (three, log_three) = [decode(v, chunks) for v in arrived]
    same = x == y
    close = jnp.where(same, two, three)
    log_close = jnp.where(same, log_two, log_three)
    distant = jnp.where(same, three, two)
    beyond = close + jnp.exp(log_close) * distant
    main = jnp.where(same, one + jnp.exp(log_one) * beyond, beyond)
    side = jnp.where(same, 0.0, one)
    upper = y == 1
    return jnp.where(upper, main, side), jnp.where(upper, side, main)


def shards(inputs, step_size, decay_rate, skip, b_in, c_in, doc_start, cotangent):
    heads, tokens = step_size.shape
    channels = inputs.shape[1]
    width = channels // heads
    state = b_in.shape[1]
    half = state // 2
    group = min(8, heads)
    groups = heads // group
    wide = group * width
    per = wide // LANES
    chunks = channels // LANES
    context, tensor = lax.axis_size("context"), lax.axis_size("tensor")
    index = lax.axis_index("context")
    core = index & 1
    flag = core.reshape(1).astype(jnp.int32)
    decay = decay_rate.reshape(heads, 1)
    doc = doc_start.reshape(1, tokens)

    tok = pl.BlockSpec((tokens, wide), lambda i: (0, i))
    small = [
        whole((heads, tokens)),
        whole((heads, 1)),
        whole((1, tokens)),
        whole((tokens, state)),
        whole((tokens, state)),
    ]
    piece = pl.BlockSpec((per, state + META, LANES), lambda i: (i, 0, 0))
    weights = pltpu.VMEM((2, groups, tokens, group), F32)
    mine, send = pl.pallas_call(
        functools.partial(states_kernel, group, width),
        grid=(groups,),
        in_specs=[SMEM, tok, tok] + small,
        out_specs=[piece, piece],
        out_shape=[jax.ShapeDtypeStruct((chunks, state + META, LANES), F32)] * 2,
        scratch_shapes=[
            pltpu.VMEM((state, tokens), BF16),
            pltpu.VMEM((state, tokens), BF16),
            weights,
            pltpu.VMEM((groups, META, group), F32),
        ],
        compiler_params=PARAMS,
        name="states",
    )(flag, inputs, cotangent, step_size, decay, doc, b_in, c_in)

    theirs = swap_with(send, "context", 1)
    lower = core == 0
    own_f, own_b = mine[:, :half], mine[:, half:state]
    sib_f, sib_b = theirs[:, :half], theirs[:, half:state]
    own_l, own_mf, own_mb = [mine[:, state + k : state + k + 1] for k in range(3)]
    sib_l, sib_mf, sib_mb = [theirs[:, state + k : state + k + 1] for k in range(3)]
    own_e, sib_e = jnp.exp(own_l), jnp.exp(sib_l)
    f_own, f_sib = jnp.where(lower, sib_e, 1.0), jnp.where(lower, 1.0, own_e)
    b_own, b_sib = jnp.where(lower, 1.0, sib_e), jnp.where(lower, own_e, 1.0)
    chip_f = f_own * own_f + f_sib * sib_f
    chip_b = b_own * own_b + b_sib * sib_b
    chip_l = jnp.maximum(own_l + sib_l, NEVER)
    if context == 8:
        arrived = meet_chips(
            chip_f,
            chip_b,
            f_own * own_mf + f_sib * sib_mf,
            b_own * own_mb + b_sib * sib_mb,
            chip_l,
            "context",
        )
        before, after = join_chips(arrived, "context", chunks)
    else:
        before, after = scan_chips(chip_f, chip_b, chip_l, "context")

    full = jax.ShapeDtypeStruct((tokens, channels), F32)
    coded = jax.ShapeDtypeStruct((tokens, channels), BF16)
    mixed_loc, gx_loc, xh, xl, gh, gl, grads_loc = pl.pallas_call(
        functools.partial(local_kernel, group, width),
        grid=(groups,),
        in_specs=[
            SMEM,
            tok,
            tok,
            small[0],
            pl.BlockSpec((group, tokens), lambda i: (i, 0)),
        ]
        + small[1:],
        out_specs=[tok] * 6 + [whole((2, tokens, state))],
        out_shape=[full, full] + [coded] * 4 + [jax.ShapeDtypeStruct((2, tokens, state), F32)],
        scratch_shapes=[
            weights,
            pltpu.VMEM((2, groups, BLOCK, group), F32),
            pltpu.VMEM((2, groups, group, BLOCK), F32),
            pltpu.VMEM((3, BLOCK, BLOCK), F32),
            pltpu.VMEM((3, BLOCK, BLOCK), F32),
            pltpu.VMEM((3, BLOCK, BLOCK), F32),
        ],
        compiler_params=PARAMS,
        cost_estimate=pl.CostEstimate(
            flops=20 * tokens * tokens * channels,
            transcendentals=heads * tokens * tokens,
            bytes_accessed=20 * tokens * channels,
        ),
        name="local",
    )(skip, inputs, cotangent, step_size, step_size, decay, doc, b_in, c_in)

    entering = jnp.stack(
        [
            jnp.where(lower, before, sib_e * before + sib_f),
            jnp.where(lower, sib_b + sib_e * after, after),
        ]
    )
    passed = jnp.stack(
        [
            jnp.where(lower, own_e * before + own_f, before),
            jnp.where(lower, after, own_b + own_e * after),
        ]
    )
    other = swap_with(passed, "context", 1)

    parts = tensor if tokens % (8 * tensor) == 0 else 1
    state_spec = pl.BlockSpec((2, per, half, LANES), lambda i: (0, i, 0, 0))
    grads = pl.pallas_call(
        functools.partial(grads_kernel, parts),
        grid=(groups,),
        in_specs=[SMEM, state_spec, state_spec] + [tok] * 4 + [whole((2, tokens, state))],
        out_specs=whole((parts, 2, tokens // parts, state)),
        out_shape=jax.ShapeDtypeStruct((parts, 2, tokens // parts, state), F32),
        scratch_shapes=[
            pltpu.VMEM((2, state, wide), BF16),
            pltpu.VMEM((2, state, wide), BF16),
            pltpu.VMEM((2, tokens, state), F32),
        ],
        compiler_params=PARAMS,
        name="grads",
    )(flag, entering, other, xh, xl, gh, gl, grads_loc)

    mixed, grad_inputs = pl.pallas_call(
        functools.partial(outputs_kernel, group, width),
        grid=(groups,),
        in_specs=[SMEM, state_spec, state_spec, tok, tok] + small,
        out_specs=[tok, tok],
        out_shape=[coded, coded],
        scratch_shapes=[
            pltpu.VMEM((2, state, wide), BF16),
            pltpu.VMEM((2, state, wide), BF16),
            weights,
        ],
        compiler_params=PARAMS,
        cost_estimate=pl.CostEstimate(
            flops=8 * tokens * state * channels,
            transcendentals=2 * heads * tokens,
            bytes_accessed=16 * tokens * channels,
        ),
        name="outputs",
    )(flag, entering, other, mixed_loc, gx_loc, step_size, decay, doc, b_in, c_in)

    if tensor == 4 and parts == 4:
        place = lax.axis_index("tensor")
        pick = lambda at: lax.dynamic_index_in_dim(grads, at, 0, False)
        total = pick(place)
        for k in (2, 3, 1):
            total = total + swap_with(pick(place ^ k), "tensor", k)
        total = total.astype(BF16)
        summed = jnp.zeros((parts,) + total.shape, BF16)
        summed = lax.dynamic_update_index_in_dim(summed, total, place, 0)
        for k in (2, 3, 1):
            summed = lax.dynamic_update_index_in_dim(
                summed, swap_with(total, "tensor", k), place ^ k, 0
            )
    else:
        summed = lax.psum(grads, "tensor").astype(BF16)
    grad_b = summed[:, 0].reshape(tokens, state)
    grad_c = summed[:, 1].reshape(tokens, state)
    return (mixed, grad_inputs, grad_b, grad_c)


def solution(mesh):
    in_specs = (
        P("context", "tensor"),
        P("tensor", "context"),
        P("tensor"),
        P("tensor"),
        P("context", None),
        P("context", None),
        P("context"),
        P("context", "tensor"),
    )
    out_specs = (
        P("context", "tensor"),
        P("context", "tensor"),
        P("context", None),
        P("context", None),
    )
    return jax.shard_map(shards, mesh=mesh, in_specs=in_specs, out_specs=out_specs, check_vma=False)
```

time: 195 us -> 82.1 us (0.42)
  blocking collectives: 40.6 us -> 0 us
  matrix products: 35.1 us -> 0 us
  waiting for transfers between devices: 51.4 us -> 25 us
  Pallas kernels: 0 us -> 25 us
  other arithmetic: 28.9 us -> 7.2 us
  between operations: 15.9 us -> 0.89 us
  starting transfers between devices: 0.08 us -> 12.9 us
  local copies, waits for them, and re-layouts: 21.1 us -> 10.4 us
    all_gather x2 -> x0, waiting for transfers between devices: 51.3 us -> none  [entering_2(): everything = jax.tree.map(lambda part: lax.all_gather(part, axis), value)]
    dot_general x24 -> x0, matrix products: 35.1 us -> none  [the longest x14 27.6 us: contract(): return jnp.einsum(spec, *operands, precision=HIGH)]
    psum x1 -> x0, blocking collectives: 25 us -> none  [shards(): total_b, total_c = lax.psum((grad_b_part, grad_c_part), 'tensor')]
    ppermute x0 -> x11, waiting for transfers between devices: none -> 25 us  [swap_with(): return lax.ppermute(value, axis, [(i, i ^ mask) for i in range(size)])]
    pallas_call x0 -> x4, Pallas kernels: none -> 25 us  [the longest x1 10.5 us: shards(): pl.pallas_call(functools.partial(local_kernel, group, width), grid=(group...]
    select_n x16 -> x0, other arithmetic: 23.5 us -> none  [hop(): return jax.tree.map(lambda a, b: jnp.where(reached, a, b), new, before)]
    unnamed x1 -> x0, blocking collectives: 15.6 us -> none
    ppermute x0 -> x11, starting transfers between devices: none -> 12.9 us  [swap_with(): return lax.ppermute(value, axis, [(i, i ^ mask) for i in range(size)])]
  transfers between devices with their start and end apart: 2 -> 11, of which waited for: 2 -> 7; matrix products, arithmetic and copies ran while one was open for 23% -> 2% of each run, Pallas kernels for 0% -> 20%
where the time goes in v1:
time: 82.1 us; the launch traced here: 81.3 us
  Pallas kernels  25 us (30%)
  waiting for transfers between devices  25 us (30%)
  starting transfers between devices  12.9 us (16%)
  local copies, waits for them, and re-layouts  10.4 us (13%)
  other arithmetic  7.2 us (9%)
  between operations  0.89 us (1%)
    ppermute x11, waiting for transfers between devices, swap_with(): return lax.ppermute(value, axis, [(i, i ^ mask) for i in range(size)])  25 us
    ppermute x11, starting transfers between devices, swap_with(): return lax.ppermute(value, axis, [(i, i ^ mask) for i in range(size)])  12.9 us
    pallas_call x1, Pallas kernels, shards(): pl.pallas_call(functools.partial(local_kernel, group, width), grid=(group...  10.5 us
    unnamed x37, local copies, waits for them, and re-layouts  7.87 us
    pallas_call x1, Pallas kernels, shards(): pl.pallas_call(functools.partial(outputs_kernel, group, width), grid=(gro...  5.91 us
    pallas_call x1, Pallas kernels, shards(): pl.pallas_call(functools.partial(states_kernel, group, width), grid=(grou...  4.42 us
    pallas_call x1, Pallas kernels, shards(): pl.pallas_call(functools.partial(grads_kernel, parts), grid=(groups,), in...  4.13 us
    another operation x4, other arithmetic  2.89 us
  transfers between devices with their start and end apart: 11, of which 7 were waited for; matrix products, arithmetic and copies ran while one was open for 2% of the time, Pallas kernels for 20%

profile of v1, /device:TPU:0, one launch (start us, length us, event | category | flops | bytes accessed | tf_op | source)
XLA Modules:
  0.0 81.3 jit_solution(6472556216605516090)
XLA Ops:
  0.6 0.7 copy.18.decay_ref
  1.4 1.2 %copy-done.1 = bf16[256,2048]{1,0:T(8,128)(2,1)S(1)} copy-done((bf16[256,2048]{1,0:T(8,128)(2,1)S(1)}, bf16[256,2048]{1,0:T(8,128)(2,1)}, u32[]{:S(2)}) %copy-start.1) | copy-done | bytes 1048600
  2.6 1.2 %copy-done.3 = bf16[256,2048]{1,0:T(8,128)(2,1)S(1)} copy-done((bf16[256,2048]{1,0:T(8,128)(2,1)S(1)}, bf16[256,2048]{1,0:T(8,128)(2,1)}, u32[]{:S(2)}) %copy-start.3) | copy-done | bytes 1048600
  3.8 0.8 %copy-done.5 = bf16[256,128]{1,0:T(8,128)(2,1)S(1)} copy-done((bf16[256,128]{1,0:T(8,128)(2,1)S(1)}, bf16[256,128]{1,0:T(8,128)(2,1)}, u32[]{:S(2)}) %copy-start.5) | copy-done | bytes 65560
  4.7 0.8 %copy-done.7 = bf16[256,128]{1,0:T(8,128)(2,1)S(1)} copy-done((bf16[256,128]{1,0:T(8,128)(2,1)S(1)}, bf16[256,128]{1,0:T(8,128)(2,1)}, u32[]{:S(2)}) %copy-start.7) | copy-done | bytes 65560
  5.5 0.8 copy-done.9
  6.3 0.7 copy-done.11
  6.9 4.4 %states.1 = (f32[16,136,128]{2,1,0:T(8,128)S(1)}, f32[16,136,128]{2,1,0:T(8,128)S(1)}) custom-call(s32[1]{0:T(128)} %bitcast.core_ref, bf16[256,2048]{1,0:T(8,128)(2,1)S(1)} %copy-done.1, bf16[256,2048]{1,0:T(8,128)(2,1)S(1)} %copy-done.3, f32[32,256]{1,0:T(8,128)S(1)} %copy-done.9, f32[32,1]{1,0:T(8,128)S(1)} %copy.18.decay_ref, s32[1,256]{1,0:T(1,128)S(1)} %bitcast.63, ...), custom_call_target="tpu_custom_call" | custom-call | tf_op jit(solution)/shard_map/states/pallas_call | solution.py:436
  11.9 2.5 %collective-permute-done = f32[16,136,128]{2,1,0:T(8,128)} collective-permute-done((f32[16,136,128]{2,1,0:T(8,128)S(1)}, f32[16,136,128]{2,1,0:T(8,128)}, u32[]{:S(2)}, u32[]{:S(2)}) %collective-permute-start) | collective-permute-done | bytes 1114144 | tf_op jit(solution)/shard_map/ppermute | solution.py:331
  14.4 1.2 %fusion.4 = (f16[16,1,128]{2,1,0:T(2,128)(2,1)S(1)}, f32[16,1,128]{2,1,0:T(1,128)S(1)}, f16[16,1,128]{2,1,0:T(2,128)(2,1)S(1)}, f32[16,1,128]{2,1,0:T(1,128)S(1)...) fusion(f32[16,136,128]{2,1,0:T(8,128)} %collective-permute-done, ...), kind=kLoop, calls=%fused_computation.45 | loop fusion | flops 47104 | bytes 139266 | tf_op jit(solution)/shard_map/convert.10
  15.8 1.5 %multiply_convert_fusion.1 = (f16[16,64,128]{2,1,0:T(8,128)(2,1)S(1)}, f16[16,64,128]{2,1,0:T(8,128)(2,1)S(1)}) fusion(f32[16,128]{1,0:T(8,128)S(1)} %bitcast.80, pred[]{:T(512)S(6)} %eq.18, f32[16,136,128]{2,1,0:T(8,128)} %collective-permute-done, f32[16,128]{1,0:T(8,128)S(1)} %bitcast.77, f32[16,136,128]{2,1,0:T(8,128)S(1)} %get-tuple-element.16, ...), kind=kLoop, calls=%fused_computation.8 | loop fusion | flops 1572864 | bytes 2670594 | tf_op jit(solution)/shard_map/convert.13
  17.5 2.9 %collective-permute-start.1 = (f16[1088,128]{1,0:T(8,128)(2,1)S(1)}, f16[1088,128]{1,0:T(8,128)(2,1)S(1)}, u32[]{:S(2)}, u32[]{:S(2)}) collective-permute-start(f16[1088,128]{1,0:T(8,128)(2,1)S(1)} %constant_dynamic-update-slice_fusion), channel_id=1, source_target_pairs={{0,8},{4,12},{8,0},{12,4},{16,24},{20,28},{24,16},{28,20},{1,9},{5... | collective-permute-start | bytes 835592 | tf_op jit(solution)/shard_map/ppermute | solution.py:331
  20.5 1.5 %collective-permute-start.2 = (f16[1088,128]{1,0:T(8,128)(2,1)S(1)}, f16[1088,128]{1,0:T(8,128)(2,1)S(1)}, u32[]{:S(2)}, u32[]{:S(2)}) collective-permute-start(f16[1088,128]{1,0:T(8,128)(2,1)S(1)} %constant_dynamic-update-slice_fusion.5), channel_id=1, source_target_pairs={{0,16},{4,20},{8,24},{12,28},{16,0},{20,4},{24,8},{28,12},{1,17},{... | collective-permute-start | bytes 835592 | tf_op jit(solution)/shard_map/ppermute | solution.py:331
  22.0 5.9 %collective-permute-done.1 = f16[1088,128]{1,0:T(8,128)(2,1)S(1)} collective-permute-done((f16[1088,128]{1,0:T(8,128)(2,1)S(1)}, f16[1088,128]{1,0:T(8,128)(2,1)S(1)}, u32[]{:S(2)}, u32[]{:S(2)}) %collective-permute-start.1) | collective-permute-done | bytes 278560 | tf_op jit(solution)/shard_map/ppermute | solution.py:331
  27.9 6.9 %collective-permute-done.2 = f16[1088,128]{1,0:T(8,128)(2,1)S(1)} collective-permute-done((f16[1088,128]{1,0:T(8,128)(2,1)S(1)}, f16[1088,128]{1,0:T(8,128)(2,1)S(1)}, u32[]{:S(2)}, u32[]{:S(2)}) %collective-permute-start.2) | collective-permute-done | bytes 278560 | tf_op jit(solution)/shard_map/ppermute | solution.py:331
  35.1 0.9 %slice-done = f32[1024,128]{1,0:T(8,128)S(1)} async-done(((f32[1088,128]{1,0:T(8,128)}), f32[1024,128]{1,0:T(8,128)S(1)}, s32[]{:S(2)}) %slice-start) | async-done | bytes 524312 | tf_op jit(solution)/shard_map/slice | solution.py:372
  36.0 1.2 %select_bitcast_fusion.1 = (f32[1,16,64,128]{3,2,1,0:T(8,128)S(1)}, f32[16,64,128]{2,1,0:T(8,128)S(1)}, f32[1,16,64,128]{3,2,1,0:T(8,128)S(1)}, f32[16,64,128]{2,1,0:T(8,128)}) fusion(f32[16,136,128]{2,1,0:T(8,128)S(1)} %get-tuple-element.16, f32[16,128]{1,0:T(8,128)S(1)} %bitcast.74, pred[]{:T(512)S(6)} %eq.15, f32[16,128]{1,0:T(8,128)S(1)} %get-tuple-element.63, ...), kind=kLoop, calls=%fused_computation.3 | loop fusion | flops 2490368 | bytes 4767747 | tf_op jit(solution)/shard_map/stack | solution.py:515
  37.3 1.0 %pad_maximum_fusion.1 = f32[2,16,64,128]{3,2,1,0:T(8,128)} fusion(f32[1,16,64,128]{3,2,1,0:T(8,128)S(1)} %get-tuple-element.44, f32[1,16,64,128]{3,2,1,0:T(8,128)S(1)} %get-tuple-element.28), kind=kLoop, calls=%fused_computation.1 | loop fusion | flops 262144 | bytes 2097152 | tf_op jit(solution)/shard_map/stack | solution.py:515
  38.3 0.5 copy-done.2
  38.9 10.5 %local.1 = (f32[256,2048]{1,0:T(8,128)}, f32[256,2048]{1,0:T(8,128)}, bf16[256,2048]{1,0:T(8,128)(2,1)S(1)}, bf16[256,2048]{1,0:T(8,128)(2,1)S(1)}, bf16[256,204...) custom-call(f32[32]{0:T(128)S(1)} %copy-done.13, bf16[256,2048]{1,0:T(8,128)(2,1)S(1)} %copy-done.2, ...), custom_call_target="tpu_custom_call" | custom-call | flops 2684354560 | bytes 10485760 | tf_op jit(solution)/shard_map/local/pallas_call | solution.py:479
  49.4 1.8 %select_bitcast_fusion.3 = (f32[1,16,64,128]{3,2,1,0:T(8,128)S(1)}, f32[1,16,64,128]{3,2,1,0:T(8,128)S(1)}) fusion(f32[16,64,128]{2,1,0:T(8,128)S(1)} %get-tuple-element.29, f32[16,136,128]{2,1,0:T(8,128)} %collective-permute-done, f32[16,128]{1,0:T(8,128)S(1)} %bitcast.73, pred[]{:T(512)S(6)} %eq.15, f32[16,64,128]{2,1,0:T(8,128)S(1)} %copy-done.15), kind=kLoop, calls=%fused_computation.5 | loop fusion | flops 786432 | bytes 3153921 | tf_op jit(solution)/shard_map/stack | solution.py:509
  51.3 4.1 %grads.1 = f32[4,2,64,128]{3,2,1,0:T(8,128)S(1)} custom-call(s32[1]{0:T(128)} %bitcast.core_ref, f32[2,16,64,128]{3,2,1,0:T(8,128)S(1)} %pad_maximum_fusion.own_ref, f32[2,16,64,128]{3,2,1,0:T(8,128)S(1)} %collective-permute-done.4.other_ref, bf16[256,2048]{1,0:T(8,128)(2,1)S(1)} %get-tuple-element.21.xh_ref, ...), custom_call_target="tpu_custom_call" | custom-call | tf_op jit(solution)/shard_map/grads/pallas_call | solution.py:525
  55.5 2.6 %collective-permute-start.5 = (f32[2,64,128]{2,1,0:T(8,128)S(1)}, f32[2,64,128]{2,1,0:T(8,128)S(1)}, u32[]{:S(2)}, u32[]{:S(2)}) collective-permute-start(f32[2,64,128]{2,1,0:T(8,128)S(1)} %get-tuple-element.65), channel_id=1, source_target_pairs={{0,2},{1,3},{2,0},{3,1},{4,6},{5,7},{6,4},{7,5},{8,10},{9,11},{10,... | collective-permute-start | bytes 196616 | tf_op jit(solution)/shard_map/ppermute | solution.py:331
  58.1 1.4 %collective-permute-start.6 = (f32[2,64,128]{2,1,0:T(8,128)S(1)}, f32[2,64,128]{2,1,0:T(8,128)S(1)}, u32[]{:S(2)}, u32[]{:S(2)}) collective-permute-start(f32[2,64,128]{2,1,0:T(8,128)S(1)} %get-tuple-element.67), channel_id=1, source_target_pairs={{0,3},{1,2},{2,1},{3,0},{4,7},{5,6},{6,5},{7,4},{8,11},{9,10},{10,... | collective-permute-start | bytes 196616 | tf_op jit(solution)/shard_map/ppermute | solution.py:331
  59.7 3.5 %collective-permute-done.5 = f32[2,64,128]{2,1,0:T(8,128)S(1)} collective-permute-done((f32[2,64,128]{2,1,0:T(8,128)S(1)}, f32[2,64,128]{2,1,0:T(8,128)S(1)}, u32[]{:S(2)}, u32[]{:S(2)}) %collective-permute-start.5) | collective-permute-done | bytes 65568 | tf_op jit(solution)/shard_map/ppermute | solution.py:331
  63.2 1.3 %collective-permute-done.6 = f32[2,64,128]{2,1,0:T(8,128)S(1)} collective-permute-done((f32[2,64,128]{2,1,0:T(8,128)S(1)}, f32[2,64,128]{2,1,0:T(8,128)S(1)}, u32[]{:S(2)}, u32[]{:S(2)}) %collective-permute-start.6) | collective-permute-done | bytes 65568 | tf_op jit(solution)/shard_map/ppermute | solution.py:331
  64.8 2.6 %collective-permute-start.8 = (bf16[2,64,128]{2,1,0:T(8,128)(2,1)S(1)}, bf16[2,64,128]{2,1,0:T(8,128)(2,1)S(1)}, u32[]{:S(2)}, u32[]{:S(2)}) collective-permute-start(bf16[2,64,128]{2,1,0:T(8,128)(2,1)S(1)} %get-tuple-element.27), channel_id=1, source_target_pairs={{0,2},{1,3},{2,0},{3,1},{4,6},{5,7},{6,4},{7,5},{8,10},{9,11},{10,... | collective-permute-start | bytes 98312 | tf_op jit(solution)/shard_map/ppermute | solution.py:331
  67.4 1.6 %copy-done = f32[256,2048]{1,0:T(8,128)S(1)} copy-done((f32[256,2048]{1,0:T(8,128)S(1)}, f32[256,2048]{1,0:T(8,128)}, u32[]{:S(2)}) %copy-start) | copy-done | bytes 2097176
  69.0 5.9 %outputs.1 = (bf16[256,2048]{1,0:T(8,128)(2,1)}, bf16[256,2048]{1,0:T(8,128)(2,1)}) custom-call(s32[1]{0:T(128)} %bitcast.core_ref, f32[2,16,64,128]{3,2,1,0:T(8,128)S(1)} %pad_maximum_fusion.own_ref, f32[2,16,64,128]{3,2,1,0:T(8,128)S(1)} %collective-permute-done.4.other_ref, f32[256,2048]{1,0:T(8,128)S(1)} %copy-done, ...), custom_call_target="tpu_custom_call" | custom-call | flops 536870912 | bytes 8388608 | tf_op jit(solution)/shard_map/outputs/pallas_call | solution.py:540
  74.9 0.6 collective-permute-start.9
  75.9 4.7 %collective-permute-done.9 = bf16[2,64,128]{2,1,0:T(8,128)(2,1)S(1)} collective-permute-done((bf16[2,64,128]{2,1,0:T(8,128)(2,1)S(1)}, bf16[2,64,128]{2,1,0:T(8,128)(2,1)S(1)}, u32[]{:S(2)}, u32[]{:S(2)}) %collective-permute-start.9) | collective-permute-done | bytes 32800 | tf_op jit(solution)/shard_map/ppermute | solution.py:331
  80.6 0.7 fusion.25
  (59 shorter events, 2.2 us)
Async XLA Ops:
  1.4 1.2 %copy-start.1 = (bf16[256,2048]{1,0:T(8,128)(2,1)S(1)}, bf16[256,2048]{1,0:T(8,128)(2,1)}, u32[]{:S(2)}) copy-start(bf16[256,2048]{1,0:T(8,128)(2,1)} %x_ref.3) | copy-start | bytes 3145732
  2.6 1.2 %copy-start.3 = (bf16[256,2048]{1,0:T(8,128)(2,1)S(1)}, bf16[256,2048]{1,0:T(8,128)(2,1)}, u32[]{:S(2)}) copy-start(bf16[256,2048]{1,0:T(8,128)(2,1)} %g_ref.3) | copy-start | bytes 3145732
  3.8 0.8 %copy-start.5 = (bf16[256,128]{1,0:T(8,128)(2,1)S(1)}, bf16[256,128]{1,0:T(8,128)(2,1)}, u32[]{:S(2)}) copy-start(bf16[256,128]{1,0:T(8,128)(2,1)} %b_ref.5) | copy-start | bytes 196612
  4.7 0.8 %copy-start.7 = (bf16[256,128]{1,0:T(8,128)(2,1)S(1)}, bf16[256,128]{1,0:T(8,128)(2,1)}, u32[]{:S(2)}) copy-start(bf16[256,128]{1,0:T(8,128)(2,1)} %c_ref.5) | copy-start | bytes 196612
  5.5 0.8 copy-start.9
  6.3 0.7 copy-start.11
  11.4 3.0 %collective-permute-start = (f32[16,136,128]{2,1,0:T(8,128)S(1)}, f32[16,136,128]{2,1,0:T(8,128)}, u32[]{:S(2)}, u32[]{:S(2)}) collective-permute-start(f32[16,136,128]{2,1,0:T(8,128)S(1)} %get-tuple-element.15), channel_id=1, source_target_pairs={{0,4},{4,0},{8,12},{12,8},{16,20},{20,16},{24,28},{28,24},{1,5},{5... | collective-permute-start | bytes 3342344 | tf_op jit(solution)/shard_map/ppermute | solution.py:331
  17.5 10.4 %collective-permute-start.1 = (f16[1088,128]{1,0:T(8,128)(2,1)S(1)}, f16[1088,128]{1,0:T(8,128)(2,1)S(1)}, u32[]{:S(2)}, u32[]{:S(2)}) collective-permute-start(f16[1088,128]{1,0:T(8,128)(2,1)S(1)} %constant_dynamic-update-slice_fusion), channel_id=1, source_target_pairs={{0,8},{4,12},{8,0},{12,4},{16,24},{20,28},{24,16},{28,20},{1,9},{5... | collective-permute-start | bytes 835592 | tf_op jit(solution)/shard_map/ppermute | solution.py:331
  20.5 14.4 %collective-permute-start.2 = (f16[1088,128]{1,0:T(8,128)(2,1)S(1)}, f16[1088,128]{1,0:T(8,128)(2,1)S(1)}, u32[]{:S(2)}, u32[]{:S(2)}) collective-permute-start(f16[1088,128]{1,0:T(8,128)(2,1)S(1)} %constant_dynamic-update-slice_fusion.5), channel_id=1, source_target_pairs={{0,16},{4,20},{8,24},{12,28},{16,0},{20,4},{24,8},{28,12},{1,17},{... | collective-permute-start | bytes 835592 | tf_op jit(solution)/shard_map/ppermute | solution.py:331
  22.0 13.0 %collective-permute-start.3 = (f16[1088,128]{1,0:T(8,128)(2,1)S(1)}, f16[1088,128]{1,0:T(8,128)(2,1)S(1)}, u32[]{:S(2)}, u32[]{:S(2)}) collective-permute-start(f16[1088,128]{1,0:T(8,128)(2,1)S(1)} %constant_dynamic-update-slice_fusion.5), channel_id=1, source_target_pairs={{0,24},{4,28},{8,16},{12,20},{16,8},{20,12},{24,0},{28,4},{1,25},{... | collective-permute-start | bytes 835592 | tf_op jit(solution)/shard_map/ppermute | solution.py:331
  27.9 7.0 %copy-start.14 = (f32[1088,128]{1,0:T(8,128)}, f32[1088,128]{1,0:T(8,128)S(1)}, u32[]{:S(2)}) copy-start(f32[1088,128]{1,0:T(8,128)S(1)} %convert_element_type.14) | copy-start | bytes 1671172
  35.0 1.0 %slice-start = ((f32[1088,128]{1,0:T(8,128)}), f32[1024,128]{1,0:T(8,128)S(1)}, s32[]{:S(2)}) async-start(f32[1088,128]{1,0:T(8,128)} %copy-done.14), calls=%async_computation | async-start | bytes 1048576 | tf_op jit(solution)/shard_map/slice | solution.py:372
  37.2 1.6 %copy-start.2 = (bf16[256,2048]{1,0:T(8,128)(2,1)S(1)}, bf16[256,2048]{1,0:T(8,128)(2,1)}, u32[]{:S(2)}) copy-start(bf16[256,2048]{1,0:T(8,128)(2,1)} %x_ref.3) | copy-start | bytes 3145732
  37.2 1.6 %copy-start.6 = (bf16[256,128]{1,0:T(8,128)(2,1)S(1)}, bf16[256,128]{1,0:T(8,128)(2,1)}, u32[]{:S(2)}) copy-start(bf16[256,128]{1,0:T(8,128)(2,1)} %b_ref.5) | copy-start | bytes 196612
  37.2 1.6 %copy-start.8 = (bf16[256,128]{1,0:T(8,128)(2,1)S(1)}, bf16[256,128]{1,0:T(8,128)(2,1)}, u32[]{:S(2)}) copy-start(bf16[256,128]{1,0:T(8,128)(2,1)} %c_ref.5) | copy-start | bytes 196612
  37.2 1.6 %copy-start.10 = (f32[32,256]{1,0:T(8,128)S(1)}, f32[32,256]{1,0:T(8,128)}, u32[]{:S(2)}) copy-start(f32[32,256]{1,0:T(8,128)} %step_ref.5) | copy-start | bytes 98308
  37.2 1.6 %copy-start.12 = (s32[256]{0:T(256)S(1)}, s32[256]{0:T(256)}, u32[]{:S(2)}) copy-start(s32[256]{0:T(256)} %param.14) | copy-start | bytes 3076
  37.2 1.6 %copy-start.13 = (f32[32]{0:T(128)S(1)}, f32[32]{0:T(128)}, u32[]{:S(2)}) copy-start(f32[32]{0:T(128)} %skip_ref.1) | copy-start | bytes 388
  38.3 13.0 %collective-permute-start.4 = (f32[2,16,64,128]{3,2,1,0:T(8,128)}, f32[2,16,64,128]{3,2,1,0:T(8,128)S(1)}, u32[]{:S(2)}, u32[]{:S(2)}) collective-permute-start(f32[2,16,64,128]{3,2,1,0:T(8,128)} %pad_maximum_fusion.1), channel_id=1, source_target_pairs={{0,4},{4,0},{8,12},{12,8},{16,20},{20,16},{24,28},{28,24},{1,5},{5... | collective-permute-start | bytes 3145736 | tf_op jit(solution)/shard_map/ppermute | solution.py:331
  38.8 10.5 %copy-start.15 = (f32[16,64,128]{2,1,0:T(8,128)S(1)}, f32[16,64,128]{2,1,0:T(8,128)}, u32[]{:S(2)}) copy-start(f32[16,64,128]{2,1,0:T(8,128)} %get-tuple-element.45) | copy-start | bytes 1572868
  49.4 1.8 %copy-start.4 = (bf16[256,2048]{1,0:T(8,128)(2,1)}, bf16[256,2048]{1,0:T(8,128)(2,1)S(1)}, u32[]{:S(2)}) copy-start(bf16[256,2048]{1,0:T(8,128)(2,1)S(1)} %get-tuple-element.24.gl_ref) | copy-start | bytes 3145732
  55.5 7.7 %collective-permute-start.5 = (f32[2,64,128]{2,1,0:T(8,128)S(1)}, f32[2,64,128]{2,1,0:T(8,128)S(1)}, u32[]{:S(2)}, u32[]{:S(2)}) collective-permute-start(f32[2,64,128]{2,1,0:T(8,128)S(1)} %get-tuple-element.65), channel_id=1, source_target_pairs={{0,2},{1,3},{2,0},{3,1},{4,6},{5,7},{6,4},{7,5},{8,10},{9,11},{10,... | collective-permute-start | bytes 196616 | tf_op jit(solution)/shard_map/ppermute | solution.py:331
  58.1 6.4 %collective-permute-start.6 = (f32[2,64,128]{2,1,0:T(8,128)S(1)}, f32[2,64,128]{2,1,0:T(8,128)S(1)}, u32[]{:S(2)}, u32[]{:S(2)}) collective-permute-start(f32[2,64,128]{2,1,0:T(8,128)S(1)} %get-tuple-element.67), channel_id=1, source_target_pairs={{0,3},{1,2},{2,1},{3,0},{4,7},{5,6},{6,5},{7,4},{8,11},{9,10},{10,... | collective-permute-start | bytes 196616 | tf_op jit(solution)/shard_map/ppermute | solution.py:331
  59.5 5.2 %collective-permute-start.7 = (f32[2,64,128]{2,1,0:T(8,128)S(1)}, f32[2,64,128]{2,1,0:T(8,128)S(1)}, u32[]{:S(2)}, u32[]{:S(2)}) collective-permute-start(f32[2,64,128]{2,1,0:T(8,128)S(1)} %get-tuple-element.66), channel_id=1, source_target_pairs={{0,1},{1,0},{2,3},{3,2},{4,5},{5,4},{6,7},{7,6},{8,9},{9,8},{10,11... | collective-permute-start | bytes 196616 | tf_op jit(solution)/shard_map/ppermute | solution.py:331
  64.8 11.2 %collective-permute-start.8 = (bf16[2,64,128]{2,1,0:T(8,128)(2,1)S(1)}, bf16[2,64,128]{2,1,0:T(8,128)(2,1)S(1)}, u32[]{:S(2)}, u32[]{:S(2)}) collective-permute-start(bf16[2,64,128]{2,1,0:T(8,128)(2,1)S(1)} %get-tuple-element.27), channel_id=1, source_target_pairs={{0,2},{1,3},{2,0},{3,1},{4,6},{5,7},{6,4},{7,5},{8,10},{9,11},{10,... | collective-permute-start | bytes 98312 | tf_op jit(solution)/shard_map/ppermute | solution.py:331
  67.4 1.6 %copy-start = (f32[256,2048]{1,0:T(8,128)S(1)}, f32[256,2048]{1,0:T(8,128)}, u32[]{:S(2)}) copy-start(f32[256,2048]{1,0:T(8,128)} %get-tuple-element.17.mixed_ref) | copy-start | bytes 6291460
  74.9 5.7 %collective-permute-start.9 = (bf16[2,64,128]{2,1,0:T(8,128)(2,1)S(1)}, bf16[2,64,128]{2,1,0:T(8,128)(2,1)S(1)}, u32[]{:S(2)}, u32[]{:S(2)}) collective-permute-start(bf16[2,64,128]{2,1,0:T(8,128)(2,1)S(1)} %get-tuple-element.27), channel_id=1, source_target_pairs={{0,3},{1,2},{2,1},{3,0},{4,7},{5,6},{6,5},{7,4},{8,11},{9,10},{10,... | collective-permute-start | bytes 98312 | tf_op jit(solution)/shard_map/ppermute | solution.py:331
  75.5 5.1 %collective-permute-start.10 = (bf16[2,64,128]{2,1,0:T(8,128)(2,1)S(1)}, bf16[2,64,128]{2,1,0:T(8,128)(2,1)S(1)}, u32[]{:S(2)}, u32[]{:S(2)}) collective-permute-start(bf16[2,64,128]{2,1,0:T(8,128)(2,1)S(1)} %get-tuple-element.27), channel_id=1, source_target_pairs={{0,1},{1,0},{2,3},{3,2},{4,5},{5,4},{6,7},{7,6},{8,9},{9,8},{10,11... | collective-permute-start | bytes 98312 | tf_op jit(solution)/shard_map/ppermute | solution.py:331

commit v2 on v1

--- a/solution.py
+++ b/solution.py
@@ -92,55 +92,95 @@
     return jnp.where(iota(shape, 0) == iota(shape, 1) // width, 1.0, 0.0).astype(BF16)
 
 
+def fetch(pairs, sems):
+    copies = [pltpu.make_async_copy(src, dst, sems.at[k]) for k, (src, dst) in enumerate(pairs)]
+    for copy in copies:
+        copy.start()
+    return copies
+
+
+def column(row):
+    shape = (row.shape[1], row.shape[1])
+    spot = iota(shape, 0) == iota(shape, 1)
+    return jnp.sum(jnp.where(spot, row, 0.0), axis=1, keepdims=True)
+
+
 def states_kernel(
-    group, width, core_ref, x_ref, g_ref, step_ref, decay_ref, doc_ref, b_ref, c_ref,
-    mine_ref, send_ref, b_t, c_t, weights, meta,
+    group, width, core_ref, x_hbm, g_hbm, step_hbm, decay_hbm, doc_hbm, b_hbm, c_hbm,
+    mine_ref, send_ref, meta_ref, x_ref, g_ref, step_ref, decay_ref, doc_ref, b_ref, c_ref,
+    b_t, c_t, weights, meta, small_sems, big_sems,
 ):
     step_id = pl.program_id(0)
     groups = weights.shape[1]
     half = b_t.shape[0] // 2
+    wide = group * width
+    chunks = wide // LANES
+
+    def big(k):
+        return [
+            pltpu.make_async_copy(
+                src.at[:, pl.ds(pl.multiple_of(k * wide, LANES), wide)], dst.at[k], big_sems.at[n, k]
+            )
+            for n, (src, dst) in enumerate(((x_hbm, x_ref), (g_hbm, g_ref)))
+        ]
 
     @pl.when(step_id == 0)
     def _():
+        small = fetch(
+            (
+                (step_hbm, step_ref),
+                (decay_hbm, decay_ref),
+                (doc_hbm, doc_ref),
+                (b_hbm, b_ref),
+                (c_hbm, c_ref),
+            ),
+            small_sems,
+        )
+        for k in range(groups):
+            for copy in big(k):
+                copy.start()
+        for copy in small:
+            copy.wait()
         swap = core_ref[0] == 1
-        for ref, out in ((b_ref, b_t), (c_ref, c_t)):
-            turned = ref[...].astype(F32).T
-            swapped = jnp.concatenate([turned[half:], turned[:half]], 0)
-            out[...] = jnp.where(swap, swapped, turned).astype(BF16)
         step = step_ref[...]
-        keep, last, total = edge_weights(step, block_sums(step, decay_ref[...], doc_ref[...]))
+        sums = block_sums(step, column(decay_ref[...]), doc_ref[...])
+        keep, last, total = edge_weights(step, sums)
         bound_f = BOUND * jnp.sum(last, axis=0, keepdims=True)
         bound_b = BOUND * jnp.sum(keep, axis=0, keepdims=True)
-        rows = jnp.concatenate(
-            [total, bound_f, bound_b, jnp.zeros((META - 3, total.shape[1]), F32)], 0
-        )
+        rows = [total, jnp.exp(total), bound_f, bound_b]
+        rows = jnp.concatenate(rows + [jnp.zeros((META - 4, total.shape[1]), F32)], 0)
         for k in range(groups):
             heads = slice(k * group, (k + 1) * group)
             weights[0, k] = last[:, heads]
             weights[1, k] = keep[:, heads]
             meta[k] = rows[:, heads]
-
+        for ref, out in ((b_ref, b_t), (c_ref, c_t)):
+            turned = ref[...].astype(F32).T
+            swapped = jnp.concatenate([turned[half:], turned[:half]], 0)
+            out[...] = jnp.where(swap, swapped, turned).astype(BF16)
+
+    for copy in big(step_id):
+        copy.wait()
     spread = expander(group, width)
     rows = functools.reduce(jnp.add, [dot(p, spread, NN) for p in split3(meta[step_id])])
+    for k in range(chunks):
+        for n in range(META):
+            meta_ref[n, pl.ds(step_id * chunks + k, 1)] = rows[n : n + 1, k * LANES : (k + 1) * LANES]
     for kind, (ref, turned) in enumerate(((x_ref, b_t), (g_ref, c_t))):
         hi, lo = split2(weights[kind, step_id])
         turned = turned[...]
-        for k in range(group * width // LANES):
+        for k in range(chunks):
             lanes = slice(k * LANES, (k + 1) * LANES)
             scale = dot(hi, spread[:, lanes], NN) + dot(lo, spread[:, lanes], NN)
-            scaled = split2(ref[:, lanes].astype(F32) * scale)
+            scaled = split2(ref[step_id, :, lanes].astype(F32) * scale)
             state = dot(turned, scaled[0], NN) + dot(turned, scaled[1], NN)
             mine_ref[k, kind * half : (kind + 1) * half] = state[:half]
             send_ref[k, kind * half : (kind + 1) * half] = state[half:]
-    for k in range(group * width // LANES):
-        lanes = slice(k * LANES, (k + 1) * LANES)
-        mine_ref[k, 2 * half :] = rows[:, lanes]
-        send_ref[k, 2 * half :] = rows[:, lanes]
 
 
 def local_kernel(
     group, width, skip_ref, x_ref, g_ref, step_ref, step_blk, decay_ref, doc_ref, b_ref, c_ref,
-    mixed_ref, gx_ref, xh_ref, xl_ref, gh_ref, gl_ref, grads_ref,
+    mixed_ref, gx_ref, xh_ref, xl_ref, gh_ref, gl_ref, coded_ref, grads_ref,
     weights, down_s, across_s, bias, inter, common,
 ):
     step_id = pl.program_id(0)
@@ -150,7 +190,7 @@
     @pl.when(step_id == 0)
     def _():
         step = step_ref[...]
-        sums = block_sums(step, decay_ref[...], doc_ref[...])
+        sums = block_sums(step, column(decay_ref[...]), doc_ref[...])
         keep, last, _ = edge_weights(step, sums)
         for k in range(groups):
             heads = slice(k * group, (k + 1) * group)
@@ -174,6 +214,8 @@
     spread = expander(group, width)
     for ref, high, low, kind in ((x_ref, xh_ref, xl_ref, 0), (g_ref, gh_ref, gl_ref, 1)):
         hi, lo = split2(weights[kind, step_id])
+        coded_ref[kind, 0, 0] = hi
+        coded_ref[kind, 0, 1] = lo
         for k in range(group * width // LANES):
             lanes = slice(k * LANES, (k + 1) * LANES)
             scale = dot(hi, spread[:, lanes], NN) + dot(lo, spread[:, lanes], NN)
@@ -249,23 +291,20 @@
         grads_ref[1, BLOCK:] = sum(dot(v, b0, NN) for v in c10) + sum(dot(v, b1, NN) for v in c11)
 
 
-def place_state(core, own, other, kind, high, low):
-    half = own.shape[2]
-    at = pl.multiple_of(core * half, half)
-    away = pl.multiple_of((1 - core) * half, half)
-    for k in range(own.shape[1]):
-        lanes = slice(k * LANES, (k + 1) * LANES)
-        hi, lo = split2(own[kind, k])
-        high[pl.ds(at, half), lanes] = hi
-        low[pl.ds(at, half), lanes] = lo
-        hi, lo = split2(other[kind, k])
-        high[pl.ds(away, half), lanes] = hi
-        low[pl.ds(away, half), lanes] = lo
+def place_state(core, own, other, high, low):
+    half = own.shape[1]
+    for part, first in ((own, core), (other, 1 - core)):
+        rows = pl.ds(pl.multiple_of(first * half, half), half)
+        for k in range(own.shape[0]):
+            lanes = slice(k * LANES, (k + 1) * LANES)
+            hi, lo = split2(part[k])
+            high[rows, lanes] = hi
+            low[rows, lanes] = lo
 
 
 def grads_kernel(
-    parts, core_ref, own_ref, other_ref, xh_ref, xl_ref, gh_ref, gl_ref, local_ref, out_ref,
-    high, low, total,
+    parts, core_ref, own_f, other_f, own_b, other_b, xh_ref, xl_ref, gh_ref, gl_ref, local_ref,
+    out_ref, high, low, total,
 ):
     step_id = pl.program_id(0)
 
@@ -273,9 +312,12 @@
     def _():
         total[...] = local_ref[...]
 
-    for slot, kind, vh, vl in ((0, 1, xh_ref, xl_ref), (1, 0, gh_ref, gl_ref)):
-        place_state(core_ref[0], own_ref, other_ref, kind, high.at[kind], low.at[kind])
-        hi, lo = high[kind], low[kind]
+    for slot, own, other, vh, vl in (
+        (0, own_b, other_b, xh_ref, xl_ref),
+        (1, own_f, other_f, gh_ref, gl_ref),
+    ):
+        place_state(core_ref[0], own, other, high.at[slot], low.at[slot])
+        hi, lo = high[slot], low[slot]
         first = vh[...]
         total[slot] += dot(first, hi, NT) + dot(first, lo, NT) + dot(vl[...], hi, NT)
 
@@ -287,35 +329,18 @@
                 out_ref[k, slot] = total[slot, k * rows : (k + 1) * rows]
 
 
-def outputs_kernel(
-    group, width, core_ref, own_ref, other_ref, mixed_ref, gx_ref, step_ref, decay_ref, doc_ref,
-    b_ref, c_ref, mixed_out, gx_out, high, low, weights,
+def output_kernel(
+    group, width, core_ref, own, other, base_ref, coded_ref, proj_ref, out_ref, high, low
 ):
-    step_id = pl.program_id(0)
-    groups = weights.shape[1]
-
-    @pl.when(step_id == 0)
-    def _():
-        step = step_ref[...]
-        keep, last, _ = edge_weights(step, block_sums(step, decay_ref[...], doc_ref[...]))
-        for k in range(groups):
-            heads = slice(k * group, (k + 1) * group)
-            weights[0, k] = last[:, heads]
-            weights[1, k] = keep[:, heads]
-
+    place_state(core_ref[0], own, other, high, low)
     spread = expander(group, width)
-    for kind, weight, proj, base, out in (
-        (0, 1, c_ref, mixed_ref, mixed_out),
-        (1, 0, b_ref, gx_ref, gx_out),
-    ):
-        place_state(core_ref[0], own_ref, other_ref, kind, high.at[kind], low.at[kind])
-        hi, lo = split2(weights[weight, step_id])
-        proj = proj[...]
-        for k in range(group * width // LANES):
-            lanes = slice(k * LANES, (k + 1) * LANES)
-            scale = dot(hi, spread[:, lanes], NN) + dot(lo, spread[:, lanes], NN)
-            carried = dot(proj, high[kind, :, lanes], NN) + dot(proj, low[kind, :, lanes], NN)
-            out[:, lanes] = (base[:, lanes] + scale * carried).astype(BF16)
+    hi, lo = coded_ref[0, 0, 0], coded_ref[0, 0, 1]
+    proj = proj_ref[...]
+    for k in range(group * width // LANES):
+        lanes = slice(k * LANES, (k + 1) * LANES)
+        scale = dot(hi, spread[:, lanes], NN) + dot(lo, spread[:, lanes], NN)
+        carried = dot(proj, high[:, lanes], NN) + dot(proj, low[:, lanes], NN)
+        out_ref[:, lanes] = (base_ref[:, lanes] + scale * carried).astype(BF16)
 
 
 def whole(shape):
@@ -323,7 +348,8 @@
 
 
 SMEM = pl.BlockSpec(memory_space=pltpu.SMEM)
-PARAMS = pltpu.CompilerParams(vmem_limit_bytes=48 << 20)
+HBM = pl.BlockSpec(memory_space=pltpu.HBM)
+PARAMS = pltpu.CompilerParams(vmem_limit_bytes=24 << 20)
 
 
 def swap_with(value, axis, mask):
@@ -352,54 +378,45 @@
 
 
 def encode(state, bound, log_decay):
-    chunks = state.shape[0]
     power = jnp.clip(jnp.ceil(jnp.log2(bound)), -100.0, 120.0)
-    data = state * jnp.exp2(14.0 - power)
+    data = state * jnp.exp2(14.0 - power)[:, None]
     first = lax.reduce_precision(log_decay, 5, 10)
     second = lax.reduce_precision(log_decay - first, 5, 10)
     third = lax.reduce_precision(log_decay - first - second, 5, 10)
-    rows = [v.reshape(chunks, LANES) for v in (first, second, third, power)]
-    return jnp.concatenate([data.reshape(-1, LANES)] + rows, 0).astype(jnp.float16)
+    rows = [data.reshape(-1, LANES), first, second, third, power]
+    return jnp.concatenate([v.astype(jnp.float16) for v in rows], 0)
 
 
 def decode(coded, chunks):
-    values = coded.astype(F32)
     size = coded.shape[0] - 4 * chunks
-    rows = [
-        values[size + k * chunks : size + (k + 1) * chunks].reshape(chunks, 1, LANES)
-        for k in range(4)
+    rows = [coded[size + k * chunks : size + (k + 1) * chunks].astype(F32) for k in range(4)]
+    state = coded[:size].reshape(chunks, -1, LANES).astype(F32)
+    return state * jnp.exp2(rows[3] - 14.0)[:, None], jnp.exp(rows[0] + rows[1] + rows[2])[:, None]
+
+
+def chip_place(axis):
+    index = lax.axis_index(axis)
+    return (index >> 1) & 1, (index >> 2) & 1
+
+
+def pack_chip(total_f, total_b, bound_f, bound_b, log_decay, axis):
+    return [
+        encode(
+            jnp.where(first, total_f, total_b), jnp.where(first, bound_f, bound_b), log_decay
+        )
+        for first in [bit == 0 for bit in chip_place(axis)]
     ]
-    state = values[:size].reshape(chunks, -1, LANES) * jnp.exp2(rows[3] - 14.0)
-    return state, rows[0] + rows[1] + rows[2]
-
-
-def meet_chips(total_f, total_b, bound_f, bound_b, total_l, axis):
-    index = lax.axis_index(axis)
-    chunks = total_f.shape[0]
-    x, y = (index >> 1) & 1, (index >> 2) & 1
-    near_up, far_up = x == 0, y == 0
-    near = encode(
-        jnp.where(near_up, total_f, total_b), jnp.where(near_up, bound_f, bound_b), total_l
-    )
-    far = encode(
-        jnp.where(far_up, total_f, total_b), jnp.where(far_up, bound_f, bound_b), total_l
-    )
-    from_two = swap_with(far, axis, 4)
-    from_three = swap_with(far, axis, 6)
-    from_one = swap_with(near, axis, 2)
-    return from_one, from_two, from_three
 
 
 def join_chips(arrived, axis, chunks):
-    index = lax.axis_index(axis)
-    x, y = (index >> 1) & 1, (index >> 2) & 1
-    (one, log_one), (two, log_two), (three, log_three) = [decode(v, chunks) for v in arrived]
+    x, y = chip_place(axis)
+    (one, decay_one), (two, decay_two), (three, decay_three) = [decode(v, chunks) for v in arrived]
     same = x == y
     close = jnp.where(same, two, three)
-    log_close = jnp.where(same, log_two, log_three)
+    decay_close = jnp.where(same, decay_two, decay_three)
     distant = jnp.where(same, three, two)
-    beyond = close + jnp.exp(log_close) * distant
-    main = jnp.where(same, one + jnp.exp(log_one) * beyond, beyond)
+    beyond = close + decay_close * distant
+    main = jnp.where(same, one + decay_one * beyond, beyond)
     side = jnp.where(same, 0.0, one)
     upper = y == 1
     return jnp.where(upper, main, side), jnp.where(upper, side, main)
@@ -417,52 +434,54 @@
     per = wide // LANES
     chunks = channels // LANES
     context, tensor = lax.axis_size("context"), lax.axis_size("tensor")
-    index = lax.axis_index("context")
-    core = index & 1
+    core = lax.axis_index("context") & 1
     flag = core.reshape(1).astype(jnp.int32)
-    decay = decay_rate.reshape(heads, 1)
+    decay = decay_rate.reshape(1, heads)
     doc = doc_start.reshape(1, tokens)
 
     tok = pl.BlockSpec((tokens, wide), lambda i: (0, i))
-    small = [
-        whole((heads, tokens)),
-        whole((heads, 1)),
-        whole((1, tokens)),
-        whole((tokens, state)),
-        whole((tokens, state)),
-    ]
-    piece = pl.BlockSpec((per, state + META, LANES), lambda i: (i, 0, 0))
+    piece = pl.BlockSpec((per, state, LANES), lambda i: (i, 0, 0))
     weights = pltpu.VMEM((2, groups, tokens, group), F32)
-    mine, send = pl.pallas_call(
+    mine, send, meta = pl.pallas_call(
         functools.partial(states_kernel, group, width),
         grid=(groups,),
-        in_specs=[SMEM, tok, tok] + small,
-        out_specs=[piece, piece],
-        out_shape=[jax.ShapeDtypeStruct((chunks, state + META, LANES), F32)] * 2,
+        in_specs=[SMEM] + [HBM] * 7,
+        out_specs=[piece, piece, whole((META, chunks, LANES))],
+        out_shape=[jax.ShapeDtypeStruct((chunks, state, LANES), F32)] * 2
+        + [jax.ShapeDtypeStruct((META, chunks, LANES), F32)],
         scratch_shapes=[
+            pltpu.VMEM((groups, tokens, wide), BF16),
+            pltpu.VMEM((groups, tokens, wide), BF16),
+            pltpu.VMEM((heads, tokens), F32),
+            pltpu.VMEM((1, heads), F32),
+            pltpu.VMEM((1, tokens), jnp.int32),
+            pltpu.VMEM((tokens, state), BF16),
+            pltpu.VMEM((tokens, state), BF16),
             pltpu.VMEM((state, tokens), BF16),
             pltpu.VMEM((state, tokens), BF16),
             weights,
             pltpu.VMEM((groups, META, group), F32),
+            pltpu.SemaphoreType.DMA((5,)),
+            pltpu.SemaphoreType.DMA((2, groups)),
         ],
         compiler_params=PARAMS,
         name="states",
     )(flag, inputs, cotangent, step_size, decay, doc, b_in, c_in)
 
     theirs = swap_with(send, "context", 1)
+    sib_meta = swap_with(meta, "context", 1)
     lower = core == 0
-    own_f, own_b = mine[:, :half], mine[:, half:state]
-    sib_f, sib_b = theirs[:, :half], theirs[:, half:state]
-    own_l, own_mf, own_mb = [mine[:, state + k : state + k + 1] for k in range(3)]
-    sib_l, sib_mf, sib_mb = [theirs[:, state + k : state + k + 1] for k in range(3)]
-    own_e, sib_e = jnp.exp(own_l), jnp.exp(sib_l)
+    own_f, own_b = mine[:, :half], mine[:, half:]
+    sib_f, sib_b = theirs[:, :half], theirs[:, half:]
+    own_l, own_e, own_mf, own_mb = [meta[k] for k in range(4)]
+    sib_l, sib_e, sib_mf, sib_mb = [sib_meta[k] for k in range(4)]
     f_own, f_sib = jnp.where(lower, sib_e, 1.0), jnp.where(lower, 1.0, own_e)
     b_own, b_sib = jnp.where(lower, 1.0, sib_e), jnp.where(lower, own_e, 1.0)
-    chip_f = f_own * own_f + f_sib * sib_f
-    chip_b = b_own * own_b + b_sib * sib_b
+    chip_f = f_own[:, None] * own_f + f_sib[:, None] * sib_f
+    chip_b = b_own[:, None] * own_b + b_sib[:, None] * sib_b
     chip_l = jnp.maximum(own_l + sib_l, NEVER)
     if context == 8:
-        arrived = meet_chips(
+        near, far = pack_chip(
             chip_f,
             chip_b,
             f_own * own_mf + f_sib * sib_mf,
@@ -470,25 +489,40 @@
             chip_l,
             "context",
         )
-        before, after = join_chips(arrived, "context", chunks)
-    else:
-        before, after = scan_chips(chip_f, chip_b, chip_l, "context")
+        near, far, skip = lax.optimization_barrier((near, far, skip))
+        arrived = [
+            swap_with(near, "context", 2),
+            swap_with(far, "context", 4),
+            swap_with(far, "context", 6),
+        ]
 
     full = jax.ShapeDtypeStruct((tokens, channels), F32)
     coded = jax.ShapeDtypeStruct((tokens, channels), BF16)
-    mixed_loc, gx_loc, xh, xl, gh, gl, grads_loc = pl.pallas_call(
+    mixed_loc, gx_loc, xh, xl, gh, gl, scales, grads_loc = pl.pallas_call(
         functools.partial(local_kernel, group, width),
         grid=(groups,),
         in_specs=[
             SMEM,
             tok,
             tok,
-            small[0],
+            whole((heads, tokens)),
             pl.BlockSpec((group, tokens), lambda i: (i, 0)),
-        ]
-        + small[1:],
-        out_specs=[tok] * 6 + [whole((2, tokens, state))],
-        out_shape=[full, full] + [coded] * 4 + [jax.ShapeDtypeStruct((2, tokens, state), F32)],
+            whole((1, heads)),
+            whole((1, tokens)),
+            whole((tokens, state)),
+            whole((tokens, state)),
+        ],
+        out_specs=[tok] * 6
+        + [
+            pl.BlockSpec((2, 1, 2, tokens, group), lambda i: (0, i, 0, 0, 0)),
+            whole((2, tokens, state)),
+        ],
+        out_shape=[full, full]
+        + [coded] * 4
+        + [
+            jax.ShapeDtypeStruct((2, groups, 2, tokens, group), BF16),
+            jax.ShapeDtypeStruct((2, tokens, state), F32),
+        ],
         scratch_shapes=[
             weights,
             pltpu.VMEM((2, groups, BLOCK, group), F32),
@@ -506,71 +540,76 @@
         name="local",
     )(skip, inputs, cotangent, step_size, step_size, decay, doc, b_in, c_in)
 
-    entering = jnp.stack(
-        [
-            jnp.where(lower, before, sib_e * before + sib_f),
-            jnp.where(lower, sib_b + sib_e * after, after),
-        ]
-    )
-    passed = jnp.stack(
-        [
-            jnp.where(lower, own_e * before + own_f, before),
-            jnp.where(lower, after, own_b + own_e * after),
-        ]
-    )
-    other = swap_with(passed, "context", 1)
+    if context == 8:
+        arrived, grads_loc = lax.optimization_barrier((arrived, grads_loc))
+        before, after = join_chips(arrived, "context", chunks)
+    else:
+        before, after = scan_chips(chip_f, chip_b, chip_l[:, None], "context")
+
+    own_e, sib_e = own_e[:, None], sib_e[:, None]
+    other_f = swap_with(jnp.where(lower, own_e * before + own_f, before), "context", 1)
+    other_b = swap_with(jnp.where(lower, after, own_b + own_e * after), "context", 1)
+    enter_f = jnp.where(lower, before, sib_e * before + sib_f)
+    enter_b = jnp.where(lower, sib_b + sib_e * after, after)
 
     parts = tensor if tokens % (8 * tensor) == 0 else 1
-    state_spec = pl.BlockSpec((2, per, half, LANES), lambda i: (0, i, 0, 0))
+    state_spec = pl.BlockSpec((per, half, LANES), lambda i: (i, 0, 0))
+    slots = [pltpu.VMEM((2, state, wide), BF16)] * 2
     grads = pl.pallas_call(
         functools.partial(grads_kernel, parts),
         grid=(groups,),
-        in_specs=[SMEM, state_spec, state_spec] + [tok] * 4 + [whole((2, tokens, state))],
+        in_specs=[SMEM] + [state_spec] * 4 + [tok] * 4 + [whole((2, tokens, state))],
         out_specs=whole((parts, 2, tokens // parts, state)),
         out_shape=jax.ShapeDtypeStruct((parts, 2, tokens // parts, state), F32),
-        scratch_shapes=[
-            pltpu.VMEM((2, state, wide), BF16),
-            pltpu.VMEM((2, state, wide), BF16),
-            pltpu.VMEM((2, tokens, state), F32),
-        ],
+        scratch_shapes=slots + [pltpu.VMEM((2, tokens, state), F32)],
         compiler_params=PARAMS,
         name="grads",
-    )(flag, entering, other, xh, xl, gh, gl, grads_loc)
-
-    mixed, grad_inputs = pl.pallas_call(
-        functools.partial(outputs_kernel, group, width),
-        grid=(groups,),
-        in_specs=[SMEM, state_spec, state_spec, tok, tok] + small,
-        out_specs=[tok, tok],
-        out_shape=[coded, coded],
-        scratch_shapes=[
-            pltpu.VMEM((2, state, wide), BF16),
-            pltpu.VMEM((2, state, wide), BF16),
-            weights,
-        ],
-        compiler_params=PARAMS,
-        cost_estimate=pl.CostEstimate(
-            flops=8 * tokens * state * channels,
-            transcendentals=2 * heads * tokens,
-            bytes_accessed=16 * tokens * channels,
-        ),
-        name="outputs",
-    )(flag, entering, other, mixed_loc, gx_loc, step_size, decay, doc, b_in, c_in)
+    )(flag, enter_f, other_f, enter_b, other_b, xh, xl, gh, gl, grads_loc)
+
+    def finish(kind, first, own, other, base, proj, name):
+        return pl.pallas_call(
+            functools.partial(output_kernel, group, width),
+            grid=(groups,),
+            in_specs=[
+                SMEM,
+                state_spec,
+                state_spec,
+                tok,
+                pl.BlockSpec((1, 1, 2, tokens, group), lambda i: (kind, i, 0, 0, 0)),
+                whole((tokens, state)),
+            ],
+            out_specs=tok,
+            out_shape=coded,
+            scratch_shapes=[pltpu.VMEM((state, wide), BF16)] * 2,
+            compiler_params=PARAMS,
+            cost_estimate=pl.CostEstimate(
+                flops=4 * tokens * state * channels,
+                transcendentals=0,
+                bytes_accessed=8 * tokens * channels,
+            ),
+            name=name,
+        )(first, own, other, base, scales, proj)
 
     if tensor == 4 and parts == 4:
         place = lax.axis_index("tensor")
         pick = lambda at: lax.dynamic_index_in_dim(grads, at, 0, False)
-        total = pick(place)
-        for k in (2, 3, 1):
-            total = total + swap_with(pick(place ^ k), "tensor", k)
-        total = total.astype(BF16)
+        own, leaving = pick(place), [pick(place ^ k) for k in (2, 3, 1)]
+        own, leaving, first = lax.optimization_barrier((own, leaving, flag))
+        landed = [swap_with(v, "tensor", k) for k, v in zip((2, 3, 1), leaving)]
+        mixed = finish(1, first, enter_f, other_f, mixed_loc, c_in, "mixed")
+        landed, mixed = lax.optimization_barrier((landed, mixed))
+        total = (own + landed[0] + landed[1] + landed[2]).astype(BF16)
+        total, first = lax.optimization_barrier((total, first))
+        landed = [swap_with(total, "tensor", k) for k in (2, 3, 1)]
+        grad_inputs = finish(0, first, enter_b, other_b, gx_loc, b_in, "grad_inputs")
+        landed, grad_inputs = lax.optimization_barrier((landed, grad_inputs))
         summed = jnp.zeros((parts,) + total.shape, BF16)
         summed = lax.dynamic_update_index_in_dim(summed, total, place, 0)
-        for k in (2, 3, 1):
-            summed = lax.dynamic_update_index_in_dim(
-                summed, swap_with(total, "tensor", k), place ^ k, 0
-            )
+        for k, v in zip((2, 3, 1), landed):
+            summed = lax.dynamic_update_index_in_dim(summed, v, place ^ k, 0)
     else:
+        mixed = finish(1, flag, enter_f, other_f, mixed_loc, c_in, "mixed")
+        grad_inputs = finish(0, flag, enter_b, other_b, gx_loc, b_in, "grad_inputs")
         summed = lax.psum(grads, "tensor").astype(BF16)
     grad_b = summed[:, 0].reshape(tokens, state)
     grad_c = summed[:, 1].reshape(tokens, state)

time: 82.1 us -> 69.7 us (0.85)
  waiting for transfers between devices: 25 us -> 8.04 us
  local copies, waits for them, and re-layouts: 10.4 us -> 16.8 us
  other arithmetic: 7.2 us -> 5.37 us
  Pallas kernels: 25 us -> 23.5 us
  starting transfers between devices: 12.9 us -> 14.3 us
    ppermute x11 -> x13, waiting for transfers between devices: 25 us -> 8.04 us  [swap_with(): return lax.ppermute(value, axis, [(i, i ^ mask) for i in range(size)])]
    unnamed x37 -> x58, local copies, waits for them, and re-layouts: 7.87 us -> 15.2 us
    another operation x8 -> x0, other arithmetic: 7.03 us -> none
    select_n x0 -> x1, other arithmetic: none -> 3.61 us  [shards(): jnp.where(lower, after, own_b + own_e * after)]
    convert_element_type x3 -> x2, other arithmetic: 0.11 us -> 1.56 us  [the longest x1 1.55 us: encode(): return jnp.concatenate([v.astype(jnp.float16) for v in rows], 0)]
    ppermute x11 -> x13, starting transfers between devices: 12.9 us -> 14.3 us  [swap_with(): return lax.ppermute(value, axis, [(i, i ^ mask) for i in range(size)])]
    pallas_call x1, Pallas kernels: 4.13 us -> 2.86 us  [shards(): pl.pallas_call(functools.partial(grads_kernel, parts), grid=(groups,), in...]
    pallas_call x1, Pallas kernels: 10.5 us -> 9.44 us  [shards(): pl.pallas_call(functools.partial(local_kernel, group, width), grid=(group...]
  transfers between devices with their start and end apart: 11 -> 13, of which waited for: 7 -> 7; matrix products, arithmetic and copies ran while one was open for 2% -> 1% of each run, Pallas kernels for 20% -> 22%
where the time goes in v2:
time: 69.7 us; the launch traced here: 69 us
  Pallas kernels  23.5 us (34%)
  local copies, waits for them, and re-layouts  16.8 us (24%)
  starting transfers between devices  14.3 us (21%)
  waiting for transfers between devices  8.04 us (12%)
  other arithmetic  5.37 us (8%)
  between operations  0.95 us (1%)
    unnamed x58, local copies, waits for them, and re-layouts  15.2 us
    ppermute x13, starting transfers between devices, swap_with(): return lax.ppermute(value, axis, [(i, i ^ mask) for i in range(size)])  14.3 us
    pallas_call x1, Pallas kernels, shards(): pl.pallas_call(functools.partial(local_kernel, group, width), grid=(group...  9.44 us
    ppermute x13, waiting for transfers between devices, swap_with(): return lax.ppermute(value, axis, [(i, i ^ mask) for i in range(size)])  8.04 us
    pallas_call x2, Pallas kernels, finish(): pl.pallas_call(functools.partial(output_kernel, group, width), grid=(grou...  5.8 us
    pallas_call x1, Pallas kernels, shards(): pl.pallas_call(functools.partial(states_kernel, group, width), grid=(grou...  5.44 us
    select_n x1, other arithmetic, shards(): jnp.where(lower, after, own_b + own_e * after)  3.61 us
    pallas_call x1, Pallas kernels, shards(): pl.pallas_call(functools.partial(grads_kernel, parts), grid=(groups,), in...  2.86 us
  transfers between devices with their start and end apart: 13, of which 7 were waited for; matrix products, arithmetic and copies ran while one was open for 1% of the time, Pallas kernels for 22%

profile of v2, /device:TPU:0, one launch (start us, length us, event | category | flops | bytes accessed | tf_op | source)
XLA Modules:
  0.0 69.0 jit_solution(1749489122589085789)
XLA Ops:
  0.6 1.2 %copy-done.4 = bf16[256,2048]{1,0:T(8,128)(2,1)S(1)} copy-done((bf16[256,2048]{1,0:T(8,128)(2,1)S(1)}, bf16[256,2048]{1,0:T(8,128)(2,1)}, u32[]{:S(2)}) %copy-start.4) | copy-done | bytes 1048600
  1.9 1.2 %copy-done.6 = bf16[256,2048]{1,0:T(8,128)(2,1)S(1)} copy-done((bf16[256,2048]{1,0:T(8,128)(2,1)S(1)}, bf16[256,2048]{1,0:T(8,128)(2,1)}, u32[]{:S(2)}) %copy-start.6) | copy-done | bytes 1048600
  3.1 0.8 %copy-done.16 = bf16[256,128]{1,0:T(8,128)(2,1)S(1)} copy-done((bf16[256,128]{1,0:T(8,128)(2,1)S(1)}, bf16[256,128]{1,0:T(8,128)(2,1)}, u32[]{:S(2)}) %copy-start.16) | copy-done | bytes 65560
  3.9 0.8 %copy-done.18 = bf16[256,128]{1,0:T(8,128)(2,1)S(1)} copy-done((bf16[256,128]{1,0:T(8,128)(2,1)S(1)}, bf16[256,128]{1,0:T(8,128)(2,1)}, u32[]{:S(2)}) %copy-start.18) | copy-done | bytes 65560
  4.8 0.8 %copy-done.20 = f32[32,256]{1,0:T(8,128)S(1)} copy-done((f32[32,256]{1,0:T(8,128)S(1)}, f32[32,256]{1,0:T(8,128)}, u32[]{:S(2)}) %copy-start.20) | copy-done | bytes 32792
  5.5 0.7 copy-done.22
  6.9 5.4 %states.1 = (f32[16,128,128]{2,1,0:T(8,128)S(1)}, f32[16,128,128]{2,1,0:T(8,128)}, f32[8,16,128]{2,1,0:T(8,128)S(1)}) custom-call(s32[1]{0:T(128)} %bitcast.core_ref, bf16[256,2048]{1,0:T(8,128)(2,1)S(1)} %copy-done.4, bf16[256,2048]{1,0:T(8,128)(2,1)S(1)} %copy-done.6, f32[32,256]{1,0:T(8,128)S(1)} %copy-done.20, f32[1,32]{1,0:T(1,128)S(1)} %bitcast.74, ...), custom_call_target="tpu_custom_call" | custom-call | tf_op jit(solution)/shard_map/states/pallas_call | solution.py:445
  13.6 1.6 %collective-permute-done = f32[8,16,128]{2,1,0:T(8,128)S(1)} collective-permute-done((f32[8,16,128]{2,1,0:T(8,128)S(1)}, f32[8,16,128]{2,1,0:T(8,128)S(1)}, u32[]{:S(2)}, u32[]{:S(2)}) %collective-permute-start) | collective-permute-done | bytes 65568 | tf_op jit(solution)/shard_map/ppermute | solution.py:357
  15.6 1.5 %multiply_convert_fusion = (f16[16,64,128]{2,1,0:T(8,128)(2,1)S(1)}, f16[16,64,128]{2,1,0:T(8,128)(2,1)S(1)}) fusion(f32[16,128]{1,0:T(8,128)S(1)} %get-tuple-element.72, pred[]{:T(512)S(6)} %eq.19, f32[16,128,128]{2,1,0:T(8,128)} %collective-permute-done.1, f32[16,128]{1,0:T(8,128)S(1)} %get-tuple-element.78, f32[16,128,128]{2,1,0:T(8,128)S(1)} %get-tuple-element.38, ...), kind=kLoop, calls=%fused_computation.16 | loop fusion | flops 1572864 | bytes 2670594 | tf_op jit(solution)/shard_map/convert_element_type | solution.py:387
  17.4 2.9 %collective-permute-start.3 = (f16[1088,128]{1,0:T(8,128)(2,1)S(1)}, f16[1088,128]{1,0:T(8,128)(2,1)S(1)}, u32[]{:S(2)}, u32[]{:S(2)}) collective-permute-start(f16[1088,128]{1,0:T(8,128)(2,1)S(1)} %get-tuple-element.41), channel_id=1, source_target_pairs={{0,16},{4,20},{8,24},{12,28},{16,0},{20,4},{24,8},{28,12},{1,17},{... | collective-permute-start | bytes 835592 | tf_op jit(solution)/shard_map/ppermute | solution.py:357
  20.4 1.4 %collective-permute-start.4 = (f16[1088,128]{1,0:T(8,128)(2,1)S(1)}, f16[1088,128]{1,0:T(8,128)(2,1)S(1)}, u32[]{:S(2)}, u32[]{:S(2)}) collective-permute-start(f16[1088,128]{1,0:T(8,128)(2,1)S(1)} %get-tuple-element.41), channel_id=1, source_target_pairs={{0,24},{4,28},{8,16},{12,20},{16,8},{20,12},{24,0},{28,4},{1,25},{... | collective-permute-start | bytes 835592 | tf_op jit(solution)/shard_map/ppermute | solution.py:357
  22.0 1.2 %copy-done.7 = bf16[256,2048]{1,0:T(8,128)(2,1)S(1)} copy-done((bf16[256,2048]{1,0:T(8,128)(2,1)S(1)}, bf16[256,2048]{1,0:T(8,128)(2,1)}, u32[]{:S(2)}) %copy-start.7) | copy-done | bytes 1048600
  23.2 0.8 %copy-done.21 = f32[32,256]{1,0:T(8,128)S(1)} copy-done((f32[32,256]{1,0:T(8,128)S(1)}, f32[32,256]{1,0:T(8,128)}, u32[]{:S(2)}) %copy-start.21) | copy-done | bytes 32792
  24.0 9.4 %local.1 = (f32[256,2048]{1,0:T(8,128)S(1)}, f32[256,2048]{1,0:T(8,128)S(1)}, bf16[256,2048]{1,0:T(8,128)(2,1)S(1)}, bf16[256,2048]{1,0:T(8,128)(2,1)S(1)}, bf16...) custom-call(f32[32]{0:T(128)S(1)} %copy-done.26, ...), custom_call_target="tpu_custom_call" | custom-call | flops 2684354560 | bytes 10485760 | tf_op jit(solution)/shard_map/local/pallas_call | solution.py:501
  33.4 1.0 %copy-done.12 = bf16[256,2048]{1,0:T(8,128)(2,1)} copy-done((bf16[256,2048]{1,0:T(8,128)(2,1)}, bf16[256,2048]{1,0:T(8,128)(2,1)S(1)}, u32[]{:S(2)}) %copy-start.12) | copy-done | bytes 1048600
  34.4 1.0 %copy-done.14 = bf16[256,2048]{1,0:T(8,128)(2,1)} copy-done((bf16[256,2048]{1,0:T(8,128)(2,1)}, bf16[256,2048]{1,0:T(8,128)(2,1)S(1)}, u32[]{:S(2)}) %copy-start.14) | copy-done | bytes 1048600
  35.7 3.6 %add_select_fusion = (f32[16,64,128]{2,1,0:T(8,128)}, f32[16,64,128]{2,1,0:T(8,128)}, f32[16,64,128]{2,1,0:T(8,128)S(1)}, f32[16,64,128]{2,1,0:T(8,128)S(1)}) fusion(f32[16,128,128]{2,1,0:T(8,128)S(1)} %get-tuple-element.38, f32[16,128]{1,0:T(8,128)S(1)} %copy-done.27, pred[]{:T(512)S(6)} %eq.15, f32[16,128]{1,0:T(8,128)S(1)} %get-tuple-element.90, ...), kind=kLoop, calls=%fused_computation.12 | loop fusion | flops 3670016 | bytes 5038083 | tf_op jit(solution)/shard_map/jit(_where)/select_n | solution.py:551
  39.9 1.6 %collective-permute-done.5.other_f.other = f32[16,64,128]{2,1,0:T(8,128)S(1)} collective-permute-done((f32[16,64,128]{2,1,0:T(8,128)}, f32[16,64,128]{2,1,0:T(8,128)S(1)}, u32[]{:S(2)}, u32[]{:S(2)}) %collective-permute-start.5) | collective-permute-done | bytes 524320 | tf_op jit(solution)/shard_map/ppermute | solution.py:357
  41.5 0.7 %collective-permute-done.6.other_b.other = f32[16,64,128]{2,1,0:T(8,128)S(1)} collective-permute-done((f32[16,64,128]{2,1,0:T(8,128)}, f32[16,64,128]{2,1,0:T(8,128)S(1)}, u32[]{:S(2)}, u32[]{:S(2)}) %collective-permute-start.6) | collective-permute-done | bytes 524320 | tf_op jit(solution)/shard_map/ppermute | solution.py:357
  42.2 1.2 %copy-done.9 = bf16[256,2048]{1,0:T(8,128)(2,1)S(1)} copy-done((bf16[256,2048]{1,0:T(8,128)(2,1)S(1)}, bf16[256,2048]{1,0:T(8,128)(2,1)}, u32[]{:S(2)}) %copy-start.9) | copy-done | bytes 1048600
  43.5 1.2 %copy-done.11 = bf16[256,2048]{1,0:T(8,128)(2,1)S(1)} copy-done((bf16[256,2048]{1,0:T(8,128)(2,1)S(1)}, bf16[256,2048]{1,0:T(8,128)(2,1)}, u32[]{:S(2)}) %copy-start.11) | copy-done | bytes 1048600
  44.7 1.2 %copy-done.13 = bf16[256,2048]{1,0:T(8,128)(2,1)S(1)} copy-done((bf16[256,2048]{1,0:T(8,128)(2,1)S(1)}, bf16[256,2048]{1,0:T(8,128)(2,1)}, u32[]{:S(2)}) %copy-start.13) | copy-done | bytes 1048600
  45.9 1.2 %copy-done.15 = bf16[256,2048]{1,0:T(8,128)(2,1)S(1)} copy-done((bf16[256,2048]{1,0:T(8,128)(2,1)S(1)}, bf16[256,2048]{1,0:T(8,128)(2,1)}, u32[]{:S(2)}) %copy-start.15) | copy-done | bytes 1048600
  47.1 2.9 %grads.1 = f32[4,2,64,128]{3,2,1,0:T(8,128)S(1)} custom-call(s32[1]{0:T(128)} %bitcast.core_ref, f32[16,64,128]{2,1,0:T(8,128)S(1)} %get-tuple-element.85.own_f.own, f32[16,64,128]{2,1,0:T(8,128)S(1)} %collective-permute-done.5.other_f.other, f32[16,64,128]{2,1,0:T(8,128)S(1)} %get-tuple-element.86.own_b.own, ...), custom_call_target="tpu_custom_call" | custom-call | tf_op jit(solution)/shard_map/grads/pallas_call | solution.py:558
  50.1 3.1 %collective-permute-start.7 = (f32[2,64,128]{2,1,0:T(8,128)S(1)}, f32[2,64,128]{2,1,0:T(8,128)S(1)}, u32[]{:S(2)}, u32[]{:S(2)}) collective-permute-start(f32[2,64,128]{2,1,0:T(8,128)S(1)} %get-tuple-element.52), channel_id=1, source_target_pairs={{0,2},{1,3},{2,0},{3,1},{4,6},{5,7},{6,4},{7,5},{8,10},{9,11},{10,... | collective-permute-start | bytes 196616 | tf_op jit(solution)/shard_map/ppermute | solution.py:357
  53.1 1.3 %collective-permute-start.8 = (f32[2,64,128]{2,1,0:T(8,128)S(1)}, f32[2,64,128]{2,1,0:T(8,128)S(1)}, u32[]{:S(2)}, u32[]{:S(2)}) collective-permute-start(f32[2,64,128]{2,1,0:T(8,128)S(1)} %get-tuple-element.53), channel_id=1, source_target_pairs={{0,3},{1,2},{2,1},{3,0},{4,7},{5,6},{6,5},{7,4},{8,11},{9,10},{10,... | collective-permute-start | bytes 196616 | tf_op jit(solution)/shard_map/ppermute | solution.py:357
  54.7 2.9 %mixed.1 = bf16[256,2048]{1,0:T(8,128)(2,1)} custom-call(s32[1]{0:T(128)} %bitcast.core_ref, f32[16,64,128]{2,1,0:T(8,128)S(1)} %get-tuple-element.85.own_f.own, f32[16,64,128]{2,1,0:T(8,128)S(1)} %collective-permute-done.5.other_f.other, f32[256,2048]{1,0:T(8,128)S(1)} %copy-done.3, bf16[2,4,2,256,8]{4,3,2,1,0:T(8,128)(2,1)S(1)} %get-tuple-element.57.coded_ref, ...), custom_call_target="tpu_custom_call" | custom-call | flops 268435456 | bytes 4194304 | tf_op jit(solution)/shard_map/mixed/pallas_call | solution.py:570
  57.6 1.9 %collective-permute-done.8 = f32[2,64,128]{2,1,0:T(8,128)S(1)} collective-permute-done((f32[2,64,128]{2,1,0:T(8,128)S(1)}, f32[2,64,128]{2,1,0:T(8,128)S(1)}, u32[]{:S(2)}, u32[]{:S(2)}) %collective-permute-start.8) | collective-permute-done | bytes 65568 | tf_op jit(solution)/shard_map/ppermute | solution.py:357
  59.7 2.8 %collective-permute-start.10 = (bf16[2,64,128]{2,1,0:T(8,128)(2,1)S(1)}, bf16[2,64,128]{2,1,0:T(8,128)(2,1)S(1)}, u32[]{:S(2)}, u32[]{:S(2)}) collective-permute-start(bf16[2,64,128]{2,1,0:T(8,128)(2,1)S(1)} %add_convert_fusion), channel_id=1, source_target_pairs={{0,2},{1,3},{2,0},{3,1},{4,6},{5,7},{6,4},{7,5},{8,10},{9,11},{10,... | collective-permute-start | bytes 98312 | tf_op jit(solution)/shard_map/ppermute | solution.py:357
  62.5 0.7 collective-permute-start.11
  63.8 2.9 %grad_inputs.1 = bf16[256,2048]{1,0:T(8,128)(2,1)} custom-call(s32[1]{0:T(128)} %bitcast.core_ref, f32[16,64,128]{2,1,0:T(8,128)S(1)} %get-tuple-element.86.own_b.own, f32[16,64,128]{2,1,0:T(8,128)S(1)} %collective-permute-done.6.other_b.other, f32[256,2048]{1,0:T(8,128)S(1)} %copy-done.1, bf16[2,4,2,256,8]{4,3,2,1,0:T(8,128)(2,1)S(1)} %get-tuple-element.57.coded_ref, ...), custom_call_target="tpu_custom_call" | custom-call | flops 268435456 | bytes 4194304 | tf_op jit(solution)/shard_map/grad_inputs/pallas_call | solution.py:570
  66.7 1.6 %collective-permute-done.11 = bf16[2,64,128]{2,1,0:T(8,128)(2,1)S(1)} collective-permute-done((bf16[2,64,128]{2,1,0:T(8,128)(2,1)S(1)}, bf16[2,64,128]{2,1,0:T(8,128)(2,1)S(1)}, u32[]{:S(2)}, u32[]{:S(2)}) %collective-permute-start.11) | collective-permute-done | bytes 32800 | tf_op jit(solution)/shard_map/ppermute | solution.py:357
  (80 shorter events, 5.2 us)
Async XLA Ops:
  0.6 1.2 %copy-start.4 = (bf16[256,2048]{1,0:T(8,128)(2,1)S(1)}, bf16[256,2048]{1,0:T(8,128)(2,1)}, u32[]{:S(2)}) copy-start(bf16[256,2048]{1,0:T(8,128)(2,1)} %x_ref.1) | copy-start | bytes 3145732
  1.9 1.2 %copy-start.6 = (bf16[256,2048]{1,0:T(8,128)(2,1)S(1)}, bf16[256,2048]{1,0:T(8,128)(2,1)}, u32[]{:S(2)}) copy-start(bf16[256,2048]{1,0:T(8,128)(2,1)} %g_ref.1) | copy-start | bytes 3145732
  12.3 9.6 %copy-start.5 = (bf16[256,2048]{1,0:T(8,128)(2,1)S(1)}, bf16[256,2048]{1,0:T(8,128)(2,1)}, u32[]{:S(2)}) copy-start(bf16[256,2048]{1,0:T(8,128)(2,1)} %x_ref.1) | copy-start | bytes 3145732
  12.3 9.6 %copy-start.17 = (bf16[256,128]{1,0:T(8,128)(2,1)S(1)}, bf16[256,128]{1,0:T(8,128)(2,1)}, u32[]{:S(2)}) copy-start(bf16[256,128]{1,0:T(8,128)(2,1)} %proj_ref.2) | copy-start | bytes 196612
  12.3 9.6 %copy-start.19 = (bf16[256,128]{1,0:T(8,128)(2,1)S(1)}, bf16[256,128]{1,0:T(8,128)(2,1)}, u32[]{:S(2)}) copy-start(bf16[256,128]{1,0:T(8,128)(2,1)} %proj_ref.3) | copy-start | bytes 196612
  12.3 9.6 %copy-start.23 = (s32[256]{0:T(256)S(1)}, s32[256]{0:T(256)}, u32[]{:S(2)}) copy-start(s32[256]{0:T(256)} %param.14) | copy-start | bytes 3076
  12.4 9.6 %copy-start.25 = (f32[32]{0:T(128)S(1)}, f32[32]{0:T(128)}, u32[]{:S(2)}) copy-start(f32[32]{0:T(128)} %param.10) | copy-start | bytes 388
  12.4 9.6 %copy-start.26 = (f32[32]{0:T(128)S(1)}, f32[32]{0:T(128)}, u32[]{:S(2)}) copy-start(f32[32]{0:T(128)} %skip_ref) | copy-start | bytes 388
  12.4 3.2 %collective-permute-start.1 = (f32[16,128,128]{2,1,0:T(8,128)}, f32[16,128,128]{2,1,0:T(8,128)}, u32[]{:S(2)}, u32[]{:S(2)}) collective-permute-start(f32[16,128,128]{2,1,0:T(8,128)} %get-tuple-element.39), channel_id=1, source_target_pairs={{0,4},{4,0},{8,12},{12,8},{16,20},{20,16},{24,28},{28,24},{1,5},{5... | collective-permute-start | bytes 3145736 | tf_op jit(solution)/shard_map/ppermute | solution.py:357
  12.9 2.3 %collective-permute-start = (f32[8,16,128]{2,1,0:T(8,128)S(1)}, f32[8,16,128]{2,1,0:T(8,128)S(1)}, u32[]{:S(2)}, u32[]{:S(2)}) collective-permute-start(f32[8,16,128]{2,1,0:T(8,128)S(1)} %get-tuple-element.37), channel_id=1, source_target_pairs={{0,4},{4,0},{8,12},{12,8},{16,20},{20,16},{24,28},{28,24},{1,5},{5... | collective-permute-start | bytes 196616 | tf_op jit(solution)/shard_map/ppermute | solution.py:357
  17.4 18.0 %collective-permute-start.3 = (f16[1088,128]{1,0:T(8,128)(2,1)S(1)}, f16[1088,128]{1,0:T(8,128)(2,1)S(1)}, u32[]{:S(2)}, u32[]{:S(2)}) collective-permute-start(f16[1088,128]{1,0:T(8,128)(2,1)S(1)} %get-tuple-element.41), channel_id=1, source_target_pairs={{0,16},{4,20},{8,24},{12,28},{16,0},{20,4},{24,8},{28,12},{1,17},{... | collective-permute-start | bytes 835592 | tf_op jit(solution)/shard_map/ppermute | solution.py:357
  20.4 15.0 %collective-permute-start.4 = (f16[1088,128]{1,0:T(8,128)(2,1)S(1)}, f16[1088,128]{1,0:T(8,128)(2,1)S(1)}, u32[]{:S(2)}, u32[]{:S(2)}) collective-permute-start(f16[1088,128]{1,0:T(8,128)(2,1)S(1)} %get-tuple-element.41), channel_id=1, source_target_pairs={{0,24},{4,28},{8,16},{12,20},{16,8},{20,12},{24,0},{28,4},{1,25},{... | collective-permute-start | bytes 835592 | tf_op jit(solution)/shard_map/ppermute | solution.py:357
  21.8 13.6 %collective-permute-start.2 = (f16[1088,128]{1,0:T(8,128)(2,1)S(1)}, f16[1088,128]{1,0:T(8,128)(2,1)S(1)}, u32[]{:S(2)}, u32[]{:S(2)}) collective-permute-start(f16[1088,128]{1,0:T(8,128)(2,1)S(1)} %get-tuple-element.40), channel_id=1, source_target_pairs={{0,8},{4,12},{8,0},{12,4},{16,24},{20,28},{24,16},{28,20},{1,9},{5... | collective-permute-start | bytes 835592 | tf_op jit(solution)/shard_map/ppermute | solution.py:357
  22.0 1.2 %copy-start.7 = (bf16[256,2048]{1,0:T(8,128)(2,1)S(1)}, bf16[256,2048]{1,0:T(8,128)(2,1)}, u32[]{:S(2)}) copy-start(bf16[256,2048]{1,0:T(8,128)(2,1)} %g_ref.1) | copy-start | bytes 3145732
  24.0 11.7 %copy-start.27 = (f32[16,128]{1,0:T(8,128)S(1)}, f32[16,128]{1,0:T(8,128)}, u32[]{:S(2)}) copy-start(f32[16,128]{1,0:T(8,128)} %slice_bitcast_fusion.3) | copy-start | bytes 24580
  35.4 3.9 %copy-start = (f32[256,2048]{1,0:T(8,128)}, f32[256,2048]{1,0:T(8,128)S(1)}, u32[]{:S(2)}) copy-start(f32[256,2048]{1,0:T(8,128)S(1)} %get-tuple-element.65.base_ref) | copy-start | bytes 6291460
  35.4 3.9 %copy-start.2 = (f32[256,2048]{1,0:T(8,128)}, f32[256,2048]{1,0:T(8,128)S(1)}, u32[]{:S(2)}) copy-start(f32[256,2048]{1,0:T(8,128)S(1)} %get-tuple-element.56.base_ref) | copy-start | bytes 6291460
  35.4 3.9 %copy-start.8 = (bf16[256,2048]{1,0:T(8,128)(2,1)}, bf16[256,2048]{1,0:T(8,128)(2,1)S(1)}, u32[]{:S(2)}) copy-start(bf16[256,2048]{1,0:T(8,128)(2,1)S(1)} %get-tuple-element.47.xh_ref) | copy-start | bytes 3145732
  35.4 3.9 %copy-start.10 = (bf16[256,2048]{1,0:T(8,128)(2,1)}, bf16[256,2048]{1,0:T(8,128)(2,1)S(1)}, u32[]{:S(2)}) copy-start(bf16[256,2048]{1,0:T(8,128)(2,1)S(1)} %get-tuple-element.48.xl_ref) | copy-start | bytes 3145732
  39.3 2.2 %collective-permute-start.5 = (f32[16,64,128]{2,1,0:T(8,128)}, f32[16,64,128]{2,1,0:T(8,128)S(1)}, u32[]{:S(2)}, u32[]{:S(2)}) collective-permute-start(f32[16,64,128]{2,1,0:T(8,128)} %get-tuple-element.82), channel_id=1, source_target_pairs={{0,4},{4,0},{8,12},{12,8},{16,20},{20,16},{24,28},{28,24},{1,5},{5... | collective-permute-start | bytes 1572872 | tf_op jit(solution)/shard_map/ppermute | solution.py:357
  39.4 2.9 %collective-permute-start.6 = (f32[16,64,128]{2,1,0:T(8,128)}, f32[16,64,128]{2,1,0:T(8,128)S(1)}, u32[]{:S(2)}, u32[]{:S(2)}) collective-permute-start(f32[16,64,128]{2,1,0:T(8,128)} %get-tuple-element.81), channel_id=1, source_target_pairs={{0,4},{4,0},{8,12},{12,8},{16,20},{20,16},{24,28},{28,24},{1,5},{5... | collective-permute-start | bytes 1572872 | tf_op jit(solution)/shard_map/ppermute | solution.py:357
  42.2 1.2 %copy-start.9 = (bf16[256,2048]{1,0:T(8,128)(2,1)S(1)}, bf16[256,2048]{1,0:T(8,128)(2,1)}, u32[]{:S(2)}) copy-start(bf16[256,2048]{1,0:T(8,128)(2,1)} %copy-done.8) | copy-start | bytes 3145732
  43.5 1.2 %copy-start.11 = (bf16[256,2048]{1,0:T(8,128)(2,1)S(1)}, bf16[256,2048]{1,0:T(8,128)(2,1)}, u32[]{:S(2)}) copy-start(bf16[256,2048]{1,0:T(8,128)(2,1)} %copy-done.10) | copy-start | bytes 3145732
  44.7 1.2 %copy-start.13 = (bf16[256,2048]{1,0:T(8,128)(2,1)S(1)}, bf16[256,2048]{1,0:T(8,128)(2,1)}, u32[]{:S(2)}) copy-start(bf16[256,2048]{1,0:T(8,128)(2,1)} %copy-done.12) | copy-start | bytes 3145732
  47.1 7.6 %copy-start.3 = (f32[256,2048]{1,0:T(8,128)S(1)}, f32[256,2048]{1,0:T(8,128)}, u32[]{:S(2)}) copy-start(f32[256,2048]{1,0:T(8,128)} %copy-done.2) | copy-start | bytes 6291460
  50.1 7.6 %collective-permute-start.7 = (f32[2,64,128]{2,1,0:T(8,128)S(1)}, f32[2,64,128]{2,1,0:T(8,128)S(1)}, u32[]{:S(2)}, u32[]{:S(2)}) collective-permute-start(f32[2,64,128]{2,1,0:T(8,128)S(1)} %get-tuple-element.52), channel_id=1, source_target_pairs={{0,2},{1,3},{2,0},{3,1},{4,6},{5,7},{6,4},{7,5},{8,10},{9,11},{10,... | collective-permute-start | bytes 196616 | tf_op jit(solution)/shard_map/ppermute | solution.py:357
  53.1 6.4 %collective-permute-start.8 = (f32[2,64,128]{2,1,0:T(8,128)S(1)}, f32[2,64,128]{2,1,0:T(8,128)S(1)}, u32[]{:S(2)}, u32[]{:S(2)}) collective-permute-start(f32[2,64,128]{2,1,0:T(8,128)S(1)} %get-tuple-element.53), channel_id=1, source_target_pairs={{0,3},{1,2},{2,1},{3,0},{4,7},{5,6},{6,5},{7,4},{8,11},{9,10},{10,... | collective-permute-start | bytes 196616 | tf_op jit(solution)/shard_map/ppermute | solution.py:357
  54.5 5.2 %collective-permute-start.9 = (f32[2,64,128]{2,1,0:T(8,128)S(1)}, f32[2,64,128]{2,1,0:T(8,128)S(1)}, u32[]{:S(2)}, u32[]{:S(2)}) collective-permute-start(f32[2,64,128]{2,1,0:T(8,128)S(1)} %get-tuple-element.54), channel_id=1, source_target_pairs={{0,1},{1,0},{2,3},{3,2},{4,5},{5,4},{6,7},{7,6},{8,9},{9,8},{10,11... | collective-permute-start | bytes 196616 | tf_op jit(solution)/shard_map/ppermute | solution.py:357
  54.7 9.0 %copy-start.1 = (f32[256,2048]{1,0:T(8,128)S(1)}, f32[256,2048]{1,0:T(8,128)}, u32[]{:S(2)}) copy-start(f32[256,2048]{1,0:T(8,128)} %copy-done) | copy-start | bytes 6291460
  59.7 6.9 %collective-permute-start.10 = (bf16[2,64,128]{2,1,0:T(8,128)(2,1)S(1)}, bf16[2,64,128]{2,1,0:T(8,128)(2,1)S(1)}, u32[]{:S(2)}, u32[]{:S(2)}) collective-permute-start(bf16[2,64,128]{2,1,0:T(8,128)(2,1)S(1)} %add_convert_fusion), channel_id=1, source_target_pairs={{0,2},{1,3},{2,0},{3,1},{4,6},{5,7},{6,4},{7,5},{8,10},{9,11},{10,... | collective-permute-start | bytes 98312 | tf_op jit(solution)/shard_map/ppermute | solution.py:357
  62.5 5.7 %collective-permute-start.11 = (bf16[2,64,128]{2,1,0:T(8,128)(2,1)S(1)}, bf16[2,64,128]{2,1,0:T(8,128)(2,1)S(1)}, u32[]{:S(2)}, u32[]{:S(2)}) collective-permute-start(bf16[2,64,128]{2,1,0:T(8,128)(2,1)S(1)} %add_convert_fusion), channel_id=1, source_target_pairs={{0,3},{1,2},{2,1},{3,0},{4,7},{5,6},{6,5},{7,4},{8,11},{9,10},{10,... | collective-permute-start | bytes 98312 | tf_op jit(solution)/shard_map/ppermute | solution.py:357
  63.2 5.0 %collective-permute-start.12 = (bf16[2,64,128]{2,1,0:T(8,128)(2,1)S(1)}, bf16[2,64,128]{2,1,0:T(8,128)(2,1)S(1)}, u32[]{:S(2)}, u32[]{:S(2)}) collective-permute-start(bf16[2,64,128]{2,1,0:T(8,128)(2,1)S(1)} %add_convert_fusion), channel_id=1, source_target_pairs={{0,1},{1,0},{2,3},{3,2},{4,5},{5,4},{6,7},{7,6},{8,9},{9,8},{10,11... | collective-permute-start | bytes 98312 | tf_op jit(solution)/shard_map/ppermute | solution.py:357
  (9 other events, 7.7 us)

commit v3 on v2

--- a/solution.py
+++ b/solution.py
@@ -349,7 +349,7 @@
 
 SMEM = pl.BlockSpec(memory_space=pltpu.SMEM)
 HBM = pl.BlockSpec(memory_space=pltpu.HBM)
-PARAMS = pltpu.CompilerParams(vmem_limit_bytes=24 << 20)
+PARAMS = pltpu.CompilerParams(vmem_limit_bytes=60 << 20)
 
 
 def swap_with(value, axis, mask):
@@ -390,8 +390,8 @@
 def decode(coded, chunks):
     size = coded.shape[0] - 4 * chunks
     rows = [coded[size + k * chunks : size + (k + 1) * chunks].astype(F32) for k in range(4)]
-    state = coded[:size].reshape(chunks, -1, LANES).astype(F32)
-    return state * jnp.exp2(rows[3] - 14.0)[:, None], jnp.exp(rows[0] + rows[1] + rows[2])[:, None]
+    state = coded[:size].reshape(chunks, -1, LANES)
+    return state, jnp.exp2(rows[3] - 14.0), jnp.exp(rows[0] + rows[1] + rows[2])
 
 
 def chip_place(axis):
@@ -410,16 +410,25 @@
 
 def join_chips(arrived, axis, chunks):
     x, y = chip_place(axis)
-    (one, decay_one), (two, decay_two), (three, decay_three) = [decode(v, chunks) for v in arrived]
-    same = x == y
-    close = jnp.where(same, two, three)
-    decay_close = jnp.where(same, decay_two, decay_three)
-    distant = jnp.where(same, three, two)
-    beyond = close + decay_close * distant
-    main = jnp.where(same, one + decay_one * beyond, beyond)
-    side = jnp.where(same, 0.0, one)
-    upper = y == 1
-    return jnp.where(upper, main, side), jnp.where(upper, side, main)
+    states, scales, decays = zip(*[decode(v, chunks) for v in arrived])
+    _, two, three = decays
+    same, upper = x == y, y == 1
+    beyond = jnp.where(same, decays[0], 1.0)
+    weights = [
+        jnp.ones_like(two),
+        beyond * jnp.where(same, 1.0, three),
+        beyond * jnp.where(same, two, 1.0),
+    ]
+    weights = [w * scale for w, scale in zip(weights, scales)]
+    main = [jnp.where(same, weights[0], 0.0)] + weights[1:]
+    side = [jnp.where(same, 0.0, weights[0]), 0.0, 0.0]
+    before = [jnp.where(upper, m, s) for m, s in zip(main, side)]
+    after = [jnp.where(upper, s, m) for m, s in zip(main, side)]
+    return states, before, after
+
+
+def weigh(terms):
+    return functools.reduce(jnp.add, [w[:, None] * v.astype(F32) for w, v in terms])
 
 
 def shards(inputs, step_size, decay_rate, skip, b_in, c_in, doc_start, cotangent):
@@ -540,17 +549,34 @@
         name="local",
     )(skip, inputs, cotangent, step_size, step_size, decay, doc, b_in, c_in)
 
+    one, zero = jnp.ones_like(own_e), jnp.zeros_like(own_e)
     if context == 8:
         arrived, grads_loc = lax.optimization_barrier((arrived, grads_loc))
-        before, after = join_chips(arrived, "context", chunks)
+        states, before, after = join_chips(arrived, "context", chunks)
     else:
-        before, after = scan_chips(chip_f, chip_b, chip_l[:, None], "context")
-
-    own_e, sib_e = own_e[:, None], sib_e[:, None]
-    other_f = swap_with(jnp.where(lower, own_e * before + own_f, before), "context", 1)
-    other_b = swap_with(jnp.where(lower, after, own_b + own_e * after), "context", 1)
-    enter_f = jnp.where(lower, before, sib_e * before + sib_f)
-    enter_b = jnp.where(lower, sib_b + sib_e * after, after)
+        states = scan_chips(chip_f, chip_b, chip_l[:, None], "context")
+        before, after = [one, zero], [zero, one]
+    pass_f = jnp.where(lower, own_e, 1.0)
+    pass_b = jnp.where(lower, 1.0, own_e)
+    keep_f = jnp.where(lower, 1.0, sib_e)
+    keep_b = jnp.where(lower, sib_e, 1.0)
+    at_lower = jnp.where(lower, one, zero)
+    at_upper = jnp.where(lower, zero, one)
+    weights = (
+        [pass_f * w for w in before],
+        [pass_b * w for w in after],
+        [keep_f * w for w in before],
+        [keep_b * w for w in after],
+    )
+    passed_f = weigh([*zip(weights[0], states), (at_lower, own_f)])
+    passed_b = weigh([*zip(weights[1], states), (at_upper, own_b)])
+    passed_f, passed_b, weights, states = lax.optimization_barrier(
+        (passed_f, passed_b, weights, states)
+    )
+    other_f = swap_with(passed_f, "context", 1)
+    other_b = swap_with(passed_b, "context", 1)
+    enter_f = weigh([*zip(weights[2], states), (at_upper, sib_f)])
+    enter_b = weigh([*zip(weights[3], states), (at_lower, sib_b)])
 
     parts = tensor if tokens % (8 * tensor) == 0 else 1
     state_spec = pl.BlockSpec((per, half, LANES), lambda i: (i, 0, 0))

time: 69.7 us -> 62.4 us (0.90)
  local copies, waits for them, and re-layouts: 16.8 us -> 2.93 us
  Pallas kernels: 23.5 us -> 32.9 us
  waiting for transfers between devices: 8.04 us -> 5.74 us
    unnamed x58 -> x8, local copies, waits for them, and re-layouts: 15.2 us -> 1.07 us
    pallas_call x2, Pallas kernels: 5.8 us -> 9.55 us  [finish(): pl.pallas_call(functools.partial(output_kernel, group, width), grid=(grou...]
    select_n x1 -> x0, other arithmetic: 3.61 us -> none  [shards(): jnp.where(lower, after, own_b + own_e * after)]
    pallas_call x1, Pallas kernels: 2.86 us -> 5.77 us  [shards(): pl.pallas_call(functools.partial(grads_kernel, parts), grid=(groups,), in...]
    add x0 -> x2, other arithmetic: none -> 2.57 us  [weigh(): functools.reduce(jnp.add, [w[:, None] * v.astype(F32) for w, v in terms])]
    ppermute x13, waiting for transfers between devices: 8.04 us -> 5.74 us  [swap_with(): return lax.ppermute(value, axis, [(i, i ^ mask) for i in range(size)])]
    pallas_call x1, Pallas kernels: 9.44 us -> 10.9 us  [shards(): pl.pallas_call(functools.partial(local_kernel, group, width), grid=(group...]
    pallas_call x1, Pallas kernels: 5.44 us -> 6.7 us  [shards(): pl.pallas_call(functools.partial(states_kernel, group, width), grid=(grou...]
  transfers between devices with their start and end apart: 13 -> 13, of which waited for: 7 -> 5; matrix products, arithmetic and copies ran while one was open for 1% -> 4% of each run, Pallas kernels for 22% -> 33%
where the time goes in v3:
time: 62.4 us; the launch traced here: 61.9 us
  Pallas kernels  32.9 us (53%)
  starting transfers between devices  13.7 us (22%)
  other arithmetic  5.79 us (9%)
  waiting for transfers between devices  5.74 us (9%)
  local copies, waits for them, and re-layouts  2.93 us (5%)
  between operations  0.82 us (1%)
    ppermute x13, starting transfers between devices, swap_with(): return lax.ppermute(value, axis, [(i, i ^ mask) for i in range(size)])  13.7 us
    pallas_call x1, Pallas kernels, shards(): pl.pallas_call(functools.partial(local_kernel, group, width), grid=(group...  10.9 us
    pallas_call x2, Pallas kernels, finish(): pl.pallas_call(functools.partial(output_kernel, group, width), grid=(grou...  9.55 us
    pallas_call x1, Pallas kernels, shards(): pl.pallas_call(functools.partial(states_kernel, group, width), grid=(grou...  6.7 us
    pallas_call x1, Pallas kernels, shards(): pl.pallas_call(functools.partial(grads_kernel, parts), grid=(groups,), in...  5.77 us
    ppermute x13, waiting for transfers between devices, swap_with(): return lax.ppermute(value, axis, [(i, i ^ mask) for i in range(size)])  5.74 us
    add x2, other arithmetic, weigh(): functools.reduce(jnp.add, [w[:, None] * v.astype(F32) for w, v in terms])  2.57 us
    convert_element_type x1, other arithmetic, encode(): return jnp.concatenate([v.astype(jnp.float16) for v in rows], 0)  1.56 us
  transfers between devices with their start and end apart: 13, of which 5 were waited for; matrix products, arithmetic and copies ran while one was open for 4% of the time, Pallas kernels for 33%

profile of v3, /device:TPU:0, one launch (start us, length us, event | category | flops | bytes accessed | tf_op | source)
XLA Modules:
  0.0 61.9 jit_solution(16699953202364094372)
XLA Ops:
  0.6 6.7 %states.1 = (f32[16,128,128]{2,1,0:T(8,128)}, f32[16,128,128]{2,1,0:T(8,128)}, f32[8,16,128]{2,1,0:T(8,128)}) custom-call(s32[1]{0:T(128)} %bitcast.core_ref, bf16[256,2048]{1,0:T(8,128)(2,1)} %x_ref.1, bf16[256,2048]{1,0:T(8,128)(2,1)} %g_ref.1, f32[32,256]{1,0:T(8,128)} %step_blk.1, f32[1,32]{1,0:T(1,128)} %bitcast.77, s32[1,256]{1,0:T(1,128)} %bitcast.75, ...), custom_call_target="tpu_custom_call" | custom-call | tf_op jit(solution)/shard_map/states/pallas_call | solution.py:454
  7.3 0.5 collective-permute-start.1
  7.9 0.1 collective-permute-start
  7.9 2.5 %collective-permute-done = f32[8,16,128]{2,1,0:T(8,128)S(1)} collective-permute-done((f32[8,16,128]{2,1,0:T(8,128)}, f32[8,16,128]{2,1,0:T(8,128)S(1)}, u32[]{:S(2)}, u32[]{:S(2)}) %collective-permute-start) | collective-permute-done | bytes 65568 | tf_op jit(solution)/shard_map/ppermute | solution.py:357
  10.4 0.7 %multiply_exponential_fusion.1 = (f32[16,128]{1,0:T(8,128)S(1)}, f32[16,128]{1,0:T(8,128)S(1)}, f32[16,128]{1,0:T(8,128)S(1)}, f32[16,128]{1,0:T(8,128)S(1)}, f3...) fusion(pred[]{:T(512)S(6)} %eq.19, f32[8,16,128]{2,1,0:T(8,128)S(1)} %collective-permute-done, ...), kind=kLoop, calls=%fused_computation.72 | loop fusion | flops 32768 | bytes 106498 | tf_op jit(solution)/shard_map/exp2 | solution.py:382
  11.2 1.6 %multiply_convert_fusion = (f16[16,64,128]{2,1,0:T(8,128)(2,1)S(1)}, f16[16,64,128]{2,1,0:T(8,128)(2,1)S(1)}) fusion(f32[16,128]{1,0:T(8,128)S(1)} %get-tuple-element.98, pred[]{:T(512)S(6)} %eq.19, f32[16,128,128]{2,1,0:T(8,128)S(1)} %collective-permute-done.1, f32[16,128]{1,0:T(8,128)S(1)} %get-tuple-element.104, f32[16,128,128]{2,1,0:T(8,128)} %get-tuple-element.49, ...), kind=kLoop, calls=%fused_computation.24 | loop fusion | flops 1572864 | bytes 2670594 | tf_op jit(solution)/shard_map/convert_element_type | solution.py:387
  12.8 0.1 constant_dynamic-update-slice_fusion.9
  12.9 0.1 constant_dynamic-update-slice_fusion.4
  12.9 0.7 %constant_dynamic-update-slice_fusion.8 = (f16[1088,128]{1,0:T(8,128)(2,1)S(1)}, f32[16,128]{1,0:T(8,128)S(1)}) fusion(f16[1088,128]{1,0:T(8,128)(2,1)S(1)} %constant_dynamic-update-slice_fusion.9, f32[8,16,128]{2,1,0:T(8,128)S(1)} %collective-permute-done, f32[8,16,128]{2,1,0:T(8,128)} %get-tuple-element.48), kind=kLoop, calls=%fused_computation.45 | loop fusion | flops 8192 | bytes 28672
  13.8 2.9 %collective-permute-start.2 = (f16[1088,128]{1,0:T(8,128)(2,1)S(1)}, f16[1088,128]{1,0:T(8,128)(2,1)S(1)}, u32[]{:S(2)}, u32[]{:S(2)}) collective-permute-start(f16[1088,128]{1,0:T(8,128)(2,1)S(1)} %get-tuple-element.51), channel_id=1, source_target_pairs={{0,8},{4,12},{8,0},{12,4},{16,24},{20,28},{24,16},{28,20},{1,9},{5... | collective-permute-start | bytes 835592 | tf_op jit(solution)/shard_map/ppermute | solution.py:357
  16.7 1.5 %collective-permute-start.3 = (f16[1088,128]{1,0:T(8,128)(2,1)S(1)}, f16[1088,128]{1,0:T(8,128)(2,1)S(1)}, u32[]{:S(2)}, u32[]{:S(2)}) collective-permute-start(f16[1088,128]{1,0:T(8,128)(2,1)S(1)} %get-tuple-element.52), channel_id=1, source_target_pairs={{0,16},{4,20},{8,24},{12,28},{16,0},{20,4},{24,8},{28,12},{1,17},{... | collective-permute-start | bytes 835592 | tf_op jit(solution)/shard_map/ppermute | solution.py:357
  18.2 10.9 %local.1 = (f32[256,2048]{1,0:T(8,128)}, f32[256,2048]{1,0:T(8,128)}, bf16[256,2048]{1,0:T(8,128)(2,1)}, bf16[256,2048]{1,0:T(8,128)(2,1)}, bf16[256,2048]{1,0:T...) custom-call(f32[32]{0:T(128)} %skip_ref, ...), custom_call_target="tpu_custom_call" | custom-call | flops 2684354560 | bytes 10485760 | tf_op jit(solution)/shard_map/local/pallas_call | solution.py:510
  29.2 1.9 %collective-permute-done.3 = f16[1088,128]{1,0:T(8,128)(2,1)S(1)} collective-permute-done((f16[1088,128]{1,0:T(8,128)(2,1)S(1)}, f16[1088,128]{1,0:T(8,128)(2,1)S(1)}, u32[]{:S(2)}, u32[]{:S(2)}) %collective-permute-start.3) | collective-permute-done | bytes 278560 | tf_op jit(solution)/shard_map/ppermute | solution.py:357
  31.2 0.1 slice.113
  31.3 1.2 %fusion.5 = (f32[16,64,128]{2,1,0:T(8,128)S(1)}, f32[16,64,128]{2,1,0:T(8,128)}) fusion(f16[16,64,128]{2,1,0:T(8,128)(2,1)S(1)} %bitcast.65, f16[16,64,128]{2,1,0:T(8,128)(2,1)S(1)} %bitcast.67, f16[16,64,128]{2,1,0:T(8,128)(2,1)S(1)} %bitcast.69, f32[16,128,128]{2,1,0:T(8,128)S(1)} %copy-done, f32[]{:T(128)S(6)} %select_n.225, ...), kind=kLoop, calls=%fused_computation.17 | loop fusion | flops 2228224 | bytes 2932744 | tf_op jit(solution)/shard_map/add | solution.py:431
  32.5 0.5 collective-permute-start.6
  33.0 1.4 %fusion.11 = (f32[16,64,128]{2,1,0:T(8,128)}, f32[16,64,128]{2,1,0:T(8,128)}) fusion(f16[16,64,128]{2,1,0:T(8,128)(2,1)S(1)} %bitcast.66, f16[16,64,128]{2,1,0:T(8,128)(2,1)S(1)} %bitcast.68, f16[16,64,128]{2,1,0:T(8,128)(2,1)S(1)} %bitcast.70, f32[16,128,128]{2,1,0:T(8,128)S(1)} %collective-permute-done.1, f32[16,128]{1,0:T(8,128)S(1)} %get-tuple-element.67, ...), kind=kLoop, calls=%fused_computation.23 | loop fusion | flops 2228224 | bytes 2932744 | tf_op jit(solution)/shard_map/add | solution.py:431
  34.4 0.9 %collective-permute-done.5.other_f.other = f32[16,64,128]{2,1,0:T(8,128)S(1)} collective-permute-done((f32[16,64,128]{2,1,0:T(8,128)}, f32[16,64,128]{2,1,0:T(8,128)S(1)}, u32[]{:S(2)}, u32[]{:S(2)}) %collective-permute-start.5) | collective-permute-done | bytes 524320 | tf_op jit(solution)/shard_map/ppermute | solution.py:357
  35.4 0.8 %copy-done.2 = f32[16,64,128]{2,1,0:T(8,128)} copy-done((f32[16,64,128]{2,1,0:T(8,128)}, f32[16,64,128]{2,1,0:T(8,128)S(1)}, u32[]{:S(2)}) %copy-start.2) | copy-done | bytes 524312
  36.1 0.2 copy-done.1
  36.3 5.8 %grads.1 = f32[4,2,64,128]{3,2,1,0:T(8,128)} custom-call(s32[1]{0:T(128)} %bitcast.core_ref, f32[16,64,128]{2,1,0:T(8,128)} %get-tuple-element.108.own_f.own, f32[16,64,128]{2,1,0:T(8,128)} %copy-done.2, f32[16,64,128]{2,1,0:T(8,128)} %get-tuple-element.107.own_b.own, f32[16,64,128]{2,1,0:T(8,128)} %copy-done.1, bf16[256,2048]{1,0:T(8,128)(2,1)} %get-tuple-element.69.xh_ref, ...), custom_call_target="tpu_custom_call" | custom-call | tf_op jit(solution)/shard_map/grads/pallas_call | solution.py:584
  42.1 1.0 %dynamic-slice_bitcast_fusion = (f32[2,64,128]{2,1,0:T(8,128)S(1)}, f32[2,64,128]{2,1,0:T(8,128)S(1)}, f32[2,64,128]{2,1,0:T(8,128)S(1)}, f32[2,64,128]{2,1,0:T(8,128)S(1)}) fusion(f32[4,2,64,128]{3,2,1,0:T(8,128)} %grads.1, s32[]{:T(128)S(6)} %select_n.229, s32[]{:T(128)S(6)} %select_n.228, s32[]{:T(128)S(6)} %select_n.227, s32[]{:T(128)S(6)} %select_n.226), kind=kLoop, calls=%fused_computation.29 | loop fusion | bytes 524304 | tf_op jit(solution)/shard_map/jit(dynamic_index_in_dim)/squeeze | solution.py:621
  43.0 2.7 %collective-permute-start.7 = (f32[2,64,128]{2,1,0:T(8,128)S(1)}, f32[2,64,128]{2,1,0:T(8,128)S(1)}, u32[]{:S(2)}, u32[]{:S(2)}) collective-permute-start(f32[2,64,128]{2,1,0:T(8,128)S(1)} %get-tuple-element.74), channel_id=1, source_target_pairs={{0,2},{1,3},{2,0},{3,1},{4,6},{5,7},{6,4},{7,5},{8,10},{9,11},{10,... | collective-permute-start | bytes 196616 | tf_op jit(solution)/shard_map/ppermute | solution.py:357
  45.7 1.4 %collective-permute-start.8 = (f32[2,64,128]{2,1,0:T(8,128)S(1)}, f32[2,64,128]{2,1,0:T(8,128)S(1)}, u32[]{:S(2)}, u32[]{:S(2)}) collective-permute-start(f32[2,64,128]{2,1,0:T(8,128)S(1)} %get-tuple-element.75), channel_id=1, source_target_pairs={{0,3},{1,2},{2,1},{3,0},{4,7},{5,6},{6,5},{7,4},{8,11},{9,10},{10,... | collective-permute-start | bytes 196616 | tf_op jit(solution)/shard_map/ppermute | solution.py:357
  47.0 0.2 collective-permute-start.9
  47.3 4.8 %mixed.1 = bf16[256,2048]{1,0:T(8,128)(2,1)} custom-call(s32[1]{0:T(128)} %bitcast.core_ref, f32[16,64,128]{2,1,0:T(8,128)} %get-tuple-element.108.own_f.own, f32[16,64,128]{2,1,0:T(8,128)} %copy-done.2, f32[256,2048]{1,0:T(8,128)} %get-tuple-element.78.base_ref, bf16[2,4,2,256,8]{4,3,2,1,0:T(8,128)(2,1)} %get-tuple-element.79.coded_ref, ...), custom_call_target="tpu_custom_call" | custom-call | flops 268435456 | bytes 4194304 | tf_op jit(solution)/shard_map/mixed/pallas_call | solution.py:596
  52.0 0.1 collective-permute-done.8
  52.1 0.3 collective-permute-done.9
  52.4 2.6 %collective-permute-start.10 = (bf16[2,64,128]{2,1,0:T(8,128)(2,1)S(1)}, bf16[2,64,128]{2,1,0:T(8,128)(2,1)S(1)}, u32[]{:S(2)}, u32[]{:S(2)}) collective-permute-start(bf16[2,64,128]{2,1,0:T(8,128)(2,1)S(1)} %add_convert_fusion), channel_id=1, source_target_pairs={{0,2},{1,3},{2,0},{3,1},{4,6},{5,7},{6,4},{7,5},{8,10},{9,11},{10,... | collective-permute-start | bytes 98312 | tf_op jit(solution)/shard_map/ppermute | solution.py:357
  55.1 1.2 %collective-permute-start.11 = (bf16[2,64,128]{2,1,0:T(8,128)(2,1)S(1)}, bf16[2,64,128]{2,1,0:T(8,128)(2,1)S(1)}, u32[]{:S(2)}, u32[]{:S(2)}) collective-permute-start(bf16[2,64,128]{2,1,0:T(8,128)(2,1)S(1)} %add_convert_fusion), channel_id=1, source_target_pairs={{0,3},{1,2},{2,1},{3,0},{4,7},{5,6},{6,5},{7,4},{8,11},{9,10},{10,... | collective-permute-start | bytes 98312 | tf_op jit(solution)/shard_map/ppermute | solution.py:357
  56.3 4.8 %grad_inputs.1 = bf16[256,2048]{1,0:T(8,128)(2,1)} custom-call(s32[1]{0:T(128)} %bitcast.core_ref, f32[16,64,128]{2,1,0:T(8,128)} %get-tuple-element.107.own_b.own, f32[16,64,128]{2,1,0:T(8,128)} %copy-done.1, f32[256,2048]{1,0:T(8,128)} %get-tuple-element.87.base_ref, bf16[2,4,2,256,8]{4,3,2,1,0:T(8,128)(2,1)} %get-tuple-element.79.coded_ref, ...), custom_call_target="tpu_custom_call" | custom-call | flops 268435456 | bytes 4194304 | tf_op jit(solution)/shard_map/grad_inputs/pallas_call | solution.py:596
  61.2 0.7 %fusion.31 = (bf16[4,1,64,128]{3,2,0,1:T(8,128)(2,1)}, bf16[4,1,64,128]{3,2,0,1:T(8,128)(2,1)}) fusion(bf16[4,2,64,128]{3,2,0,1:T(8,128)(2,1)S(1)} %bitcast_dynamic-update-slice_fusion), kind=kLoop, calls=%fused_computation.92 | loop fusion | bytes 262144 | tf_op jit(solution)/shard_map/slice | solution.py:641
  (30 shorter events, 0.4 us)
Async XLA Ops:
  7.3 3.9 %collective-permute-start.1 = (f32[16,128,128]{2,1,0:T(8,128)}, f32[16,128,128]{2,1,0:T(8,128)S(1)}, u32[]{:S(2)}, u32[]{:S(2)}) collective-permute-start(f32[16,128,128]{2,1,0:T(8,128)} %get-tuple-element.50), channel_id=1, source_target_pairs={{0,4},{4,0},{8,12},{12,8},{16,20},{20,16},{24,28},{28,24},{1,5},{5... | collective-permute-start | bytes 3145736 | tf_op jit(solution)/shard_map/ppermute | solution.py:357
  7.9 2.6 %collective-permute-start = (f32[8,16,128]{2,1,0:T(8,128)}, f32[8,16,128]{2,1,0:T(8,128)S(1)}, u32[]{:S(2)}, u32[]{:S(2)}) collective-permute-start(f32[8,16,128]{2,1,0:T(8,128)} %get-tuple-element.48), channel_id=1, source_target_pairs={{0,4},{4,0},{8,12},{12,8},{16,20},{20,16},{24,28},{28,24},{1,5},{5... | collective-permute-start | bytes 196616 | tf_op jit(solution)/shard_map/ppermute | solution.py:357
  13.8 15.4 %collective-permute-start.2 = (f16[1088,128]{1,0:T(8,128)(2,1)S(1)}, f16[1088,128]{1,0:T(8,128)(2,1)S(1)}, u32[]{:S(2)}, u32[]{:S(2)}) collective-permute-start(f16[1088,128]{1,0:T(8,128)(2,1)S(1)} %get-tuple-element.51), channel_id=1, source_target_pairs={{0,8},{4,12},{8,0},{12,4},{16,24},{20,28},{24,16},{28,20},{1,9},{5... | collective-permute-start | bytes 835592 | tf_op jit(solution)/shard_map/ppermute | solution.py:357
  16.7 14.4 %collective-permute-start.3 = (f16[1088,128]{1,0:T(8,128)(2,1)S(1)}, f16[1088,128]{1,0:T(8,128)(2,1)S(1)}, u32[]{:S(2)}, u32[]{:S(2)}) collective-permute-start(f16[1088,128]{1,0:T(8,128)(2,1)S(1)} %get-tuple-element.52), channel_id=1, source_target_pairs={{0,16},{4,20},{8,24},{12,28},{16,0},{20,4},{24,8},{28,12},{1,17},{... | collective-permute-start | bytes 835592 | tf_op jit(solution)/shard_map/ppermute | solution.py:357
  18.2 12.9 %collective-permute-start.4 = (f16[1088,128]{1,0:T(8,128)(2,1)S(1)}, f16[1088,128]{1,0:T(8,128)(2,1)S(1)}, u32[]{:S(2)}, u32[]{:S(2)}) collective-permute-start(f16[1088,128]{1,0:T(8,128)(2,1)S(1)} %get-tuple-element.52), channel_id=1, source_target_pairs={{0,24},{4,28},{8,16},{12,20},{16,8},{20,12},{24,0},{28,4},{1,25},{... | collective-permute-start | bytes 835592 | tf_op jit(solution)/shard_map/ppermute | solution.py:357
  29.2 2.2 %copy-start = (f32[16,128,128]{2,1,0:T(8,128)S(1)}, f32[16,128,128]{2,1,0:T(8,128)}, u32[]{:S(2)}) copy-start(f32[16,128,128]{2,1,0:T(8,128)} %get-tuple-element.49) | copy-start | bytes 3145732
  32.5 2.8 %collective-permute-start.5 = (f32[16,64,128]{2,1,0:T(8,128)}, f32[16,64,128]{2,1,0:T(8,128)S(1)}, u32[]{:S(2)}, u32[]{:S(2)}) collective-permute-start(f32[16,64,128]{2,1,0:T(8,128)} %get-tuple-element.64), channel_id=1, source_target_pairs={{0,4},{4,0},{8,12},{12,8},{16,20},{20,16},{24,28},{28,24},{1,5},{5... | collective-permute-start | bytes 1572872 | tf_op jit(solution)/shard_map/ppermute | solution.py:357
  32.5 2.8 %collective-permute-start.6 = (f32[16,64,128]{2,1,0:T(8,128)S(1)}, f32[16,64,128]{2,1,0:T(8,128)S(1)}, u32[]{:S(2)}, u32[]{:S(2)}) collective-permute-start(f32[16,64,128]{2,1,0:T(8,128)S(1)} %get-tuple-element.68), channel_id=1, source_target_pairs={{0,4},{4,0},{8,12},{12,8},{16,20},{20,16},{24,28},{28,24},{1,5},{5... | collective-permute-start | bytes 1572872 | tf_op jit(solution)/shard_map/ppermute | solution.py:357
  35.3 0.8 %copy-start.2 = (f32[16,64,128]{2,1,0:T(8,128)}, f32[16,64,128]{2,1,0:T(8,128)S(1)}, u32[]{:S(2)}) copy-start(f32[16,64,128]{2,1,0:T(8,128)S(1)} %collective-permute-done.5.other_f.other) | copy-start | bytes 1572868
  35.3 1.0 %copy-start.1 = (f32[16,64,128]{2,1,0:T(8,128)}, f32[16,64,128]{2,1,0:T(8,128)S(1)}, u32[]{:S(2)}) copy-start(f32[16,64,128]{2,1,0:T(8,128)S(1)} %collective-permute-done.6.other_b.other) | copy-start | bytes 1572868
  43.0 9.0 %collective-permute-start.7 = (f32[2,64,128]{2,1,0:T(8,128)S(1)}, f32[2,64,128]{2,1,0:T(8,128)S(1)}, u32[]{:S(2)}, u32[]{:S(2)}) collective-permute-start(f32[2,64,128]{2,1,0:T(8,128)S(1)} %get-tuple-element.74), channel_id=1, source_target_pairs={{0,2},{1,3},{2,0},{3,1},{4,6},{5,7},{6,4},{7,5},{8,10},{9,11},{10,... | collective-permute-start | bytes 196616 | tf_op jit(solution)/shard_map/ppermute | solution.py:357
  45.7 6.4 %collective-permute-start.8 = (f32[2,64,128]{2,1,0:T(8,128)S(1)}, f32[2,64,128]{2,1,0:T(8,128)S(1)}, u32[]{:S(2)}, u32[]{:S(2)}) collective-permute-start(f32[2,64,128]{2,1,0:T(8,128)S(1)} %get-tuple-element.75), channel_id=1, source_target_pairs={{0,3},{1,2},{2,1},{3,0},{4,7},{5,6},{6,5},{7,4},{8,11},{9,10},{10,... | collective-permute-start | bytes 196616 | tf_op jit(solution)/shard_map/ppermute | solution.py:357
  47.0 5.4 %collective-permute-start.9 = (f32[2,64,128]{2,1,0:T(8,128)S(1)}, f32[2,64,128]{2,1,0:T(8,128)S(1)}, u32[]{:S(2)}, u32[]{:S(2)}) collective-permute-start(f32[2,64,128]{2,1,0:T(8,128)S(1)} %get-tuple-element.76), channel_id=1, source_target_pairs={{0,1},{1,0},{2,3},{3,2},{4,5},{5,4},{6,7},{7,6},{8,9},{9,8},{10,11... | collective-permute-start | bytes 196616 | tf_op jit(solution)/shard_map/ppermute | solution.py:357
  52.4 8.7 %collective-permute-start.10 = (bf16[2,64,128]{2,1,0:T(8,128)(2,1)S(1)}, bf16[2,64,128]{2,1,0:T(8,128)(2,1)S(1)}, u32[]{:S(2)}, u32[]{:S(2)}) collective-permute-start(bf16[2,64,128]{2,1,0:T(8,128)(2,1)S(1)} %add_convert_fusion), channel_id=1, source_target_pairs={{0,2},{1,3},{2,0},{3,1},{4,6},{5,7},{6,4},{7,5},{8,10},{9,11},{10,... | collective-permute-start | bytes 98312 | tf_op jit(solution)/shard_map/ppermute | solution.py:357
  55.1 6.1 %collective-permute-start.11 = (bf16[2,64,128]{2,1,0:T(8,128)(2,1)S(1)}, bf16[2,64,128]{2,1,0:T(8,128)(2,1)S(1)}, u32[]{:S(2)}, u32[]{:S(2)}) collective-permute-start(bf16[2,64,128]{2,1,0:T(8,128)(2,1)S(1)} %add_convert_fusion), channel_id=1, source_target_pairs={{0,3},{1,2},{2,1},{3,0},{4,7},{5,6},{6,5},{7,4},{8,11},{9,10},{10,... | collective-permute-start | bytes 98312 | tf_op jit(solution)/shard_map/ppermute | solution.py:357
  56.3 4.8 %collective-permute-start.12 = (bf16[2,64,128]{2,1,0:T(8,128)(2,1)S(1)}, bf16[2,64,128]{2,1,0:T(8,128)(2,1)S(1)}, u32[]{:S(2)}, u32[]{:S(2)}) collective-permute-start(bf16[2,64,128]{2,1,0:T(8,128)(2,1)S(1)} %add_convert_fusion), channel_id=1, source_target_pairs={{0,1},{1,0},{2,3},{3,2},{4,5},{5,4},{6,7},{7,6},{8,9},{9,8},{10,11... | collective-permute-start | bytes 98312 | tf_op jit(solution)/shard_map/ppermute | solution.py:357

commit v4 on v3

--- a/solution.py
+++ b/solution.py
@@ -15,6 +15,7 @@
 MASKED = -1e30
 BOUND = 6.0 * 1.796875
 META = 8
+STATES_VMEM, LOCAL_VMEM, GRADS_VMEM, OUTPUT_VMEM = 62, 60, 48, 60
 
 NN = (((1,), (0,)), ((), ()))
 NT = (((1,), (1,)), ((), ()))
@@ -87,9 +88,28 @@
     return jnp.concatenate(keep, 0), jnp.concatenate(last, 0), total
 
 
-def expander(heads, width):
-    shape = (heads, heads * width)
-    return jnp.where(iota(shape, 0) == iota(shape, 1) // width, 1.0, 0.0).astype(BF16)
+def spread_rows(rows, first, width, columns, skipped):
+    heads = rows // 4
+    row = iota((rows, 1), 0) - skipped * heads
+    head = jnp.where(row >= heads, row - heads, row)
+    head = jnp.where((row >= 0) & (row < 2 * heads), head, -rows * rows)
+    offset = iota((1, columns), 1) - (head - first) * width
+    return jnp.where((offset >= 0) & (offset < width), 1.0, 0.0).astype(BF16)
+
+
+def last_spread(rows, first, width, columns):
+    return spread_rows(rows, first, width, columns, 0)
+
+
+def keep_spread(rows, first, width, columns):
+    return spread_rows(rows, first, width, columns, 2)
+
+
+SPREADS = (last_spread, keep_spread)
+
+
+def pieces(total, most=256):
+    return [slice(k, min(k + most, total)) for k in range(0, total, most)]
 
 
 def fetch(pairs, sems):
@@ -107,11 +127,11 @@
 
 def states_kernel(
     group, width, core_ref, x_hbm, g_hbm, step_hbm, decay_hbm, doc_hbm, b_hbm, c_hbm,
-    mine_ref, send_ref, meta_ref, x_ref, g_ref, step_ref, decay_ref, doc_ref, b_ref, c_ref,
-    b_t, c_t, weights, meta, small_sems, big_sems,
+    mine_ref, send_ref, meta_ref, edges_ref, x_ref, g_ref, step_ref, decay_ref, doc_ref, b_ref,
+    c_ref, b_t, c_t, meta, small_sems, big_sems,
 ):
     step_id = pl.program_id(0)
-    groups = weights.shape[1]
+    groups = x_ref.shape[0]
     half = b_t.shape[0] // 2
     wide = group * width
     chunks = wide // LANES
@@ -149,11 +169,9 @@
         bound_b = BOUND * jnp.sum(keep, axis=0, keepdims=True)
         rows = [total, jnp.exp(total), bound_f, bound_b]
         rows = jnp.concatenate(rows + [jnp.zeros((META - 4, total.shape[1]), F32)], 0)
-        for k in range(groups):
-            heads = slice(k * group, (k + 1) * group)
-            weights[0, k] = last[:, heads]
-            weights[1, k] = keep[:, heads]
-            meta[k] = rows[:, heads]
+        high, mid, low = split3(rows)
+        meta[...] = jnp.concatenate([high, mid, low, jnp.zeros_like(high)], 1)
+        edges_ref[...] = jnp.concatenate(split2(last) + split2(keep), 1)
         for ref, out in ((b_ref, b_t), (c_ref, c_t)):
             turned = ref[...].astype(F32).T
             swapped = jnp.concatenate([turned[half:], turned[:half]], 0)
@@ -161,41 +179,39 @@
 
     for copy in big(step_id):
         copy.wait()
-    spread = expander(group, width)
-    rows = functools.reduce(jnp.add, [dot(p, spread, NN) for p in split3(meta[step_id])])
+    edges = edges_ref[...]
+    spreads = [make(edges.shape[1], step_id * group, width, wide) for make in SPREADS]
+    rows = dot(meta[...], spreads[0] + spreads[1], NN)
     for k in range(chunks):
         for n in range(META):
             meta_ref[n, pl.ds(step_id * chunks + k, 1)] = rows[n : n + 1, k * LANES : (k + 1) * LANES]
     for kind, (ref, turned) in enumerate(((x_ref, b_t), (g_ref, c_t))):
-        hi, lo = split2(weights[kind, step_id])
         turned = turned[...]
-        for k in range(chunks):
-            lanes = slice(k * LANES, (k + 1) * LANES)
-            scale = dot(hi, spread[:, lanes], NN) + dot(lo, spread[:, lanes], NN)
+        for lanes in pieces(wide):
+            scale = dot(edges, spreads[kind][:, lanes], NN)
             scaled = split2(ref[step_id, :, lanes].astype(F32) * scale)
             state = dot(turned, scaled[0], NN) + dot(turned, scaled[1], NN)
-            mine_ref[k, kind * half : (kind + 1) * half] = state[:half]
-            send_ref[k, kind * half : (kind + 1) * half] = state[half:]
+            for k in range(state.shape[1] // LANES):
+                part = state[:, k * LANES : (k + 1) * LANES]
+                at = lanes.start // LANES + k
+                mine_ref[at, kind * half : (kind + 1) * half] = part[:half]
+                send_ref[at, kind * half : (kind + 1) * half] = part[half:]
 
 
 def local_kernel(
     group, width, skip_ref, x_ref, g_ref, step_ref, step_blk, decay_ref, doc_ref, b_ref, c_ref,
-    mixed_ref, gx_ref, xh_ref, xl_ref, gh_ref, gl_ref, coded_ref, grads_ref,
-    weights, down_s, across_s, bias, inter, common,
+    mixed_ref, gx_ref, grads_ref, down_s, across_s, bias, inter, common,
 ):
     step_id = pl.program_id(0)
-    groups = weights.shape[1]
+    groups = down_s.shape[1]
     pairs = ((0, 0), (1, 0), (1, 1))
 
     @pl.when(step_id == 0)
     def _():
         step = step_ref[...]
         sums = block_sums(step, column(decay_ref[...]), doc_ref[...])
-        keep, last, _ = edge_weights(step, sums)
         for k in range(groups):
             heads = slice(k * group, (k + 1) * group)
-            weights[0, k] = last[:, heads]
-            weights[1, k] = keep[:, heads]
             for j in range(2):
                 down_s[j, k] = sums[j][0][:, heads]
                 across_s[j, k] = sums[j][1][heads]
@@ -210,18 +226,6 @@
                 c_ref[t * BLOCK : (t + 1) * BLOCK], b_ref[s * BLOCK : (s + 1) * BLOCK], NT
             )
         common[...] = jnp.zeros_like(common)
-
-    spread = expander(group, width)
-    for ref, high, low, kind in ((x_ref, xh_ref, xl_ref, 0), (g_ref, gh_ref, gl_ref, 1)):
-        hi, lo = split2(weights[kind, step_id])
-        coded_ref[kind, 0, 0] = hi
-        coded_ref[kind, 0, 1] = lo
-        for k in range(group * width // LANES):
-            lanes = slice(k * LANES, (k + 1) * LANES)
-            scale = dot(hi, spread[:, lanes], NN) + dot(lo, spread[:, lanes], NN)
-            scaled = split2(ref[:, lanes].astype(F32) * scale)
-            high[:, lanes] = scaled[0]
-            low[:, lanes] = scaled[1]
 
     down = [down_s[j, step_id] for j in range(2)]
     across = [across_s[j, step_id] for j in range(2)]
@@ -303,42 +307,45 @@
 
 
 def grads_kernel(
-    parts, core_ref, own_f, other_f, own_b, other_b, xh_ref, xl_ref, gh_ref, gl_ref, local_ref,
-    out_ref, high, low, total,
+    group, width, masks, core_ref, place_ref, own_f, other_f, own_b, other_b, x_ref, g_ref, edges_ref,
+    local_ref, *rest,
 ):
+    outs, (both, total) = rest[:-2], rest[-2:]
     step_id = pl.program_id(0)
+    state = local_ref.shape[2]
 
     @pl.when(step_id == 0)
     def _():
         total[...] = local_ref[...]
 
-    for slot, own, other, vh, vl in (
-        (0, own_b, other_b, xh_ref, xl_ref),
-        (1, own_f, other_f, gh_ref, gl_ref),
-    ):
-        place_state(core_ref[0], own, other, high.at[slot], low.at[slot])
-        hi, lo = high[slot], low[slot]
-        first = vh[...]
-        total[slot] += dot(first, hi, NT) + dot(first, lo, NT) + dot(vl[...], hi, NT)
+    edges = edges_ref[...]
+    for slot, own, other, ref in ((0, own_b, other_b, x_ref), (1, own_f, other_f, g_ref)):
+        place_state(core_ref[0], own, other, both.at[slot], both.at[slot, state:])
+        spread = SPREADS[slot](edges.shape[1], step_id * group, width, group * width)
+        high, low = split2(ref[...].astype(F32) * dot(edges, spread, NN))
+        product = dot(high, both[slot], NT)
+        product = product[:, :state] + product[:, state:]
+        total[slot] += product + dot(low, both[slot, :state], NT)
 
     @pl.when(step_id == pl.num_programs(0) - 1)
     def _():
-        rows = total.shape[1] // parts
-        for k in range(parts):
+        rows = total.shape[1] // len(masks)
+        for mask, out in zip(masks, outs):
+            first = (place_ref[0] ^ mask) * rows
             for slot in range(2):
-                out_ref[k, slot] = total[slot, k * rows : (k + 1) * rows]
+                out[slot] = total[slot, pl.ds(pl.multiple_of(first, rows), rows)]
 
 
 def output_kernel(
-    group, width, core_ref, own, other, base_ref, coded_ref, proj_ref, out_ref, high, low
+    group, width, kind, core_ref, own, other, base_ref, edges_ref, proj_ref, out_ref, high, low
 ):
     place_state(core_ref[0], own, other, high, low)
-    spread = expander(group, width)
-    hi, lo = coded_ref[0, 0, 0], coded_ref[0, 0, 1]
+    edges = edges_ref[...]
+    wide = group * width
+    spread = SPREADS[kind](edges.shape[1], pl.program_id(0) * group, width, wide)
     proj = proj_ref[...]
-    for k in range(group * width // LANES):
-        lanes = slice(k * LANES, (k + 1) * LANES)
-        scale = dot(hi, spread[:, lanes], NN) + dot(lo, spread[:, lanes], NN)
+    for lanes in pieces(wide):
+        scale = dot(edges, spread[:, lanes], NN)
         carried = dot(proj, high[:, lanes], NN) + dot(proj, low[:, lanes], NN)
         out_ref[:, lanes] = (base_ref[:, lanes] + scale * carried).astype(BF16)
 
@@ -349,7 +356,10 @@
 
 SMEM = pl.BlockSpec(memory_space=pltpu.SMEM)
 HBM = pl.BlockSpec(memory_space=pltpu.HBM)
-PARAMS = pltpu.CompilerParams(vmem_limit_bytes=60 << 20)
+
+
+def grant(mib):
+    return pltpu.CompilerParams(vmem_limit_bytes=mib << 20)
 
 
 def swap_with(value, axis, mask):
@@ -450,14 +460,16 @@
 
     tok = pl.BlockSpec((tokens, wide), lambda i: (0, i))
     piece = pl.BlockSpec((per, state, LANES), lambda i: (i, 0, 0))
-    weights = pltpu.VMEM((2, groups, tokens, group), F32)
-    mine, send, meta = pl.pallas_call(
+    mine, send, raw_meta, edges = pl.pallas_call(
         functools.partial(states_kernel, group, width),
         grid=(groups,),
         in_specs=[SMEM] + [HBM] * 7,
-        out_specs=[piece, piece, whole((META, chunks, LANES))],
+        out_specs=[piece, piece, whole((META, chunks, LANES)), whole((tokens, 4 * heads))],
         out_shape=[jax.ShapeDtypeStruct((chunks, state, LANES), F32)] * 2
-        + [jax.ShapeDtypeStruct((META, chunks, LANES), F32)],
+        + [
+            jax.ShapeDtypeStruct((META, chunks, LANES), F32),
+            jax.ShapeDtypeStruct((tokens, 4 * heads), BF16),
+        ],
         scratch_shapes=[
             pltpu.VMEM((groups, tokens, wide), BF16),
             pltpu.VMEM((groups, tokens, wide), BF16),
@@ -468,17 +480,17 @@
             pltpu.VMEM((tokens, state), BF16),
             pltpu.VMEM((state, tokens), BF16),
             pltpu.VMEM((state, tokens), BF16),
-            weights,
-            pltpu.VMEM((groups, META, group), F32),
+            pltpu.VMEM((META, 4 * heads), BF16),
             pltpu.SemaphoreType.DMA((5,)),
             pltpu.SemaphoreType.DMA((2, groups)),
         ],
-        compiler_params=PARAMS,
+        compiler_params=grant(STATES_VMEM),
         name="states",
     )(flag, inputs, cotangent, step_size, decay, doc, b_in, c_in)
 
+    meta = lax.optimization_barrier(jnp.maximum(raw_meta, NEVER))
     theirs = swap_with(send, "context", 1)
-    sib_meta = swap_with(meta, "context", 1)
+    sib_meta = swap_with(raw_meta, "context", 1)
     lower = core == 0
     own_f, own_b = mine[:, :half], mine[:, half:]
     sib_f, sib_b = theirs[:, :half], theirs[:, half:]
@@ -506,8 +518,7 @@
         ]
 
     full = jax.ShapeDtypeStruct((tokens, channels), F32)
-    coded = jax.ShapeDtypeStruct((tokens, channels), BF16)
-    mixed_loc, gx_loc, xh, xl, gh, gl, scales, grads_loc = pl.pallas_call(
+    mixed_loc, gx_loc, grads_loc = pl.pallas_call(
         functools.partial(local_kernel, group, width),
         grid=(groups,),
         in_specs=[
@@ -521,30 +532,20 @@
             whole((tokens, state)),
             whole((tokens, state)),
         ],
-        out_specs=[tok] * 6
-        + [
-            pl.BlockSpec((2, 1, 2, tokens, group), lambda i: (0, i, 0, 0, 0)),
-            whole((2, tokens, state)),
-        ],
-        out_shape=[full, full]
-        + [coded] * 4
-        + [
-            jax.ShapeDtypeStruct((2, groups, 2, tokens, group), BF16),
-            jax.ShapeDtypeStruct((2, tokens, state), F32),
-        ],
+        out_specs=[tok, tok, whole((2, tokens, state))],
+        out_shape=[full, full, jax.ShapeDtypeStruct((2, tokens, state), F32)],
         scratch_shapes=[
-            weights,
             pltpu.VMEM((2, groups, BLOCK, group), F32),
             pltpu.VMEM((2, groups, group, BLOCK), F32),
             pltpu.VMEM((3, BLOCK, BLOCK), F32),
             pltpu.VMEM((3, BLOCK, BLOCK), F32),
             pltpu.VMEM((3, BLOCK, BLOCK), F32),
         ],
-        compiler_params=PARAMS,
+        compiler_params=grant(LOCAL_VMEM),
         cost_estimate=pl.CostEstimate(
             flops=20 * tokens * tokens * channels,
             transcendentals=heads * tokens * tokens,
-            bytes_accessed=20 * tokens * channels,
+            bytes_accessed=12 * tokens * channels,
         ),
         name="local",
     )(skip, inputs, cotangent, step_size, step_size, decay, doc, b_in, c_in)
@@ -578,68 +579,80 @@
     enter_f = weigh([*zip(weights[2], states), (at_upper, sib_f)])
     enter_b = weigh([*zip(weights[3], states), (at_lower, sib_b)])
 
-    parts = tensor if tokens % (8 * tensor) == 0 else 1
+    masks = (0, 2, 3, 1) if tensor == 4 else (0,)
+    rows = tokens // len(masks)
+    place = lax.axis_index("tensor")
     state_spec = pl.BlockSpec((per, half, LANES), lambda i: (i, 0, 0))
-    slots = [pltpu.VMEM((2, state, wide), BF16)] * 2
-    grads = pl.pallas_call(
-        functools.partial(grads_kernel, parts),
+    parts = pl.pallas_call(
+        functools.partial(grads_kernel, group, width, masks),
         grid=(groups,),
-        in_specs=[SMEM] + [state_spec] * 4 + [tok] * 4 + [whole((2, tokens, state))],
-        out_specs=whole((parts, 2, tokens // parts, state)),
-        out_shape=jax.ShapeDtypeStruct((parts, 2, tokens // parts, state), F32),
-        scratch_shapes=slots + [pltpu.VMEM((2, tokens, state), F32)],
-        compiler_params=PARAMS,
+        in_specs=[SMEM, SMEM]
+        + [state_spec] * 4
+        + [tok, tok, whole((tokens, 4 * heads)), whole((2, tokens, state))],
+        out_specs=[whole((2, rows, state))] * len(masks),
+        out_shape=[jax.ShapeDtypeStruct((2, rows, state), F32)] * len(masks),
+        scratch_shapes=[
+            pltpu.VMEM((2, 2 * state, wide), BF16),
+            pltpu.VMEM((2, tokens, state), F32),
+        ],
+        compiler_params=grant(GRADS_VMEM),
         name="grads",
-    )(flag, enter_f, other_f, enter_b, other_b, xh, xl, gh, gl, grads_loc)
+    )(
+        flag,
+        place.reshape(1) if tensor == 4 else jnp.zeros((1,), jnp.int32),
+        enter_f,
+        other_f,
+        enter_b,
+        other_b,
+        inputs,
+        cotangent,
+        edges,
+        grads_loc,
+    )
 
     def finish(kind, first, own, other, base, proj, name):
         return pl.pallas_call(
-            functools.partial(output_kernel, group, width),
+            functools.partial(output_kernel, group, width, kind),
             grid=(groups,),
             in_specs=[
                 SMEM,
                 state_spec,
                 state_spec,
                 tok,
-                pl.BlockSpec((1, 1, 2, tokens, group), lambda i: (kind, i, 0, 0, 0)),
+                whole((tokens, 4 * heads)),
                 whole((tokens, state)),
             ],
             out_specs=tok,
-            out_shape=coded,
+            out_shape=jax.ShapeDtypeStruct((tokens, channels), BF16),
             scratch_shapes=[pltpu.VMEM((state, wide), BF16)] * 2,
-            compiler_params=PARAMS,
+            compiler_params=grant(OUTPUT_VMEM),
             cost_estimate=pl.CostEstimate(
                 flops=4 * tokens * state * channels,
                 transcendentals=0,
                 bytes_accessed=8 * tokens * channels,
             ),
             name=name,
-        )(first, own, other, base, scales, proj)
-
-    if tensor == 4 and parts == 4:
-        place = lax.axis_index("tensor")
-        pick = lambda at: lax.dynamic_index_in_dim(grads, at, 0, False)
-        own, leaving = pick(place), [pick(place ^ k) for k in (2, 3, 1)]
-        own, leaving, first = lax.optimization_barrier((own, leaving, flag))
-        landed = [swap_with(v, "tensor", k) for k, v in zip((2, 3, 1), leaving)]
+        )(first, own, other, base, edges, proj)
+
+    if tensor == 4:
+        (own, *leaving), first = lax.optimization_barrier((parts, flag))
+        landed = [swap_with(v, "tensor", k) for k, v in zip(masks[1:], leaving)]
         mixed = finish(1, first, enter_f, other_f, mixed_loc, c_in, "mixed")
         landed, mixed = lax.optimization_barrier((landed, mixed))
         total = (own + landed[0] + landed[1] + landed[2]).astype(BF16)
         total, first = lax.optimization_barrier((total, first))
-        landed = [swap_with(total, "tensor", k) for k in (2, 3, 1)]
+        landed = [swap_with(total, "tensor", k) for k in masks[1:]]
         grad_inputs = finish(0, first, enter_b, other_b, gx_loc, b_in, "grad_inputs")
         landed, grad_inputs = lax.optimization_barrier((landed, grad_inputs))
-        summed = jnp.zeros((parts,) + total.shape, BF16)
-        summed = lax.dynamic_update_index_in_dim(summed, total, place, 0)
-        for k, v in zip((2, 3, 1), landed):
+        summed = jnp.zeros((4,) + total.shape, BF16)
+        for k, v in zip(masks, [total] + landed):
             summed = lax.dynamic_update_index_in_dim(summed, v, place ^ k, 0)
+        grad_b, grad_c = summed[:, 0], summed[:, 1]
     else:
         mixed = finish(1, flag, enter_f, other_f, mixed_loc, c_in, "mixed")
         grad_inputs = finish(0, flag, enter_b, other_b, gx_loc, b_in, "grad_inputs")
-        summed = lax.psum(grads, "tensor").astype(BF16)
-    grad_b = summed[:, 0].reshape(tokens, state)
-    grad_c = summed[:, 1].reshape(tokens, state)
-    return (mixed, grad_inputs, grad_b, grad_c)
+        grad_b, grad_c = lax.psum(parts[0], "tensor").astype(BF16)
+    return (mixed, grad_inputs, grad_b.reshape(tokens, state), grad_c.reshape(tokens, state))
 
 
 def solution(mesh):

time: 62.4 us -> 57.5 us (0.921)
  Pallas kernels: 32.9 us -> 29.4 us
  local copies, waits for them, and re-layouts: 2.93 us -> 1.06 us
  waiting for transfers between devices: 5.74 us -> 6.53 us
    pallas_call x3, Pallas kernels: 15.3 us -> 14 us  [the longest x2 9.09 us: finish(): pl.pallas_call(functools.partial(output_kernel, group, width, kind), grid...]
    pallas_call x1, Pallas kernels: 10.9 us -> 9.68 us  [shards(): pl.pallas_call(functools.partial(local_kernel, group, width), grid=(group...]
    pallas_call x1, Pallas kernels: 6.7 us -> 5.63 us  [shards(): pl.pallas_call(functools.partial(states_kernel, group, width), grid=(grou...]
    squeeze x1 -> x0, local copies, waits for them, and re-layouts: 0.95 us -> none  [shards(): pick = lambda at: lax.dynamic_index_in_dim(grads, at, 0, False)]
    unnamed x8 -> x22, local copies, waits for them, and re-layouts: 1.07 us -> 0.16 us
    max x0 -> x1, other arithmetic: none -> 0.84 us  [shards(): meta = lax.optimization_barrier(jnp.maximum(raw_meta, NEVER))]
    ppermute x13, waiting for transfers between devices: 5.74 us -> 6.53 us  [swap_with(): return lax.ppermute(value, axis, [(i, i ^ mask) for i in range(size)])]
    exp2 x2, other arithmetic: 0.77 us -> 0.04 us  [encode(): data = state * jnp.exp2(14.0 - power)[:, None]]
  transfers between devices with their start and end apart: 13 -> 13, of which waited for: 5 -> 6; matrix products, arithmetic and copies ran while one was open for 4% -> 4% of each run, Pallas kernels for 33% -> 33%
where the time goes in v4:
time: 57.5 us; the launch traced here: 57.1 us
  Pallas kernels  29.4 us (51%)
  starting transfers between devices  13.6 us (24%)
  waiting for transfers between devices  6.53 us (11%)
  other arithmetic  5.6 us (10%)
  local copies, waits for them, and re-layouts  1.06 us (2%)
  between operations  0.91 us (2%)
    ppermute x13, starting transfers between devices, swap_with(): return lax.ppermute(value, axis, [(i, i ^ mask) for i in range(size)])  13.6 us
    pallas_call x1, Pallas kernels, shards(): pl.pallas_call(functools.partial(local_kernel, group, width), grid=(group...  9.68 us
    pallas_call x2, Pallas kernels, finish(): pl.pallas_call(functools.partial(output_kernel, group, width, kind), grid...  9.09 us
    ppermute x13, waiting for transfers between devices, swap_with(): return lax.ppermute(value, axis, [(i, i ^ mask) for i in range(size)])  6.53 us
    pallas_call x1, Pallas kernels, shards(): pl.pallas_call(functools.partial(states_kernel, group, width), grid=(grou...  5.63 us
    pallas_call x1, Pallas kernels, shards(): pl.pallas_call(functools.partial(grads_kernel, group, width, masks), grid...  4.95 us
    add x2, other arithmetic, weigh(): functools.reduce(jnp.add, [w[:, None] * v.astype(F32) for w, v in terms])  2.96 us
    convert_element_type x1, other arithmetic, encode(): return jnp.concatenate([v.astype(jnp.float16) for v in rows], 0)  1.56 us
  transfers between devices with their start and end apart: 13, of which 6 were waited for; matrix products, arithmetic and copies ran while one was open for 4% of the time, Pallas kernels for 33%

profile of v4, /device:TPU:0, one launch (start us, length us, event | category | flops | bytes accessed | tf_op | source)
XLA Modules:
  0.0 57.1 jit_solution(2194599143134201788)
XLA Ops:
  0.6 5.6 %states.1 = (f32[16,128,128]{2,1,0:T(8,128)}, f32[16,128,128]{2,1,0:T(8,128)}, f32[8,16,128]{2,1,0:T(8,128)}, bf16[256,128]{1,0:T(8,128)(2,1)}) custom-call(s32[1]{0:T(128)} %bitcast.core_ref, bf16[256,2048]{1,0:T(8,128)(2,1)} %x_ref.3, bf16[256,2048]{1,0:T(8,128)(2,1)} %g_ref.3, f32[32,256]{1,0:T(8,128)} %step_blk.1, f32[1,32]{1,0:T(1,128)} %bitcast.82, ...), custom_call_target="tpu_custom_call" | custom-call | tf_op jit(solution)/shard_map/states/pallas_call | solution.py:463
  6.3 0.5 collective-permute-start.1
  6.8 0.1 collective-permute-start
  6.9 0.8 %broadcast_maximum_fusion = f32[8,16,128]{2,1,0:T(8,128)S(1)} fusion(f32[8,16,128]{2,1,0:T(8,128)} %get-tuple-element.48), kind=kLoop, calls=%fused_computation.33 | loop fusion | flops 16384 | bytes 131072 | tf_op jit(solution)/shard_map/max | solution.py:491
  7.7 1.7 %collective-permute-done = f32[8,16,128]{2,1,0:T(8,128)S(1)} collective-permute-done((f32[8,16,128]{2,1,0:T(8,128)}, f32[8,16,128]{2,1,0:T(8,128)S(1)}, u32[]{:S(2)}, u32[]{:S(2)}) %collective-permute-start) | collective-permute-done | bytes 65568 | tf_op jit(solution)/shard_map/ppermute | solution.py:367
  9.4 1.6 %multiply_convert_fusion = (f16[16,64,128]{2,1,0:T(8,128)(2,1)S(1)}, f16[16,64,128]{2,1,0:T(8,128)(2,1)S(1)}) fusion(f32[16,128]{1,0:T(8,128)S(1)} %get-tuple-element.98, pred[]{:T(512)S(6)} %eq.19, f32[16,128,128]{2,1,0:T(8,128)S(1)} %collective-permute-done.1, f32[16,128]{1,0:T(8,128)S(1)} %get-tuple-element.104, f32[16,128,128]{2,1,0:T(8,128)} %get-tuple-element.49, ...), kind=kLoop, calls=%fused_computation.24 | loop fusion | flops 1572864 | bytes 2670594 | tf_op jit(solution)/shard_map/convert_element_type | solution.py:397
  11.0 0.1 constant_dynamic-update-slice_fusion.9
  11.1 0.1 constant_dynamic-update-slice_fusion.4
  11.3 2.9 %collective-permute-start.2 = (f16[1088,128]{1,0:T(8,128)(2,1)S(1)}, f16[1088,128]{1,0:T(8,128)(2,1)S(1)}, u32[]{:S(2)}, u32[]{:S(2)}) collective-permute-start(f16[1088,128]{1,0:T(8,128)(2,1)S(1)} %get-tuple-element.51), channel_id=1, source_target_pairs={{0,8},{4,12},{8,0},{12,4},{16,24},{20,28},{24,16},{28,20},{1,9},{5... | collective-permute-start | bytes 835592 | tf_op jit(solution)/shard_map/ppermute | solution.py:367
  14.2 1.5 %collective-permute-start.3 = (f16[1088,128]{1,0:T(8,128)(2,1)S(1)}, f16[1088,128]{1,0:T(8,128)(2,1)S(1)}, u32[]{:S(2)}, u32[]{:S(2)}) collective-permute-start(f16[1088,128]{1,0:T(8,128)(2,1)S(1)} %get-tuple-element.52), channel_id=1, source_target_pairs={{0,16},{4,20},{8,24},{12,28},{16,0},{20,4},{24,8},{28,12},{1,17},{... | collective-permute-start | bytes 835592 | tf_op jit(solution)/shard_map/ppermute | solution.py:367
  15.7 9.7 %local.1 = (f32[256,2048]{1,0:T(8,128)}, f32[256,2048]{1,0:T(8,128)}, f32[2,256,128]{2,1,0:T(8,128)}) custom-call(f32[32]{0:T(128)} %skip_ref, bf16[256,2048]{1,0:T(8,128)(2,1)} %x_ref.3, bf16[256,2048]{1,0:T(8,128)(2,1)} %g_ref.3, f32[32,256]{1,0:T(8,128)} %step_blk.1, f32[32,256]{1,0:T(8,128)} %step_blk.1, f32[1,32]{1,0:T(1,128)} %bitcast.83, ...), custom_call_target="tpu_custom_call" | custom-call | flops 2684354560 | bytes 6291456 | tf_op jit(solution)/shard_map/local/pallas_call | solution.py:521
  25.4 3.1 %collective-permute-done.3 = f16[1088,128]{1,0:T(8,128)(2,1)S(1)} collective-permute-done((f16[1088,128]{1,0:T(8,128)(2,1)S(1)}, f16[1088,128]{1,0:T(8,128)(2,1)S(1)}, u32[]{:S(2)}, u32[]{:S(2)}) %collective-permute-start.3) | collective-permute-done | bytes 278560 | tf_op jit(solution)/shard_map/ppermute | solution.py:367
  28.7 0.1 slice.108
  28.7 0.1 slice.113
  28.9 1.4 %fusion.5 = (f32[16,64,128]{2,1,0:T(8,128)}, f32[16,64,128]{2,1,0:T(8,128)}) fusion(f16[16,64,128]{2,1,0:T(8,128)(2,1)S(1)} %bitcast.70, f16[16,64,128]{2,1,0:T(8,128)(2,1)S(1)} %bitcast.72, f16[16,64,128]{2,1,0:T(8,128)(2,1)S(1)} %bitcast.74, f32[16,128,128]{2,1,0:T(8,128)S(1)} %copy-done.6, f32[]{:T(128)S(6)} %select_n.220, ...), kind=kLoop, calls=%fused_computation.17 | loop fusion | flops 2228224 | bytes 2932744 | tf_op jit(solution)/shard_map/add | solution.py:441
  30.3 0.1 collective-permute-start.5
  30.4 0.5 collective-permute-start.6
  30.9 1.6 %fusion.11 = (f32[16,64,128]{2,1,0:T(8,128)S(1)}, f32[16,64,128]{2,1,0:T(8,128)S(1)}) fusion(f16[16,64,128]{2,1,0:T(8,128)(2,1)} %bitcast.71, f16[16,64,128]{2,1,0:T(8,128)(2,1)} %bitcast.73, f16[16,64,128]{2,1,0:T(8,128)(2,1)} %bitcast.75, f32[16,128,128]{2,1,0:T(8,128)S(1)} %collective-permute-done.1, f32[16,128]{1,0:T(8,128)S(1)} %get-tuple-element.67, ...), kind=kLoop, calls=%fused_computation.23 | loop fusion | flops 2228224 | bytes 2932744 | tf_op jit(solution)/shard_map/add | solution.py:441
  32.5 0.1 collective-permute-done.5.other_f.other
  32.6 0.7 %collective-permute-done.6.other_b.other = f32[16,64,128]{2,1,0:T(8,128)} collective-permute-done((f32[16,64,128]{2,1,0:T(8,128)}, f32[16,64,128]{2,1,0:T(8,128)}, u32[]{:S(2)}, u32[]{:S(2)}) %collective-permute-start.6) | collective-permute-done | bytes 524320 | tf_op jit(solution)/shard_map/ppermute | solution.py:367
  33.4 5.0 %grads.1 = (f32[2,64,128]{2,1,0:T(8,128)S(1)}, f32[2,64,128]{2,1,0:T(8,128)}, f32[2,64,128]{2,1,0:T(8,128)}, f32[2,64,128]{2,1,0:T(8,128)}) custom-call(s32[1]{0:T(128)} %bitcast.core_ref, s32[1]{0:T(128)} %bitcast.1.place_ref, f32[16,64,128]{2,1,0:T(8,128)S(1)} %get-tuple-element.108.own_f.own, f32[16,64,128]{2,1,0:T(8,128)} %collective-permute-done.5.other_f.other, ...), custom_call_target="tpu_custom_call" | custom-call | tf_op jit(solution)/shard_map/grads/pallas_call | solution.py:586
  38.4 2.7 %collective-permute-start.7 = (f32[2,64,128]{2,1,0:T(8,128)}, f32[2,64,128]{2,1,0:T(8,128)S(1)}, u32[]{:S(2)}, u32[]{:S(2)}) collective-permute-start(f32[2,64,128]{2,1,0:T(8,128)} %get-tuple-element.75), channel_id=1, source_target_pairs={{0,2},{1,3},{2,0},{3,1},{4,6},{5,7},{6,4},{7,5},{8,10},{9,11},{10,... | collective-permute-start | bytes 196616 | tf_op jit(solution)/shard_map/ppermute | solution.py:367
  41.0 1.4 %collective-permute-start.8 = (f32[2,64,128]{2,1,0:T(8,128)}, f32[2,64,128]{2,1,0:T(8,128)S(1)}, u32[]{:S(2)}, u32[]{:S(2)}) collective-permute-start(f32[2,64,128]{2,1,0:T(8,128)} %get-tuple-element.76), channel_id=1, source_target_pairs={{0,3},{1,2},{2,1},{3,0},{4,7},{5,6},{6,5},{7,4},{8,11},{9,10},{10,... | collective-permute-start | bytes 196616 | tf_op jit(solution)/shard_map/ppermute | solution.py:367
  42.4 0.2 collective-permute-start.9
  42.6 4.5 %mixed.1 = bf16[256,2048]{1,0:T(8,128)(2,1)} custom-call(s32[1]{0:T(128)} %bitcast.core_ref, f32[16,64,128]{2,1,0:T(8,128)} %copy-done.1, f32[16,64,128]{2,1,0:T(8,128)} %collective-permute-done.5.other_f.other, f32[256,2048]{1,0:T(8,128)} %get-tuple-element.79.base_ref, bf16[256,128]{1,0:T(8,128)(2,1)} %get-tuple-element.69.edges_ref, bf16[256,128]{1,0:T(8,128)(2,1)} %proj_ref.2), custom_call_target="tpu_custom_call" | custom-call | flops 268435456 | bytes 4194304 | tf_op jit(solution)/shard_map/mixed/pallas_call | solution.py:614
  47.1 0.5 collective-permute-done.8
  47.6 0.3 collective-permute-done.9
  48.0 2.6 %collective-permute-start.10 = (bf16[2,64,128]{2,1,0:T(8,128)(2,1)S(1)}, bf16[2,64,128]{2,1,0:T(8,128)(2,1)S(1)}, u32[]{:S(2)}, u32[]{:S(2)}) collective-permute-start(bf16[2,64,128]{2,1,0:T(8,128)(2,1)S(1)} %add_convert_fusion), channel_id=1, source_target_pairs={{0,2},{1,3},{2,0},{3,1},{4,6},{5,7},{6,4},{7,5},{8,10},{9,11},{10,... | collective-permute-start | bytes 98312 | tf_op jit(solution)/shard_map/ppermute | solution.py:367
  50.6 0.8 %collective-permute-start.11 = (bf16[2,64,128]{2,1,0:T(8,128)(2,1)S(1)}, bf16[2,64,128]{2,1,0:T(8,128)(2,1)S(1)}, u32[]{:S(2)}, u32[]{:S(2)}) collective-permute-start(bf16[2,64,128]{2,1,0:T(8,128)(2,1)S(1)} %add_convert_fusion), channel_id=1, source_target_pairs={{0,3},{1,2},{2,1},{3,0},{4,7},{5,6},{6,5},{7,4},{8,11},{9,10},{10,... | collective-permute-start | bytes 98312 | tf_op jit(solution)/shard_map/ppermute | solution.py:367
  51.4 0.3 collective-permute-start.12
  51.8 4.6 %grad_inputs.1 = bf16[256,2048]{1,0:T(8,128)(2,1)} custom-call(s32[1]{0:T(128)} %bitcast.core_ref, f32[16,64,128]{2,1,0:T(8,128)} %copy-done, f32[16,64,128]{2,1,0:T(8,128)} %collective-permute-done.6.other_b.other, f32[256,2048]{1,0:T(8,128)} %get-tuple-element.87.base_ref, bf16[256,128]{1,0:T(8,128)(2,1)} %get-tuple-element.69.edges_ref, ...), custom_call_target="tpu_custom_call" | custom-call | flops 268435456 | bytes 4194304 | tf_op jit(solution)/shard_map/grad_inputs/pallas_call | solution.py:614
  56.4 0.7 %fusion.33 = (bf16[4,1,64,128]{3,2,0,1:T(8,128)(2,1)}, bf16[4,1,64,128]{3,2,0,1:T(8,128)(2,1)}) fusion(bf16[4,2,64,128]{3,2,0,1:T(8,128)(2,1)S(1)} %bitcast_dynamic-update-slice_fusion), kind=kLoop, calls=%fused_computation.91 | loop fusion | bytes 262144 | tf_op jit(solution)/shard_map/slice | solution.py:650
  (44 shorter events, 0.5 us)
Async XLA Ops:
  6.3 3.2 %collective-permute-start.1 = (f32[16,128,128]{2,1,0:T(8,128)}, f32[16,128,128]{2,1,0:T(8,128)S(1)}, u32[]{:S(2)}, u32[]{:S(2)}) collective-permute-start(f32[16,128,128]{2,1,0:T(8,128)} %get-tuple-element.50), channel_id=1, source_target_pairs={{0,4},{4,0},{8,12},{12,8},{16,20},{20,16},{24,28},{28,24},{1,5},{5... | collective-permute-start | bytes 3145736 | tf_op jit(solution)/shard_map/ppermute | solution.py:367
  6.8 2.6 %collective-permute-start = (f32[8,16,128]{2,1,0:T(8,128)}, f32[8,16,128]{2,1,0:T(8,128)S(1)}, u32[]{:S(2)}, u32[]{:S(2)}) collective-permute-start(f32[8,16,128]{2,1,0:T(8,128)} %get-tuple-element.48), channel_id=1, source_target_pairs={{0,4},{4,0},{8,12},{12,8},{16,20},{20,16},{24,28},{28,24},{1,5},{5... | collective-permute-start | bytes 196616 | tf_op jit(solution)/shard_map/ppermute | solution.py:367
  11.3 14.2 %collective-permute-start.2 = (f16[1088,128]{1,0:T(8,128)(2,1)S(1)}, f16[1088,128]{1,0:T(8,128)(2,1)S(1)}, u32[]{:S(2)}, u32[]{:S(2)}) collective-permute-start(f16[1088,128]{1,0:T(8,128)(2,1)S(1)} %get-tuple-element.51), channel_id=1, source_target_pairs={{0,8},{4,12},{8,0},{12,4},{16,24},{20,28},{24,16},{28,20},{1,9},{5... | collective-permute-start | bytes 835592 | tf_op jit(solution)/shard_map/ppermute | solution.py:367
  14.2 14.4 %collective-permute-start.3 = (f16[1088,128]{1,0:T(8,128)(2,1)S(1)}, f16[1088,128]{1,0:T(8,128)(2,1)S(1)}, u32[]{:S(2)}, u32[]{:S(2)}) collective-permute-start(f16[1088,128]{1,0:T(8,128)(2,1)S(1)} %get-tuple-element.52), channel_id=1, source_target_pairs={{0,16},{4,20},{8,24},{12,28},{16,0},{20,4},{24,8},{28,12},{1,17},{... | collective-permute-start | bytes 835592 | tf_op jit(solution)/shard_map/ppermute | solution.py:367
  15.7 12.9 %collective-permute-start.4 = (f16[1088,128]{1,0:T(8,128)(2,1)S(1)}, f16[1088,128]{1,0:T(8,128)(2,1)S(1)}, u32[]{:S(2)}, u32[]{:S(2)}) collective-permute-start(f16[1088,128]{1,0:T(8,128)(2,1)S(1)} %get-tuple-element.52), channel_id=1, source_target_pairs={{0,24},{4,28},{8,16},{12,20},{16,8},{20,12},{24,0},{28,4},{1,25},{... | collective-permute-start | bytes 835592 | tf_op jit(solution)/shard_map/ppermute | solution.py:367
  25.4 3.4 %copy-start.6 = (f32[16,128,128]{2,1,0:T(8,128)S(1)}, f32[16,128,128]{2,1,0:T(8,128)}, u32[]{:S(2)}) copy-start(f32[16,128,128]{2,1,0:T(8,128)} %get-tuple-element.49) | copy-start | bytes 3145732
  28.6 1.6 %copy-start.7 = (f16[1024,128]{1,0:T(8,128)(2,1)}, f16[1024,128]{1,0:T(8,128)(2,1)S(1)}, u32[]{:S(2)}) copy-start(f16[1024,128]{1,0:T(8,128)(2,1)S(1)} %slice.100) | copy-start | bytes 786436
  28.7 1.6 %copy-start.8 = (f16[1024,128]{1,0:T(8,128)(2,1)}, f16[1024,128]{1,0:T(8,128)(2,1)S(1)}, u32[]{:S(2)}) copy-start(f16[1024,128]{1,0:T(8,128)(2,1)S(1)} %slice.108) | copy-start | bytes 786436
  28.8 1.5 %copy-start.9 = (f16[1024,128]{1,0:T(8,128)(2,1)}, f16[1024,128]{1,0:T(8,128)(2,1)S(1)}, u32[]{:S(2)}) copy-start(f16[1024,128]{1,0:T(8,128)(2,1)S(1)} %slice.113) | copy-start | bytes 786436
  30.3 3.1 %copy-start.2 = (bf16[256,2048]{1,0:T(8,128)(2,1)S(1)}, bf16[256,2048]{1,0:T(8,128)(2,1)}, u32[]{:S(2)}) copy-start(bf16[256,2048]{1,0:T(8,128)(2,1)} %x_ref.3) | copy-start | bytes 3145732
  30.3 3.1 %copy-start.3 = (bf16[256,2048]{1,0:T(8,128)(2,1)S(1)}, bf16[256,2048]{1,0:T(8,128)(2,1)}, u32[]{:S(2)}) copy-start(bf16[256,2048]{1,0:T(8,128)(2,1)} %g_ref.3) | copy-start | bytes 3145732
  30.3 3.1 %copy-start.4 = (bf16[256,128]{1,0:T(8,128)(2,1)S(1)}, bf16[256,128]{1,0:T(8,128)(2,1)}, u32[]{:S(2)}) copy-start(bf16[256,128]{1,0:T(8,128)(2,1)} %get-tuple-element.69.edges_ref) | copy-start | bytes 196612
  30.3 3.1 %copy-start.5 = (f32[2,256,128]{2,1,0:T(8,128)S(1)}, f32[2,256,128]{2,1,0:T(8,128)}, u32[]{:S(2)}) copy-start(f32[2,256,128]{2,1,0:T(8,128)} %get-tuple-element.70.local_ref) | copy-start | bytes 786436
  30.3 2.3 %collective-permute-start.5 = (f32[16,64,128]{2,1,0:T(8,128)}, f32[16,64,128]{2,1,0:T(8,128)}, u32[]{:S(2)}, u32[]{:S(2)}) collective-permute-start(f32[16,64,128]{2,1,0:T(8,128)} %get-tuple-element.64), channel_id=1, source_target_pairs={{0,4},{4,0},{8,12},{12,8},{16,20},{20,16},{24,28},{28,24},{1,5},{5... | collective-permute-start | bytes 1572872 | tf_op jit(solution)/shard_map/ppermute | solution.py:367
  30.4 3.0 %collective-permute-start.6 = (f32[16,64,128]{2,1,0:T(8,128)}, f32[16,64,128]{2,1,0:T(8,128)}, u32[]{:S(2)}, u32[]{:S(2)}) collective-permute-start(f32[16,64,128]{2,1,0:T(8,128)} %get-tuple-element.68), channel_id=1, source_target_pairs={{0,4},{4,0},{8,12},{12,8},{16,20},{20,16},{24,28},{28,24},{1,5},{5... | collective-permute-start | bytes 1572872 | tf_op jit(solution)/shard_map/ppermute | solution.py:367
  32.5 5.9 %copy-start = (f32[16,64,128]{2,1,0:T(8,128)}, f32[16,64,128]{2,1,0:T(8,128)S(1)}, u32[]{:S(2)}) copy-start(f32[16,64,128]{2,1,0:T(8,128)S(1)} %get-tuple-element.107.own_b.own) | copy-start | bytes 1572868
  32.5 5.9 %copy-start.1 = (f32[16,64,128]{2,1,0:T(8,128)}, f32[16,64,128]{2,1,0:T(8,128)S(1)}, u32[]{:S(2)}) copy-start(f32[16,64,128]{2,1,0:T(8,128)S(1)} %get-tuple-element.108.own_f.own) | copy-start | bytes 1572868
  38.4 8.8 %collective-permute-start.7 = (f32[2,64,128]{2,1,0:T(8,128)}, f32[2,64,128]{2,1,0:T(8,128)S(1)}, u32[]{:S(2)}, u32[]{:S(2)}) collective-permute-start(f32[2,64,128]{2,1,0:T(8,128)} %get-tuple-element.75), channel_id=1, source_target_pairs={{0,2},{1,3},{2,0},{3,1},{4,6},{5,7},{6,4},{7,5},{8,10},{9,11},{10,... | collective-permute-start | bytes 196616 | tf_op jit(solution)/shard_map/ppermute | solution.py:367
  41.0 6.6 %collective-permute-start.8 = (f32[2,64,128]{2,1,0:T(8,128)}, f32[2,64,128]{2,1,0:T(8,128)S(1)}, u32[]{:S(2)}, u32[]{:S(2)}) collective-permute-start(f32[2,64,128]{2,1,0:T(8,128)} %get-tuple-element.76), channel_id=1, source_target_pairs={{0,3},{1,2},{2,1},{3,0},{4,7},{5,6},{6,5},{7,4},{8,11},{9,10},{10,... | collective-permute-start | bytes 196616 | tf_op jit(solution)/shard_map/ppermute | solution.py:367
  42.4 5.6 %collective-permute-start.9 = (f32[2,64,128]{2,1,0:T(8,128)}, f32[2,64,128]{2,1,0:T(8,128)S(1)}, u32[]{:S(2)}, u32[]{:S(2)}) collective-permute-start(f32[2,64,128]{2,1,0:T(8,128)} %get-tuple-element.77), channel_id=1, source_target_pairs={{0,1},{1,0},{2,3},{3,2},{4,5},{5,4},{6,7},{7,6},{8,9},{9,8},{10,11... | collective-permute-start | bytes 196616 | tf_op jit(solution)/shard_map/ppermute | solution.py:367
  48.0 8.4 %collective-permute-start.10 = (bf16[2,64,128]{2,1,0:T(8,128)(2,1)S(1)}, bf16[2,64,128]{2,1,0:T(8,128)(2,1)S(1)}, u32[]{:S(2)}, u32[]{:S(2)}) collective-permute-start(bf16[2,64,128]{2,1,0:T(8,128)(2,1)S(1)} %add_convert_fusion), channel_id=1, source_target_pairs={{0,2},{1,3},{2,0},{3,1},{4,6},{5,7},{6,4},{7,5},{8,10},{9,11},{10,... | collective-permute-start | bytes 98312 | tf_op jit(solution)/shard_map/ppermute | solution.py:367
  50.6 5.8 %collective-permute-start.11 = (bf16[2,64,128]{2,1,0:T(8,128)(2,1)S(1)}, bf16[2,64,128]{2,1,0:T(8,128)(2,1)S(1)}, u32[]{:S(2)}, u32[]{:S(2)}) collective-permute-start(bf16[2,64,128]{2,1,0:T(8,128)(2,1)S(1)} %add_convert_fusion), channel_id=1, source_target_pairs={{0,3},{1,2},{2,1},{3,0},{4,7},{5,6},{6,5},{7,4},{8,11},{9,10},{10,... | collective-permute-start | bytes 98312 | tf_op jit(solution)/shard_map/ppermute | solution.py:367
  51.4 5.0 %collective-permute-start.12 = (bf16[2,64,128]{2,1,0:T(8,128)(2,1)S(1)}, bf16[2,64,128]{2,1,0:T(8,128)(2,1)S(1)}, u32[]{:S(2)}, u32[]{:S(2)}) collective-permute-start(bf16[2,64,128]{2,1,0:T(8,128)(2,1)S(1)} %add_convert_fusion), channel_id=1, source_target_pairs={{0,1},{1,0},{2,3},{3,2},{4,5},{5,4},{6,7},{7,6},{8,9},{9,8},{10,11... | collective-permute-start | bytes 98312 | tf_op jit(solution)/shard_map/ppermute | solution.py:367

commit v5 on v4

--- a/solution.py
+++ b/solution.py
@@ -198,9 +198,17 @@
                 send_ref[at, kind * half : (kind + 1) * half] = part[half:]
 
 
+def write_rows(masks, place_ref, total, out_ref):
+    rows = total.shape[1] // len(masks)
+    for k, mask in enumerate(masks):
+        at = pl.ds(pl.multiple_of((place_ref[0] ^ mask) * rows, rows), rows)
+        for slot in range(2):
+            out_ref[k, slot] = total[slot, at]
+
+
 def local_kernel(
-    group, width, skip_ref, x_ref, g_ref, step_ref, step_blk, decay_ref, doc_ref, b_ref, c_ref,
-    mixed_ref, gx_ref, grads_ref, down_s, across_s, bias, inter, common,
+    group, width, masks, skip_ref, place_ref, x_ref, g_ref, step_ref, step_blk, decay_ref, doc_ref, b_ref, c_ref,
+    mixed_ref, gx_ref, grads_ref, down_s, across_s, bias, inter, common, sums_s,
 ):
     step_id = pl.program_id(0)
     groups = down_s.shape[1]
@@ -289,10 +297,11 @@
         c00, c10, c11 = [split2(common[n]) for n in range(3)]
         b0, b1 = b_ref[:BLOCK], b_ref[BLOCK:]
         c0, c1 = c_ref[:BLOCK], c_ref[BLOCK:]
-        grads_ref[0, :BLOCK] = sum(dot(v, c0, TN) for v in c00) + sum(dot(v, c1, TN) for v in c10)
-        grads_ref[0, BLOCK:] = sum(dot(v, c1, TN) for v in c11)
-        grads_ref[1, :BLOCK] = sum(dot(v, b0, NN) for v in c00)
-        grads_ref[1, BLOCK:] = sum(dot(v, b0, NN) for v in c10) + sum(dot(v, b1, NN) for v in c11)
+        sums_s[0, :BLOCK] = sum(dot(v, c0, TN) for v in c00) + sum(dot(v, c1, TN) for v in c10)
+        sums_s[0, BLOCK:] = sum(dot(v, c1, TN) for v in c11)
+        sums_s[1, :BLOCK] = sum(dot(v, b0, NN) for v in c00)
+        sums_s[1, BLOCK:] = sum(dot(v, b0, NN) for v in c10) + sum(dot(v, b1, NN) for v in c11)
+        write_rows(masks, place_ref, sums_s, grads_ref)
 
 
 def place_state(core, own, other, high, low):
@@ -308,15 +317,14 @@
 
 def grads_kernel(
     group, width, masks, core_ref, place_ref, own_f, other_f, own_b, other_b, x_ref, g_ref, edges_ref,
-    local_ref, *rest,
+    out_ref, both, total,
 ):
-    outs, (both, total) = rest[:-2], rest[-2:]
     step_id = pl.program_id(0)
-    state = local_ref.shape[2]
+    state = total.shape[2]
 
     @pl.when(step_id == 0)
     def _():
-        total[...] = local_ref[...]
+        total[...] = jnp.zeros_like(total)
 
     edges = edges_ref[...]
     for slot, own, other, ref in ((0, own_b, other_b, x_ref), (1, own_f, other_f, g_ref)):
@@ -329,11 +337,7 @@
 
     @pl.when(step_id == pl.num_programs(0) - 1)
     def _():
-        rows = total.shape[1] // len(masks)
-        for mask, out in zip(masks, outs):
-            first = (place_ref[0] ^ mask) * rows
-            for slot in range(2):
-                out[slot] = total[slot, pl.ds(pl.multiple_of(first, rows), rows)]
+        write_rows(masks, place_ref, total, out_ref)
 
 
 def output_kernel(
@@ -518,10 +522,16 @@
         ]
 
     full = jax.ShapeDtypeStruct((tokens, channels), F32)
+    masks = (0, 2, 3, 1) if tensor == 4 else (0,)
+    rows = tokens // len(masks)
+    place = lax.axis_index("tensor")
+    part = jax.ShapeDtypeStruct((len(masks), 2, rows, state), F32)
+    spot = place.reshape(1) if tensor == 4 else jnp.zeros((1,), jnp.int32)
     mixed_loc, gx_loc, grads_loc = pl.pallas_call(
-        functools.partial(local_kernel, group, width),
+        functools.partial(local_kernel, group, width, masks),
         grid=(groups,),
         in_specs=[
+            SMEM,
             SMEM,
             tok,
             tok,
@@ -532,14 +542,15 @@
             whole((tokens, state)),
             whole((tokens, state)),
         ],
-        out_specs=[tok, tok, whole((2, tokens, state))],
-        out_shape=[full, full, jax.ShapeDtypeStruct((2, tokens, state), F32)],
+        out_specs=[tok, tok, whole(part.shape)],
+        out_shape=[full, full, part],
         scratch_shapes=[
             pltpu.VMEM((2, groups, BLOCK, group), F32),
             pltpu.VMEM((2, groups, group, BLOCK), F32),
             pltpu.VMEM((3, BLOCK, BLOCK), F32),
             pltpu.VMEM((3, BLOCK, BLOCK), F32),
             pltpu.VMEM((3, BLOCK, BLOCK), F32),
+            pltpu.VMEM((2, tokens, state), F32),
         ],
         compiler_params=grant(LOCAL_VMEM),
         cost_estimate=pl.CostEstimate(
@@ -548,7 +559,7 @@
             bytes_accessed=12 * tokens * channels,
         ),
         name="local",
-    )(skip, inputs, cotangent, step_size, step_size, decay, doc, b_in, c_in)
+    )(skip, spot, inputs, cotangent, step_size, step_size, decay, doc, b_in, c_in)
 
     one, zero = jnp.ones_like(own_e), jnp.zeros_like(own_e)
     if context == 8:
@@ -579,18 +590,13 @@
     enter_f = weigh([*zip(weights[2], states), (at_upper, sib_f)])
     enter_b = weigh([*zip(weights[3], states), (at_lower, sib_b)])
 
-    masks = (0, 2, 3, 1) if tensor == 4 else (0,)
-    rows = tokens // len(masks)
-    place = lax.axis_index("tensor")
     state_spec = pl.BlockSpec((per, half, LANES), lambda i: (i, 0, 0))
-    parts = pl.pallas_call(
+    carried = pl.pallas_call(
         functools.partial(grads_kernel, group, width, masks),
         grid=(groups,),
-        in_specs=[SMEM, SMEM]
-        + [state_spec] * 4
-        + [tok, tok, whole((tokens, 4 * heads)), whole((2, tokens, state))],
-        out_specs=[whole((2, rows, state))] * len(masks),
-        out_shape=[jax.ShapeDtypeStruct((2, rows, state), F32)] * len(masks),
+        in_specs=[SMEM, SMEM] + [state_spec] * 4 + [tok, tok, whole((tokens, 4 * heads))],
+        out_specs=whole(part.shape),
+        out_shape=part,
         scratch_shapes=[
             pltpu.VMEM((2, 2 * state, wide), BF16),
             pltpu.VMEM((2, tokens, state), F32),
@@ -598,17 +604,9 @@
         compiler_params=grant(GRADS_VMEM),
         name="grads",
     )(
-        flag,
-        place.reshape(1) if tensor == 4 else jnp.zeros((1,), jnp.int32),
-        enter_f,
-        other_f,
-        enter_b,
-        other_b,
-        inputs,
-        cotangent,
-        edges,
-        grads_loc,
+        flag, spot, enter_f, other_f, enter_b, other_b, inputs, cotangent, edges
     )
+    parts = [carried[k] + grads_loc[k] for k in range(len(masks))]
 
     def finish(kind, first, own, other, base, proj, name):
         return pl.pallas_call(

time: 57.5 us -> 54.2 us (0.943)
  other arithmetic: 5.6 us -> 3.43 us
  Pallas kernels: 29.4 us -> 27.5 us
  waiting for transfers between devices: 6.53 us -> 7.24 us
    add x2, other arithmetic: 2.96 us -> 0.77 us  [weigh(): functools.reduce(jnp.add, [w[:, None] * v.astype(F32) for w, v in terms])]
    pallas_call x1, Pallas kernels: 4.95 us -> 3.17 us  [shards(): pl.pallas_call(functools.partial(grads_kernel, group, width, masks), grid...]
    ppermute x13, waiting for transfers between devices: 6.53 us -> 7.24 us  [swap_with(): return lax.ppermute(value, axis, [(i, i ^ mask) for i in range(size)])]
  transfers between devices with their start and end apart: 13 -> 13, of which waited for: 6 -> 6; matrix products, arithmetic and copies ran while one was open for 4% -> 2% of each run, Pallas kernels for 33% -> 35%
where the time goes in v5:
time: 54.2 us; the launch traced here: 53.9 us
  Pallas kernels  27.5 us (51%)
  starting transfers between devices  13.7 us (25%)
  waiting for transfers between devices  7.24 us (13%)
  other arithmetic  3.43 us (6%)
  local copies, waits for them, and re-layouts  1.06 us (2%)
  between operations  0.93 us (2%)
    ppermute x13, starting transfers between devices, swap_with(): return lax.ppermute(value, axis, [(i, i ^ mask) for i in range(size)])  13.7 us
    pallas_call x1, Pallas kernels, shards(): pl.pallas_call(functools.partial(local_kernel, group, width, masks), grid...  9.63 us
    pallas_call x2, Pallas kernels, finish(): pl.pallas_call(functools.partial(output_kernel, group, width, kind), grid...  9.09 us
    ppermute x13, waiting for transfers between devices, swap_with(): return lax.ppermute(value, axis, [(i, i ^ mask) for i in range(size)])  7.24 us
    pallas_call x1, Pallas kernels, shards(): pl.pallas_call(functools.partial(states_kernel, group, width), grid=(grou...  5.63 us
    pallas_call x1, Pallas kernels, shards(): pl.pallas_call(functools.partial(grads_kernel, group, width, masks), grid...  3.17 us
    convert_element_type x1, other arithmetic, encode(): return jnp.concatenate([v.astype(jnp.float16) for v in rows], 0)  1.56 us
  transfers between devices with their start and end apart: 13, of which 6 were waited for; matrix products, arithmetic and copies ran while one was open for 2% of the time, Pallas kernels for 35%

profile of v5, /device:TPU:0, one launch (start us, length us, event | category | flops | bytes accessed | tf_op | source)
XLA Modules:
  0.0 53.9 jit_solution(2622044114406142102)
XLA Ops:
  0.6 5.6 %states.1 = (f32[16,128,128]{2,1,0:T(8,128)}, f32[16,128,128]{2,1,0:T(8,128)}, f32[8,16,128]{2,1,0:T(8,128)}, bf16[256,128]{1,0:T(8,128)(2,1)}) custom-call(s32[1]{0:T(128)} %bitcast.core_ref, bf16[256,2048]{1,0:T(8,128)(2,1)} %x_ref.3, bf16[256,2048]{1,0:T(8,128)(2,1)} %g_ref.3, f32[32,256]{1,0:T(8,128)} %step_blk.1, f32[1,32]{1,0:T(1,128)} %bitcast.90, ...), custom_call_target="tpu_custom_call" | custom-call | tf_op jit(solution)/shard_map/states/pallas_call | solution.py:467
  6.3 0.5 collective-permute-start.1
  6.8 0.1 collective-permute-start
  6.9 0.8 %broadcast_maximum_fusion = f32[8,16,128]{2,1,0:T(8,128)S(1)} fusion(f32[8,16,128]{2,1,0:T(8,128)} %get-tuple-element.44), kind=kLoop, calls=%fused_computation.41 | loop fusion | flops 16384 | bytes 131072 | tf_op jit(solution)/shard_map/max | solution.py:495
  7.7 1.7 %collective-permute-done = f32[8,16,128]{2,1,0:T(8,128)S(1)} collective-permute-done((f32[8,16,128]{2,1,0:T(8,128)}, f32[8,16,128]{2,1,0:T(8,128)S(1)}, u32[]{:S(2)}, u32[]{:S(2)}) %collective-permute-start) | collective-permute-done | bytes 65568 | tf_op jit(solution)/shard_map/ppermute | solution.py:371
  9.4 1.6 %multiply_convert_fusion = (f16[16,64,128]{2,1,0:T(8,128)(2,1)S(1)}, f16[16,64,128]{2,1,0:T(8,128)(2,1)S(1)}) fusion(f32[16,128]{1,0:T(8,128)S(1)} %get-tuple-element.90, pred[]{:T(512)S(6)} %eq.19, f32[16,128,128]{2,1,0:T(8,128)S(1)} %collective-permute-done.1, f32[16,128]{1,0:T(8,128)S(1)} %get-tuple-element.96, f32[16,128,128]{2,1,0:T(8,128)} %get-tuple-element.45, ...), kind=kLoop, calls=%fused_computation.24 | loop fusion | flops 1572864 | bytes 2670594 | tf_op jit(solution)/shard_map/convert_element_type | solution.py:401
  11.0 0.1 constant_dynamic-update-slice_fusion.9
  11.1 0.1 constant_dynamic-update-slice_fusion.4
  11.3 2.9 %collective-permute-start.2 = (f16[1088,128]{1,0:T(8,128)(2,1)S(1)}, f16[1088,128]{1,0:T(8,128)(2,1)S(1)}, u32[]{:S(2)}, u32[]{:S(2)}) collective-permute-start(f16[1088,128]{1,0:T(8,128)(2,1)S(1)} %get-tuple-element.47), channel_id=1, source_target_pairs={{0,8},{4,12},{8,0},{12,4},{16,24},{20,28},{24,16},{28,20},{1,9},{5... | collective-permute-start | bytes 835592 | tf_op jit(solution)/shard_map/ppermute | solution.py:371
  14.2 1.5 %collective-permute-start.3 = (f16[1088,128]{1,0:T(8,128)(2,1)S(1)}, f16[1088,128]{1,0:T(8,128)(2,1)S(1)}, u32[]{:S(2)}, u32[]{:S(2)}) collective-permute-start(f16[1088,128]{1,0:T(8,128)(2,1)S(1)} %get-tuple-element.48), channel_id=1, source_target_pairs={{0,16},{4,20},{8,24},{12,28},{16,0},{20,4},{24,8},{28,12},{1,17},{... | collective-permute-start | bytes 835592 | tf_op jit(solution)/shard_map/ppermute | solution.py:371
  15.7 9.6 %local.1 = (f32[256,2048]{1,0:T(8,128)}, f32[256,2048]{1,0:T(8,128)}, f32[4,2,64,128]{3,2,1,0:T(8,128)}) custom-call(f32[32]{0:T(128)} %skip_ref, s32[1]{0:T(128)} %bitcast.1.place_ref, bf16[256,2048]{1,0:T(8,128)(2,1)} %x_ref.3, bf16[256,2048]{1,0:T(8,128)(2,1)} %g_ref.3, f32[32,256]{1,0:T(8,128)} %step_blk.1, f32[32,256]{1,0:T(8,128)} %step_blk.1, ...), custom_call_target="tpu_custom_call" | custom-call | flops 2684354560 | bytes 6291456 | tf_op jit(solution)/shard_map/local/pallas_call | solution.py:530
  25.4 3.2 %collective-permute-done.3 = f16[1088,128]{1,0:T(8,128)(2,1)S(1)} collective-permute-done((f16[1088,128]{1,0:T(8,128)(2,1)S(1)}, f16[1088,128]{1,0:T(8,128)(2,1)S(1)}, u32[]{:S(2)}, u32[]{:S(2)}) %collective-permute-start.3) | collective-permute-done | bytes 278560 | tf_op jit(solution)/shard_map/ppermute | solution.py:371
  28.6 0.1 slice.132
  28.7 0.1 slice.137
  28.8 0.4 fusion.5
  29.3 0.1 collective-permute-start.5
  29.4 0.5 collective-permute-start.6
  29.9 0.4 fusion.11
  30.3 1.0 %collective-permute-done.5.other_f.other = f32[16,64,128]{2,1,0:T(8,128)S(1)} collective-permute-done((f32[16,64,128]{2,1,0:T(8,128)S(1)}, f32[16,64,128]{2,1,0:T(8,128)S(1)}, u32[]{:S(2)}, u32[]{:S(2)}) %collective-permute-start.5) | collective-permute-done | bytes 524320 | tf_op jit(solution)/shard_map/ppermute | solution.py:371
  31.3 0.7 %collective-permute-done.6.other_b.other = f32[16,64,128]{2,1,0:T(8,128)S(1)} collective-permute-done((f32[16,64,128]{2,1,0:T(8,128)S(1)}, f32[16,64,128]{2,1,0:T(8,128)S(1)}, u32[]{:S(2)}, u32[]{:S(2)}) %collective-permute-start.6) | collective-permute-done | bytes 524320 | tf_op jit(solution)/shard_map/ppermute | solution.py:371
  32.0 3.2 %grads.1 = f32[4,2,64,128]{3,2,1,0:T(8,128)S(1)} custom-call(s32[1]{0:T(128)} %bitcast.core_ref, s32[1]{0:T(128)} %bitcast.1.place_ref, f32[16,64,128]{2,1,0:T(8,128)S(1)} %get-tuple-element.100.own_f.own, f32[16,64,128]{2,1,0:T(8,128)S(1)} %collective-permute-done.5.other_f.other, f32[16,64,128]{2,1,0:T(8,128)S(1)} %get-tuple-element.99.own_b.own, ...), custom_call_target="tpu_custom_call" | custom-call | tf_op jit(solution)/shard_map/grads/pallas_call | solution.py:594
  35.3 2.7 %collective-permute-start.7 = (f32[2,64,128]{2,1,0:T(8,128)S(1)}, f32[2,64,128]{2,1,0:T(8,128)S(1)}, u32[]{:S(2)}, u32[]{:S(2)}) collective-permute-start(f32[2,64,128]{2,1,0:T(8,128)S(1)} %get-tuple-element.67), channel_id=1, source_target_pairs={{0,2},{1,3},{2,0},{3,1},{4,6},{5,7},{6,4},{7,5},{8,10},{9,11},{10,... | collective-permute-start | bytes 196616 | tf_op jit(solution)/shard_map/ppermute | solution.py:371
  38.0 1.4 %collective-permute-start.8 = (f32[2,64,128]{2,1,0:T(8,128)S(1)}, f32[2,64,128]{2,1,0:T(8,128)S(1)}, u32[]{:S(2)}, u32[]{:S(2)}) collective-permute-start(f32[2,64,128]{2,1,0:T(8,128)S(1)} %get-tuple-element.68), channel_id=1, source_target_pairs={{0,3},{1,2},{2,1},{3,0},{4,7},{5,6},{6,5},{7,4},{8,11},{9,10},{10,... | collective-permute-start | bytes 196616 | tf_op jit(solution)/shard_map/ppermute | solution.py:371
  39.3 0.2 collective-permute-start.9
  39.5 4.5 %mixed.1 = bf16[256,2048]{1,0:T(8,128)(2,1)} custom-call(s32[1]{0:T(128)} %bitcast.core_ref, f32[16,64,128]{2,1,0:T(8,128)} %copy-done.1, f32[16,64,128]{2,1,0:T(8,128)} %copy-done.5, f32[256,2048]{1,0:T(8,128)} %get-tuple-element.71.base_ref, bf16[256,128]{1,0:T(8,128)(2,1)} %get-tuple-element.65.edges_ref, bf16[256,128]{1,0:T(8,128)(2,1)} %proj_ref.2), custom_call_target="tpu_custom_call" | custom-call | flops 268435456 | bytes 4194304 | tf_op jit(solution)/shard_map/mixed/pallas_call | solution.py:612
  44.1 0.3 collective-permute-done.8
  44.4 0.3 collective-permute-done.9
  44.7 2.6 %collective-permute-start.10 = (bf16[2,64,128]{2,1,0:T(8,128)(2,1)S(1)}, bf16[2,64,128]{2,1,0:T(8,128)(2,1)S(1)}, u32[]{:S(2)}, u32[]{:S(2)}) collective-permute-start(bf16[2,64,128]{2,1,0:T(8,128)(2,1)S(1)} %add_convert_fusion), channel_id=1, source_target_pairs={{0,2},{1,3},{2,0},{3,1},{4,6},{5,7},{6,4},{7,5},{8,10},{9,11},{10,... | collective-permute-start | bytes 98312 | tf_op jit(solution)/shard_map/ppermute | solution.py:371
  47.3 1.0 %collective-permute-start.11 = (bf16[2,64,128]{2,1,0:T(8,128)(2,1)S(1)}, bf16[2,64,128]{2,1,0:T(8,128)(2,1)S(1)}, u32[]{:S(2)}, u32[]{:S(2)}) collective-permute-start(bf16[2,64,128]{2,1,0:T(8,128)(2,1)S(1)} %add_convert_fusion), channel_id=1, source_target_pairs={{0,3},{1,2},{2,1},{3,0},{4,7},{5,6},{6,5},{7,4},{8,11},{9,10},{10,... | collective-permute-start | bytes 98312 | tf_op jit(solution)/shard_map/ppermute | solution.py:371
  48.4 0.1 collective-permute-start.12
  48.5 4.6 %grad_inputs.1 = bf16[256,2048]{1,0:T(8,128)(2,1)} custom-call(s32[1]{0:T(128)} %bitcast.core_ref, f32[16,64,128]{2,1,0:T(8,128)} %copy-done, f32[16,64,128]{2,1,0:T(8,128)} %copy-done.4, f32[256,2048]{1,0:T(8,128)} %get-tuple-element.79.base_ref, bf16[256,128]{1,0:T(8,128)(2,1)} %get-tuple-element.65.edges_ref, bf16[256,128]{1,0:T(8,128)(2,1)} %proj_ref.3), custom_call_target="tpu_custom_call" | custom-call | flops 268435456 | bytes 4194304 | tf_op jit(solution)/shard_map/grad_inputs/pallas_call | solution.py:612
  53.2 0.7 %fusion.37 = (bf16[4,1,64,128]{3,2,0,1:T(8,128)(2,1)}, bf16[4,1,64,128]{3,2,0,1:T(8,128)(2,1)}) fusion(bf16[4,2,64,128]{3,2,0,1:T(8,128)(2,1)S(1)} %bitcast_dynamic-update-slice_fusion), kind=kLoop, calls=%fused_computation.99 | loop fusion | bytes 262144 | tf_op jit(solution)/shard_map/slice | solution.py:648
  (43 shorter events, 0.5 us)
Async XLA Ops:
  6.3 3.2 %collective-permute-start.1 = (f32[16,128,128]{2,1,0:T(8,128)}, f32[16,128,128]{2,1,0:T(8,128)S(1)}, u32[]{:S(2)}, u32[]{:S(2)}) collective-permute-start(f32[16,128,128]{2,1,0:T(8,128)} %get-tuple-element.46), channel_id=1, source_target_pairs={{0,4},{4,0},{8,12},{12,8},{16,20},{20,16},{24,28},{28,24},{1,5},{5... | collective-permute-start | bytes 3145736 | tf_op jit(solution)/shard_map/ppermute | solution.py:371
  6.8 2.6 %collective-permute-start = (f32[8,16,128]{2,1,0:T(8,128)}, f32[8,16,128]{2,1,0:T(8,128)S(1)}, u32[]{:S(2)}, u32[]{:S(2)}) collective-permute-start(f32[8,16,128]{2,1,0:T(8,128)} %get-tuple-element.44), channel_id=1, source_target_pairs={{0,4},{4,0},{8,12},{12,8},{16,20},{20,16},{24,28},{28,24},{1,5},{5... | collective-permute-start | bytes 196616 | tf_op jit(solution)/shard_map/ppermute | solution.py:371
  11.3 14.1 %collective-permute-start.2 = (f16[1088,128]{1,0:T(8,128)(2,1)S(1)}, f16[1088,128]{1,0:T(8,128)(2,1)S(1)}, u32[]{:S(2)}, u32[]{:S(2)}) collective-permute-start(f16[1088,128]{1,0:T(8,128)(2,1)S(1)} %get-tuple-element.47), channel_id=1, source_target_pairs={{0,8},{4,12},{8,0},{12,4},{16,24},{20,28},{24,16},{28,20},{1,9},{5... | collective-permute-start | bytes 835592 | tf_op jit(solution)/shard_map/ppermute | solution.py:371
  14.2 14.4 %collective-permute-start.3 = (f16[1088,128]{1,0:T(8,128)(2,1)S(1)}, f16[1088,128]{1,0:T(8,128)(2,1)S(1)}, u32[]{:S(2)}, u32[]{:S(2)}) collective-permute-start(f16[1088,128]{1,0:T(8,128)(2,1)S(1)} %get-tuple-element.48), channel_id=1, source_target_pairs={{0,16},{4,20},{8,24},{12,28},{16,0},{20,4},{24,8},{28,12},{1,17},{... | collective-permute-start | bytes 835592 | tf_op jit(solution)/shard_map/ppermute | solution.py:371
  15.7 12.9 %collective-permute-start.4 = (f16[1088,128]{1,0:T(8,128)(2,1)S(1)}, f16[1088,128]{1,0:T(8,128)(2,1)S(1)}, u32[]{:S(2)}, u32[]{:S(2)}) collective-permute-start(f16[1088,128]{1,0:T(8,128)(2,1)S(1)} %get-tuple-element.48), channel_id=1, source_target_pairs={{0,24},{4,28},{8,16},{12,20},{16,8},{20,12},{24,0},{28,4},{1,25},{... | collective-permute-start | bytes 835592 | tf_op jit(solution)/shard_map/ppermute | solution.py:371
  25.4 3.5 %copy-start.7 = (f32[16,128,128]{2,1,0:T(8,128)S(1)}, f32[16,128,128]{2,1,0:T(8,128)}, u32[]{:S(2)}) copy-start(f32[16,128,128]{2,1,0:T(8,128)} %get-tuple-element.45) | copy-start | bytes 3145732
  29.2 2.8 %copy-start.2 = (bf16[256,2048]{1,0:T(8,128)(2,1)S(1)}, bf16[256,2048]{1,0:T(8,128)(2,1)}, u32[]{:S(2)}) copy-start(bf16[256,2048]{1,0:T(8,128)(2,1)} %x_ref.3) | copy-start | bytes 3145732
  29.3 2.8 %copy-start.3 = (bf16[256,2048]{1,0:T(8,128)(2,1)S(1)}, bf16[256,2048]{1,0:T(8,128)(2,1)}, u32[]{:S(2)}) copy-start(bf16[256,2048]{1,0:T(8,128)(2,1)} %g_ref.3) | copy-start | bytes 3145732
  29.3 2.7 %copy-start.6 = (bf16[256,128]{1,0:T(8,128)(2,1)S(1)}, bf16[256,128]{1,0:T(8,128)(2,1)}, u32[]{:S(2)}) copy-start(bf16[256,128]{1,0:T(8,128)(2,1)} %get-tuple-element.65.edges_ref) | copy-start | bytes 196612
  29.3 2.0 %collective-permute-start.5 = (f32[16,64,128]{2,1,0:T(8,128)S(1)}, f32[16,64,128]{2,1,0:T(8,128)S(1)}, u32[]{:S(2)}, u32[]{:S(2)}) collective-permute-start(f32[16,64,128]{2,1,0:T(8,128)S(1)} %get-tuple-element.60), channel_id=1, source_target_pairs={{0,4},{4,0},{8,12},{12,8},{16,20},{20,16},{24,28},{28,24},{1,5},{5... | collective-permute-start | bytes 1572872 | tf_op jit(solution)/shard_map/ppermute | solution.py:371
  29.4 2.6 %collective-permute-start.6 = (f32[16,64,128]{2,1,0:T(8,128)S(1)}, f32[16,64,128]{2,1,0:T(8,128)S(1)}, u32[]{:S(2)}, u32[]{:S(2)}) collective-permute-start(f32[16,64,128]{2,1,0:T(8,128)S(1)} %get-tuple-element.64), channel_id=1, source_target_pairs={{0,4},{4,0},{8,12},{12,8},{16,20},{20,16},{24,28},{28,24},{1,5},{5... | collective-permute-start | bytes 1572872 | tf_op jit(solution)/shard_map/ppermute | solution.py:371
  30.2 5.0 %copy-start = (f32[16,64,128]{2,1,0:T(8,128)}, f32[16,64,128]{2,1,0:T(8,128)S(1)}, u32[]{:S(2)}) copy-start(f32[16,64,128]{2,1,0:T(8,128)S(1)} %get-tuple-element.99.own_b.own) | copy-start | bytes 1572868
  30.2 5.0 %copy-start.1 = (f32[16,64,128]{2,1,0:T(8,128)}, f32[16,64,128]{2,1,0:T(8,128)S(1)}, u32[]{:S(2)}) copy-start(f32[16,64,128]{2,1,0:T(8,128)S(1)} %get-tuple-element.100.own_f.own) | copy-start | bytes 1572868
  31.3 4.0 %copy-start.5 = (f32[16,64,128]{2,1,0:T(8,128)}, f32[16,64,128]{2,1,0:T(8,128)S(1)}, u32[]{:S(2)}) copy-start(f32[16,64,128]{2,1,0:T(8,128)S(1)} %collective-permute-done.5.other_f.other) | copy-start | bytes 1572868
  32.0 3.2 %copy-start.4 = (f32[16,64,128]{2,1,0:T(8,128)}, f32[16,64,128]{2,1,0:T(8,128)S(1)}, u32[]{:S(2)}) copy-start(f32[16,64,128]{2,1,0:T(8,128)S(1)} %collective-permute-done.6.other_b.other) | copy-start | bytes 1572868
  32.0 3.2 %copy-start.8 = (f32[4,2,64,128]{3,2,1,0:T(8,128)S(1)}, f32[4,2,64,128]{3,2,1,0:T(8,128)}, u32[]{:S(2)}) copy-start(f32[4,2,64,128]{3,2,1,0:T(8,128)} %get-tuple-element.66) | copy-start | bytes 786436
  35.3 8.8 %collective-permute-start.7 = (f32[2,64,128]{2,1,0:T(8,128)S(1)}, f32[2,64,128]{2,1,0:T(8,128)S(1)}, u32[]{:S(2)}, u32[]{:S(2)}) collective-permute-start(f32[2,64,128]{2,1,0:T(8,128)S(1)} %get-tuple-element.67), channel_id=1, source_target_pairs={{0,2},{1,3},{2,0},{3,1},{4,6},{5,7},{6,4},{7,5},{8,10},{9,11},{10,... | collective-permute-start | bytes 196616 | tf_op jit(solution)/shard_map/ppermute | solution.py:371
  38.0 6.4 %collective-permute-start.8 = (f32[2,64,128]{2,1,0:T(8,128)S(1)}, f32[2,64,128]{2,1,0:T(8,128)S(1)}, u32[]{:S(2)}, u32[]{:S(2)}) collective-permute-start(f32[2,64,128]{2,1,0:T(8,128)S(1)} %get-tuple-element.68), channel_id=1, source_target_pairs={{0,3},{1,2},{2,1},{3,0},{4,7},{5,6},{6,5},{7,4},{8,11},{9,10},{10,... | collective-permute-start | bytes 196616 | tf_op jit(solution)/shard_map/ppermute | solution.py:371
  39.3 5.4 %collective-permute-start.9 = (f32[2,64,128]{2,1,0:T(8,128)S(1)}, f32[2,64,128]{2,1,0:T(8,128)S(1)}, u32[]{:S(2)}, u32[]{:S(2)}) collective-permute-start(f32[2,64,128]{2,1,0:T(8,128)S(1)} %get-tuple-element.69), channel_id=1, source_target_pairs={{0,1},{1,0},{2,3},{3,2},{4,5},{5,4},{6,7},{7,6},{8,9},{9,8},{10,11... | collective-permute-start | bytes 196616 | tf_op jit(solution)/shard_map/ppermute | solution.py:371
  44.7 8.4 %collective-permute-start.10 = (bf16[2,64,128]{2,1,0:T(8,128)(2,1)S(1)}, bf16[2,64,128]{2,1,0:T(8,128)(2,1)S(1)}, u32[]{:S(2)}, u32[]{:S(2)}) collective-permute-start(bf16[2,64,128]{2,1,0:T(8,128)(2,1)S(1)} %add_convert_fusion), channel_id=1, source_target_pairs={{0,2},{1,3},{2,0},{3,1},{4,6},{5,7},{6,4},{7,5},{8,10},{9,11},{10,... | collective-permute-start | bytes 98312 | tf_op jit(solution)/shard_map/ppermute | solution.py:371
  47.3 5.8 %collective-permute-start.11 = (bf16[2,64,128]{2,1,0:T(8,128)(2,1)S(1)}, bf16[2,64,128]{2,1,0:T(8,128)(2,1)S(1)}, u32[]{:S(2)}, u32[]{:S(2)}) collective-permute-start(bf16[2,64,128]{2,1,0:T(8,128)(2,1)S(1)} %add_convert_fusion), channel_id=1, source_target_pairs={{0,3},{1,2},{2,1},{3,0},{4,7},{5,6},{6,5},{7,4},{8,11},{9,10},{10,... | collective-permute-start | bytes 98312 | tf_op jit(solution)/shard_map/ppermute | solution.py:371
  48.4 4.8 %collective-permute-start.12 = (bf16[2,64,128]{2,1,0:T(8,128)(2,1)S(1)}, bf16[2,64,128]{2,1,0:T(8,128)(2,1)S(1)}, u32[]{:S(2)}, u32[]{:S(2)}) collective-permute-start(bf16[2,64,128]{2,1,0:T(8,128)(2,1)S(1)} %add_convert_fusion), channel_id=1, source_target_pairs={{0,1},{1,0},{2,3},{3,2},{4,5},{5,4},{6,7},{7,6},{8,9},{9,8},{10,11... | collective-permute-start | bytes 98312 | tf_op jit(solution)/shard_map/ppermute | solution.py:371

commit v6 on v5

--- a/solution.py
+++ b/solution.py
@@ -464,9 +464,13 @@
 
     tok = pl.BlockSpec((tokens, wide), lambda i: (0, i))
     piece = pl.BlockSpec((per, state, LANES), lambda i: (i, 0, 0))
+    sgroup = min(32, heads)
+    sgroups = heads // sgroup
+    swide = sgroup * width
+    piece = pl.BlockSpec((swide // LANES, state, LANES), lambda i: (i, 0, 0))
     mine, send, raw_meta, edges = pl.pallas_call(
-        functools.partial(states_kernel, group, width),
-        grid=(groups,),
+        functools.partial(states_kernel, sgroup, width),
+        grid=(sgroups,),
         in_specs=[SMEM] + [HBM] * 7,
         out_specs=[piece, piece, whole((META, chunks, LANES)), whole((tokens, 4 * heads))],
         out_shape=[jax.ShapeDtypeStruct((chunks, state, LANES), F32)] * 2
@@ -475,8 +479,8 @@
             jax.ShapeDtypeStruct((tokens, 4 * heads), BF16),
         ],
         scratch_shapes=[
-            pltpu.VMEM((groups, tokens, wide), BF16),
-            pltpu.VMEM((groups, tokens, wide), BF16),
+            pltpu.VMEM((sgroups, tokens, swide), BF16),
+            pltpu.VMEM((sgroups, tokens, swide), BF16),
             pltpu.VMEM((heads, tokens), F32),
             pltpu.VMEM((1, heads), F32),
             pltpu.VMEM((1, tokens), jnp.int32),
@@ -486,13 +490,14 @@
             pltpu.VMEM((state, tokens), BF16),
             pltpu.VMEM((META, 4 * heads), BF16),
             pltpu.SemaphoreType.DMA((5,)),
-            pltpu.SemaphoreType.DMA((2, groups)),
+            pltpu.SemaphoreType.DMA((2, sgroups)),
         ],
         compiler_params=grant(STATES_VMEM),
         name="states",
     )(flag, inputs, cotangent, step_size, decay, doc, b_in, c_in)
 
-    meta = lax.optimization_barrier(jnp.maximum(raw_meta, NEVER))
+    least = float(jnp.finfo(F32).min)
+    meta, mine = lax.optimization_barrier((jnp.maximum(raw_meta, NEVER), jnp.maximum(mine, least)))
     theirs = swap_with(send, "context", 1)
     sib_meta = swap_with(raw_meta, "context", 1)
     lower = core == 0
@@ -590,15 +595,18 @@
     enter_f = weigh([*zip(weights[2], states), (at_upper, sib_f)])
     enter_b = weigh([*zip(weights[3], states), (at_lower, sib_b)])
 
-    state_spec = pl.BlockSpec((per, half, LANES), lambda i: (i, 0, 0))
+    ggroup = min(32, heads)
+    gwide = ggroup * width
+    gtok = pl.BlockSpec((tokens, gwide), lambda i: (0, i))
+    gstate = pl.BlockSpec((gwide // LANES, half, LANES), lambda i: (i, 0, 0))
     carried = pl.pallas_call(
-        functools.partial(grads_kernel, group, width, masks),
-        grid=(groups,),
-        in_specs=[SMEM, SMEM] + [state_spec] * 4 + [tok, tok, whole((tokens, 4 * heads))],
+        functools.partial(grads_kernel, ggroup, width, masks),
+        grid=(heads // ggroup,),
+        in_specs=[SMEM, SMEM] + [gstate] * 4 + [gtok, gtok, whole((tokens, 4 * heads))],
         out_specs=whole(part.shape),
         out_shape=part,
         scratch_shapes=[
-            pltpu.VMEM((2, 2 * state, wide), BF16),
+            pltpu.VMEM((2, 2 * state, gwide), BF16),
             pltpu.VMEM((2, tokens, state), F32),
         ],
         compiler_params=grant(GRADS_VMEM),
@@ -607,6 +615,8 @@
         flag, spot, enter_f, other_f, enter_b, other_b, inputs, cotangent, edges
     )
     parts = [carried[k] + grads_loc[k] for k in range(len(masks))]
+
+    state_spec = pl.BlockSpec((per, half, LANES), lambda i: (i, 0, 0))
 
     def finish(kind, first, own, other, base, proj, name):
         return pl.pallas_call(

time: 54.2 us -> 51.3 us (0.946)
  Pallas kernels: 27.5 us -> 25.8 us
  other arithmetic: 3.43 us -> 2.69 us
    pallas_call x2, Pallas kernels: 8.8 us -> 7.13 us  [the longest x1 4.7 us: shards(): pl.pallas_call(functools.partial(states_kernel, sgroup, width), grid=(sgr...]
    convert_element_type x1, other arithmetic: 1.56 us -> 0.36 us  [encode(): return jnp.concatenate([v.astype(jnp.float16) for v in rows], 0)]
    max x1 -> x2, other arithmetic: 0.84 us -> 1.32 us  [the longest x1 1.32 us: shards(): jnp.maximum(mine, least)]
  transfers between devices with their start and end apart: 13 -> 13, of which waited for: 6 -> 6; matrix products, arithmetic and copies ran while one was open for 2% -> 3% of each run, Pallas kernels for 35% -> 37%
where the time goes in v6:
time: 51.3 us; the launch traced here: 51 us
  Pallas kernels  25.8 us (50%)
  starting transfers between devices  13.7 us (27%)
  waiting for transfers between devices  6.76 us (13%)
  other arithmetic  2.69 us (5%)
  local copies, waits for them, and re-layouts  1.06 us (2%)
  between operations  0.95 us (2%)
    ppermute x13, starting transfers between devices, swap_with(): return lax.ppermute(value, axis, [(i, i ^ mask) for i in range(size)])  13.7 us
    pallas_call x1, Pallas kernels, shards(): pl.pallas_call(functools.partial(local_kernel, group, width, masks), grid...  9.61 us
    pallas_call x2, Pallas kernels, finish(): pl.pallas_call(functools.partial(output_kernel, group, width, kind), grid...  9.09 us
    ppermute x13, waiting for transfers between devices, swap_with(): return lax.ppermute(value, axis, [(i, i ^ mask) for i in range(size)])  6.76 us
    pallas_call x1, Pallas kernels, shards(): pl.pallas_call(functools.partial(states_kernel, sgroup, width), grid=(sgr...  4.7 us
    pallas_call x1, Pallas kernels, shards(): pl.pallas_call(functools.partial(grads_kernel, ggroup, width, masks), gri...  2.43 us
    max x1, other arithmetic, shards(): jnp.maximum(mine, least)  1.32 us
  transfers between devices with their start and end apart: 13, of which 6 were waited for; matrix products, arithmetic and copies ran while one was open for 3% of the time, Pallas kernels for 37%

profile of v6, /device:TPU:0, one launch (start us, length us, event | category | flops | bytes accessed | tf_op | source)
XLA Modules:
  0.0 51.0 jit_solution(17674710149164111583)
XLA Ops:
  0.6 4.7 %states.1 = (f32[16,128,128]{2,1,0:T(8,128)}, f32[16,128,128]{2,1,0:T(8,128)}, f32[8,16,128]{2,1,0:T(8,128)}, bf16[256,128]{1,0:T(8,128)(2,1)}) custom-call(s32[1]{0:T(128)} %bitcast.core_ref, bf16[256,2048]{1,0:T(8,128)(2,1)} %x_ref.3, bf16[256,2048]{1,0:T(8,128)(2,1)} %g_ref.3, f32[32,256]{1,0:T(8,128)} %step_blk.1, f32[1,32]{1,0:T(1,128)} %bitcast.86, ...), custom_call_target="tpu_custom_call" | custom-call | tf_op jit(solution)/shard_map/states/pallas_call | solution.py:471
  5.4 0.5 %collective-permute-start.1 = (f32[16,128,128]{2,1,0:T(8,128)}, f32[16,128,128]{2,1,0:T(8,128)S(1)}, u32[]{:S(2)}, u32[]{:S(2)}) collective-permute-start(f32[16,128,128]{2,1,0:T(8,128)} %get-tuple-element.50), channel_id=1, source_target_pairs={{0,4},{4,0},{8,12},{12,8},{16,20},{20,16},{24,28},{28,24},{1,5},{5... | collective-permute-start | bytes 3145736 | tf_op jit(solution)/shard_map/ppermute | solution.py:371
  5.9 0.1 collective-permute-start
  6.0 1.3 %broadcast_maximum_fusion = f32[16,128,128]{2,1,0:T(8,128)S(1)} fusion(f32[16,128,128]{2,1,0:T(8,128)} %get-tuple-element.47), kind=kLoop, calls=%fused_computation.28 | loop fusion | flops 262144 | bytes 2097152 | tf_op jit(solution)/shard_map/max | solution.py:500
  7.3 1.1 %collective-permute-done = f32[8,16,128]{2,1,0:T(8,128)S(1)} collective-permute-done((f32[8,16,128]{2,1,0:T(8,128)}, f32[8,16,128]{2,1,0:T(8,128)S(1)}, u32[]{:S(2)}, u32[]{:S(2)}) %collective-permute-start) | collective-permute-done | bytes 65568 | tf_op jit(solution)/shard_map/ppermute | solution.py:371
  8.5 0.4 multiply_convert_fusion
  8.9 0.1 constant_dynamic-update-slice_fusion.9
  8.9 0.1 constant_dynamic-update-slice_fusion.4
  9.2 2.9 %collective-permute-start.2 = (f16[1088,128]{1,0:T(8,128)(2,1)S(1)}, f16[1088,128]{1,0:T(8,128)(2,1)S(1)}, u32[]{:S(2)}, u32[]{:S(2)}) collective-permute-start(f16[1088,128]{1,0:T(8,128)(2,1)S(1)} %get-tuple-element.51), channel_id=1, source_target_pairs={{0,8},{4,12},{8,0},{12,4},{16,24},{20,28},{24,16},{28,20},{1,9},{5... | collective-permute-start | bytes 835592 | tf_op jit(solution)/shard_map/ppermute | solution.py:371
  12.1 1.5 %collective-permute-start.3 = (f16[1088,128]{1,0:T(8,128)(2,1)S(1)}, f16[1088,128]{1,0:T(8,128)(2,1)S(1)}, u32[]{:S(2)}, u32[]{:S(2)}) collective-permute-start(f16[1088,128]{1,0:T(8,128)(2,1)S(1)} %get-tuple-element.52), channel_id=1, source_target_pairs={{0,16},{4,20},{8,24},{12,28},{16,0},{20,4},{24,8},{28,12},{1,17},{... | collective-permute-start | bytes 835592 | tf_op jit(solution)/shard_map/ppermute | solution.py:371
  13.6 9.6 %local.1 = (f32[256,2048]{1,0:T(8,128)}, f32[256,2048]{1,0:T(8,128)}, f32[4,2,64,128]{3,2,1,0:T(8,128)}) custom-call(f32[32]{0:T(128)} %skip_ref, s32[1]{0:T(128)} %bitcast.1.place_ref, bf16[256,2048]{1,0:T(8,128)(2,1)} %x_ref.3, bf16[256,2048]{1,0:T(8,128)(2,1)} %g_ref.3, f32[32,256]{1,0:T(8,128)} %step_blk.1, f32[32,256]{1,0:T(8,128)} %step_blk.1, ...), custom_call_target="tpu_custom_call" | custom-call | flops 2684354560 | bytes 6291456 | tf_op jit(solution)/shard_map/local/pallas_call | solution.py:535
  23.2 3.2 %collective-permute-done.3 = f16[1088,128]{1,0:T(8,128)(2,1)S(1)} collective-permute-done((f16[1088,128]{1,0:T(8,128)(2,1)S(1)}, f16[1088,128]{1,0:T(8,128)(2,1)S(1)}, u32[]{:S(2)}, u32[]{:S(2)}) %collective-permute-start.3) | collective-permute-done | bytes 278560 | tf_op jit(solution)/shard_map/ppermute | solution.py:371
  26.5 0.1 slice.132
  26.6 0.1 slice.137
  26.7 0.4 fusion.5
  27.1 0.1 collective-permute-start.5
  27.2 0.5 collective-permute-start.6
  27.7 0.4 fusion.11
  28.1 1.0 %collective-permute-done.5.other_f.other = f32[16,64,128]{2,1,0:T(8,128)S(1)} collective-permute-done((f32[16,64,128]{2,1,0:T(8,128)S(1)}, f32[16,64,128]{2,1,0:T(8,128)S(1)}, u32[]{:S(2)}, u32[]{:S(2)}) %collective-permute-start.5) | collective-permute-done | bytes 524320 | tf_op jit(solution)/shard_map/ppermute | solution.py:371
  29.1 0.7 %collective-permute-done.6.other_b.other = f32[16,64,128]{2,1,0:T(8,128)S(1)} collective-permute-done((f32[16,64,128]{2,1,0:T(8,128)S(1)}, f32[16,64,128]{2,1,0:T(8,128)S(1)}, u32[]{:S(2)}, u32[]{:S(2)}) %collective-permute-start.6) | collective-permute-done | bytes 524320 | tf_op jit(solution)/shard_map/ppermute | solution.py:371
  29.9 2.4 %grads.1 = f32[4,2,64,128]{3,2,1,0:T(8,128)S(1)} custom-call(s32[1]{0:T(128)} %bitcast.core_ref, s32[1]{0:T(128)} %bitcast.1.place_ref, f32[16,64,128]{2,1,0:T(8,128)S(1)} %get-tuple-element.104.own_f.own, f32[16,64,128]{2,1,0:T(8,128)S(1)} %collective-permute-done.5.other_f.other, f32[16,64,128]{2,1,0:T(8,128)S(1)} %get-tuple-element.103.own_b.own, ...), custom_call_target="tpu_custom_call" | custom-call | tf_op jit(solution)/shard_map/grads/pallas_call | solution.py:602
  32.4 2.7 %collective-permute-start.7 = (f32[2,64,128]{2,1,0:T(8,128)S(1)}, f32[2,64,128]{2,1,0:T(8,128)S(1)}, u32[]{:S(2)}, u32[]{:S(2)}) collective-permute-start(f32[2,64,128]{2,1,0:T(8,128)S(1)} %get-tuple-element.71), channel_id=1, source_target_pairs={{0,2},{1,3},{2,0},{3,1},{4,6},{5,7},{6,4},{7,5},{8,10},{9,11},{10,... | collective-permute-start | bytes 196616 | tf_op jit(solution)/shard_map/ppermute | solution.py:371
  35.1 1.3 %collective-permute-start.8 = (f32[2,64,128]{2,1,0:T(8,128)S(1)}, f32[2,64,128]{2,1,0:T(8,128)S(1)}, u32[]{:S(2)}, u32[]{:S(2)}) collective-permute-start(f32[2,64,128]{2,1,0:T(8,128)S(1)} %get-tuple-element.72), channel_id=1, source_target_pairs={{0,3},{1,2},{2,1},{3,0},{4,7},{5,6},{6,5},{7,4},{8,11},{9,10},{10,... | collective-permute-start | bytes 196616 | tf_op jit(solution)/shard_map/ppermute | solution.py:371
  36.4 0.2 collective-permute-start.9
  36.6 4.5 %mixed.1 = bf16[256,2048]{1,0:T(8,128)(2,1)} custom-call(s32[1]{0:T(128)} %bitcast.core_ref, f32[16,64,128]{2,1,0:T(8,128)} %copy-done.1, f32[16,64,128]{2,1,0:T(8,128)} %copy-done.5, f32[256,2048]{1,0:T(8,128)} %get-tuple-element.75.base_ref, bf16[256,128]{1,0:T(8,128)(2,1)} %get-tuple-element.69.edges_ref, bf16[256,128]{1,0:T(8,128)(2,1)} %proj_ref.2), custom_call_target="tpu_custom_call" | custom-call | flops 268435456 | bytes 4194304 | tf_op jit(solution)/shard_map/mixed/pallas_call | solution.py:622
  41.2 0.3 collective-permute-done.8
  41.5 0.3 collective-permute-done.9
  41.8 2.6 %collective-permute-start.10 = (bf16[2,64,128]{2,1,0:T(8,128)(2,1)S(1)}, bf16[2,64,128]{2,1,0:T(8,128)(2,1)S(1)}, u32[]{:S(2)}, u32[]{:S(2)}) collective-permute-start(bf16[2,64,128]{2,1,0:T(8,128)(2,1)S(1)} %add_convert_fusion), channel_id=1, source_target_pairs={{0,2},{1,3},{2,0},{3,1},{4,6},{5,7},{6,4},{7,5},{8,10},{9,11},{10,... | collective-permute-start | bytes 98312 | tf_op jit(solution)/shard_map/ppermute | solution.py:371
  44.5 1.0 %collective-permute-start.11 = (bf16[2,64,128]{2,1,0:T(8,128)(2,1)S(1)}, bf16[2,64,128]{2,1,0:T(8,128)(2,1)S(1)}, u32[]{:S(2)}, u32[]{:S(2)}) collective-permute-start(bf16[2,64,128]{2,1,0:T(8,128)(2,1)S(1)} %add_convert_fusion), channel_id=1, source_target_pairs={{0,3},{1,2},{2,1},{3,0},{4,7},{5,6},{6,5},{7,4},{8,11},{9,10},{10,... | collective-permute-start | bytes 98312 | tf_op jit(solution)/shard_map/ppermute | solution.py:371
  45.4 0.2 collective-permute-start.12
  45.7 4.6 %grad_inputs.1 = bf16[256,2048]{1,0:T(8,128)(2,1)} custom-call(s32[1]{0:T(128)} %bitcast.core_ref, f32[16,64,128]{2,1,0:T(8,128)} %copy-done, f32[16,64,128]{2,1,0:T(8,128)} %copy-done.4, f32[256,2048]{1,0:T(8,128)} %get-tuple-element.83.base_ref, bf16[256,128]{1,0:T(8,128)(2,1)} %get-tuple-element.69.edges_ref, bf16[256,128]{1,0:T(8,128)(2,1)} %proj_ref.3), custom_call_target="tpu_custom_call" | custom-call | flops 268435456 | bytes 4194304 | tf_op jit(solution)/shard_map/grad_inputs/pallas_call | solution.py:622
  50.3 0.7 %fusion.35 = (bf16[4,1,64,128]{3,2,0,1:T(8,128)(2,1)}, bf16[4,1,64,128]{3,2,0,1:T(8,128)(2,1)}) fusion(bf16[4,2,64,128]{3,2,0,1:T(8,128)(2,1)S(1)} %bitcast_dynamic-update-slice_fusion), kind=kLoop, calls=%fused_computation.98 | loop fusion | bytes 262144 | tf_op jit(solution)/shard_map/slice | solution.py:658
  (44 shorter events, 0.5 us)
Async XLA Ops:
  5.3 1.9 %copy-start.8 = (f32[8,16,128]{2,1,0:T(8,128)S(1)}, f32[8,16,128]{2,1,0:T(8,128)}, u32[]{:S(2)}) copy-start(f32[8,16,128]{2,1,0:T(8,128)} %get-tuple-element.46) | copy-start | bytes 196612
  5.4 3.2 %collective-permute-start.1 = (f32[16,128,128]{2,1,0:T(8,128)}, f32[16,128,128]{2,1,0:T(8,128)S(1)}, u32[]{:S(2)}, u32[]{:S(2)}) collective-permute-start(f32[16,128,128]{2,1,0:T(8,128)} %get-tuple-element.50), channel_id=1, source_target_pairs={{0,4},{4,0},{8,12},{12,8},{16,20},{20,16},{24,28},{28,24},{1,5},{5... | collective-permute-start | bytes 3145736 | tf_op jit(solution)/shard_map/ppermute | solution.py:371
  5.9 2.6 %collective-permute-start = (f32[8,16,128]{2,1,0:T(8,128)}, f32[8,16,128]{2,1,0:T(8,128)S(1)}, u32[]{:S(2)}, u32[]{:S(2)}) collective-permute-start(f32[8,16,128]{2,1,0:T(8,128)} %get-tuple-element.46), channel_id=1, source_target_pairs={{0,4},{4,0},{8,12},{12,8},{16,20},{20,16},{24,28},{28,24},{1,5},{5... | collective-permute-start | bytes 196616 | tf_op jit(solution)/shard_map/ppermute | solution.py:371
  9.2 14.1 %collective-permute-start.2 = (f16[1088,128]{1,0:T(8,128)(2,1)S(1)}, f16[1088,128]{1,0:T(8,128)(2,1)S(1)}, u32[]{:S(2)}, u32[]{:S(2)}) collective-permute-start(f16[1088,128]{1,0:T(8,128)(2,1)S(1)} %get-tuple-element.51), channel_id=1, source_target_pairs={{0,8},{4,12},{8,0},{12,4},{16,24},{20,28},{24,16},{28,20},{1,9},{5... | collective-permute-start | bytes 835592 | tf_op jit(solution)/shard_map/ppermute | solution.py:371
  12.1 14.4 %collective-permute-start.3 = (f16[1088,128]{1,0:T(8,128)(2,1)S(1)}, f16[1088,128]{1,0:T(8,128)(2,1)S(1)}, u32[]{:S(2)}, u32[]{:S(2)}) collective-permute-start(f16[1088,128]{1,0:T(8,128)(2,1)S(1)} %get-tuple-element.52), channel_id=1, source_target_pairs={{0,16},{4,20},{8,24},{12,28},{16,0},{20,4},{24,8},{28,12},{1,17},{... | collective-permute-start | bytes 835592 | tf_op jit(solution)/shard_map/ppermute | solution.py:371
  13.6 12.9 %collective-permute-start.4 = (f16[1088,128]{1,0:T(8,128)(2,1)S(1)}, f16[1088,128]{1,0:T(8,128)(2,1)S(1)}, u32[]{:S(2)}, u32[]{:S(2)}) collective-permute-start(f16[1088,128]{1,0:T(8,128)(2,1)S(1)} %get-tuple-element.52), channel_id=1, source_target_pairs={{0,24},{4,28},{8,16},{12,20},{16,8},{20,12},{24,0},{28,4},{1,25},{... | collective-permute-start | bytes 835592 | tf_op jit(solution)/shard_map/ppermute | solution.py:371
  27.1 2.8 %copy-start.2 = (bf16[256,2048]{1,0:T(8,128)(2,1)S(1)}, bf16[256,2048]{1,0:T(8,128)(2,1)}, u32[]{:S(2)}) copy-start(bf16[256,2048]{1,0:T(8,128)(2,1)} %x_ref.3) | copy-start | bytes 3145732
  27.1 2.8 %copy-start.3 = (bf16[256,2048]{1,0:T(8,128)(2,1)S(1)}, bf16[256,2048]{1,0:T(8,128)(2,1)}, u32[]{:S(2)}) copy-start(bf16[256,2048]{1,0:T(8,128)(2,1)} %g_ref.3) | copy-start | bytes 3145732
  27.1 2.7 %copy-start.6 = (bf16[256,128]{1,0:T(8,128)(2,1)S(1)}, bf16[256,128]{1,0:T(8,128)(2,1)}, u32[]{:S(2)}) copy-start(bf16[256,128]{1,0:T(8,128)(2,1)} %get-tuple-element.69.edges_ref) | copy-start | bytes 196612
  27.1 2.0 %collective-permute-start.5 = (f32[16,64,128]{2,1,0:T(8,128)S(1)}, f32[16,64,128]{2,1,0:T(8,128)S(1)}, u32[]{:S(2)}, u32[]{:S(2)}) collective-permute-start(f32[16,64,128]{2,1,0:T(8,128)S(1)} %get-tuple-element.64), channel_id=1, source_target_pairs={{0,4},{4,0},{8,12},{12,8},{16,20},{20,16},{24,28},{28,24},{1,5},{5... | collective-permute-start | bytes 1572872 | tf_op jit(solution)/shard_map/ppermute | solution.py:371
  27.2 2.6 %collective-permute-start.6 = (f32[16,64,128]{2,1,0:T(8,128)S(1)}, f32[16,64,128]{2,1,0:T(8,128)S(1)}, u32[]{:S(2)}, u32[]{:S(2)}) collective-permute-start(f32[16,64,128]{2,1,0:T(8,128)S(1)} %get-tuple-element.68), channel_id=1, source_target_pairs={{0,4},{4,0},{8,12},{12,8},{16,20},{20,16},{24,28},{28,24},{1,5},{5... | collective-permute-start | bytes 1572872 | tf_op jit(solution)/shard_map/ppermute | solution.py:371
  28.1 4.2 %copy-start = (f32[16,64,128]{2,1,0:T(8,128)}, f32[16,64,128]{2,1,0:T(8,128)S(1)}, u32[]{:S(2)}) copy-start(f32[16,64,128]{2,1,0:T(8,128)S(1)} %get-tuple-element.103.own_b.own) | copy-start | bytes 1572868
  28.1 4.2 %copy-start.1 = (f32[16,64,128]{2,1,0:T(8,128)}, f32[16,64,128]{2,1,0:T(8,128)S(1)}, u32[]{:S(2)}) copy-start(f32[16,64,128]{2,1,0:T(8,128)S(1)} %get-tuple-element.104.own_f.own) | copy-start | bytes 1572868
  29.1 3.2 %copy-start.5 = (f32[16,64,128]{2,1,0:T(8,128)}, f32[16,64,128]{2,1,0:T(8,128)S(1)}, u32[]{:S(2)}) copy-start(f32[16,64,128]{2,1,0:T(8,128)S(1)} %collective-permute-done.5.other_f.other) | copy-start | bytes 1572868
  29.9 2.5 %copy-start.4 = (f32[16,64,128]{2,1,0:T(8,128)}, f32[16,64,128]{2,1,0:T(8,128)S(1)}, u32[]{:S(2)}) copy-start(f32[16,64,128]{2,1,0:T(8,128)S(1)} %collective-permute-done.6.other_b.other) | copy-start | bytes 1572868
  29.9 2.5 %copy-start.7 = (f32[4,2,64,128]{3,2,1,0:T(8,128)S(1)}, f32[4,2,64,128]{3,2,1,0:T(8,128)}, u32[]{:S(2)}) copy-start(f32[4,2,64,128]{3,2,1,0:T(8,128)} %get-tuple-element.70) | copy-start | bytes 786436
  32.4 8.8 %collective-permute-start.7 = (f32[2,64,128]{2,1,0:T(8,128)S(1)}, f32[2,64,128]{2,1,0:T(8,128)S(1)}, u32[]{:S(2)}, u32[]{:S(2)}) collective-permute-start(f32[2,64,128]{2,1,0:T(8,128)S(1)} %get-tuple-element.71), channel_id=1, source_target_pairs={{0,2},{1,3},{2,0},{3,1},{4,6},{5,7},{6,4},{7,5},{8,10},{9,11},{10,... | collective-permute-start | bytes 196616 | tf_op jit(solution)/shard_map/ppermute | solution.py:371
  35.1 6.4 %collective-permute-start.8 = (f32[2,64,128]{2,1,0:T(8,128)S(1)}, f32[2,64,128]{2,1,0:T(8,128)S(1)}, u32[]{:S(2)}, u32[]{:S(2)}) collective-permute-start(f32[2,64,128]{2,1,0:T(8,128)S(1)} %get-tuple-element.72), channel_id=1, source_target_pairs={{0,3},{1,2},{2,1},{3,0},{4,7},{5,6},{6,5},{7,4},{8,11},{9,10},{10,... | collective-permute-start | bytes 196616 | tf_op jit(solution)/shard_map/ppermute | solution.py:371
  36.4 5.4 %collective-permute-start.9 = (f32[2,64,128]{2,1,0:T(8,128)S(1)}, f32[2,64,128]{2,1,0:T(8,128)S(1)}, u32[]{:S(2)}, u32[]{:S(2)}) collective-permute-start(f32[2,64,128]{2,1,0:T(8,128)S(1)} %get-tuple-element.73), channel_id=1, source_target_pairs={{0,1},{1,0},{2,3},{3,2},{4,5},{5,4},{6,7},{7,6},{8,9},{9,8},{10,11... | collective-permute-start | bytes 196616 | tf_op jit(solution)/shard_map/ppermute | solution.py:371
  41.8 8.4 %collective-permute-start.10 = (bf16[2,64,128]{2,1,0:T(8,128)(2,1)S(1)}, bf16[2,64,128]{2,1,0:T(8,128)(2,1)S(1)}, u32[]{:S(2)}, u32[]{:S(2)}) collective-permute-start(bf16[2,64,128]{2,1,0:T(8,128)(2,1)S(1)} %add_convert_fusion), channel_id=1, source_target_pairs={{0,2},{1,3},{2,0},{3,1},{4,6},{5,7},{6,4},{7,5},{8,10},{9,11},{10,... | collective-permute-start | bytes 98312 | tf_op jit(solution)/shard_map/ppermute | solution.py:371
  44.5 5.8 %collective-permute-start.11 = (bf16[2,64,128]{2,1,0:T(8,128)(2,1)S(1)}, bf16[2,64,128]{2,1,0:T(8,128)(2,1)S(1)}, u32[]{:S(2)}, u32[]{:S(2)}) collective-permute-start(bf16[2,64,128]{2,1,0:T(8,128)(2,1)S(1)} %add_convert_fusion), channel_id=1, source_target_pairs={{0,3},{1,2},{2,1},{3,0},{4,7},{5,6},{6,5},{7,4},{8,11},{9,10},{10,... | collective-permute-start | bytes 98312 | tf_op jit(solution)/shard_map/ppermute | solution.py:371
  45.4 4.8 %collective-permute-start.12 = (bf16[2,64,128]{2,1,0:T(8,128)(2,1)S(1)}, bf16[2,64,128]{2,1,0:T(8,128)(2,1)S(1)}, u32[]{:S(2)}, u32[]{:S(2)}) collective-permute-start(bf16[2,64,128]{2,1,0:T(8,128)(2,1)S(1)} %add_convert_fusion), channel_id=1, source_target_pairs={{0,1},{1,0},{2,3},{3,2},{4,5},{5,4},{6,7},{7,6},{8,9},{9,8},{10,11... | collective-permute-start | bytes 98312 | tf_op jit(solution)/shard_map/ppermute | solution.py:371

commit v7 on v6

--- a/solution.py
+++ b/solution.py
@@ -14,6 +14,7 @@
 NEVER = -200.0
 MASKED = -1e30
 BOUND = 6.0 * 1.796875
+STEP = 1024.0
 META = 8
 STATES_VMEM, LOCAL_VMEM, GRADS_VMEM, OUTPUT_VMEM = 62, 60, 48, 60
 
@@ -261,7 +262,7 @@
                 row = across[s][h : h + 1]
                 if t != s:
                     row = row - row[:, BLOCK - 1 :]
-                weight = jnp.exp((down[t][:, h : h + 1] + bias[n]) - row)
+                weight = jnp.exp(jnp.minimum(down[t][:, h : h + 1] - row, 0.0) + bias[n])
                 weight = weight * step_blk[h : h + 1, s * BLOCK : (s + 1) * BLOCK]
                 term = weight * inner[n][e * BLOCK : (e + 1) * BLOCK]
                 totals[n] = term if e == 0 else totals[n] + term
@@ -395,9 +396,9 @@
     power = jnp.clip(jnp.ceil(jnp.log2(bound)), -100.0, 120.0)
     data = state * jnp.exp2(14.0 - power)[:, None]
     first = lax.reduce_precision(log_decay, 5, 10)
-    second = lax.reduce_precision(log_decay - first, 5, 10)
-    third = lax.reduce_precision(log_decay - first - second, 5, 10)
-    rows = [data.reshape(-1, LANES), first, second, third, power]
+    second = lax.reduce_precision(log_decay - first, 8, 10)
+    third = lax.reduce_precision(log_decay - first - second, 8, 10)
+    rows = [data.reshape(-1, LANES), first, second * STEP, third * STEP**2, power]
     return jnp.concatenate([v.astype(jnp.float16) for v in rows], 0)
 
 
@@ -405,7 +406,7 @@
     size = coded.shape[0] - 4 * chunks
     rows = [coded[size + k * chunks : size + (k + 1) * chunks].astype(F32) for k in range(4)]
     state = coded[:size].reshape(chunks, -1, LANES)
-    return state, jnp.exp2(rows[3] - 14.0), jnp.exp(rows[0] + rows[1] + rows[2])
+    return state, jnp.exp2(rows[3] - 14.0), jnp.exp(rows[0] + (rows[1] + rows[2] / STEP) / STEP)
 
 
 def chip_place(axis):

time: 51.3 us -> 51.3 us (level)
  no operation moved by 1% of the time
where the time goes in v7:
time: 51.3 us; the launch traced here: 50.9 us
  Pallas kernels  26.1 us (51%)
  starting transfers between devices  13.6 us (27%)
  waiting for transfers between devices  6.55 us (13%)
  other arithmetic  2.69 us (5%)
  local copies, waits for them, and re-layouts  1.06 us (2%)
  between operations  0.96 us (2%)
    ppermute x13, starting transfers between devices, swap_with(): return lax.ppermute(value, axis, [(i, i ^ mask) for i in range(size)])  13.6 us
    pallas_call x1, Pallas kernels, shards(): pl.pallas_call(functools.partial(local_kernel, group, width, masks), grid...  9.82 us
    pallas_call x2, Pallas kernels, finish(): pl.pallas_call(functools.partial(output_kernel, group, width, kind), grid...  9.1 us
    ppermute x13, waiting for transfers between devices, swap_with(): return lax.ppermute(value, axis, [(i, i ^ mask) for i in range(size)])  6.55 us
    pallas_call x1, Pallas kernels, shards(): pl.pallas_call(functools.partial(states_kernel, sgroup, width), grid=(sgr...  4.7 us
    pallas_call x1, Pallas kernels, shards(): pl.pallas_call(functools.partial(grads_kernel, ggroup, width, masks), gri...  2.44 us
    max x1, other arithmetic, shards(): jnp.maximum(mine, least)  1.32 us
  transfers between devices with their start and end apart: 13, of which 6 were waited for; matrix products, arithmetic and copies ran while one was open for 3% of the time, Pallas kernels for 37%

profile of v7, /device:TPU:0, one launch (start us, length us, event | category | flops | bytes accessed | tf_op | source)
XLA Modules:
  0.0 50.9 jit_solution(9508622619306885683)
XLA Ops:
  0.6 4.7 %states.1 = (f32[16,128,128]{2,1,0:T(8,128)}, f32[16,128,128]{2,1,0:T(8,128)}, f32[8,16,128]{2,1,0:T(8,128)}, bf16[256,128]{1,0:T(8,128)(2,1)}) custom-call(s32[1]{0:T(128)} %bitcast.core_ref, bf16[256,2048]{1,0:T(8,128)(2,1)} %x_ref.3, bf16[256,2048]{1,0:T(8,128)(2,1)} %g_ref.3, f32[32,256]{1,0:T(8,128)} %step_blk.1, f32[1,32]{1,0:T(1,128)} %bitcast.86, ...), custom_call_target="tpu_custom_call" | custom-call | tf_op jit(solution)/shard_map/states/pallas_call | solution.py:472
  5.4 0.5 %collective-permute-start.1 = (f32[16,128,128]{2,1,0:T(8,128)}, f32[16,128,128]{2,1,0:T(8,128)S(1)}, u32[]{:S(2)}, u32[]{:S(2)}) collective-permute-start(f32[16,128,128]{2,1,0:T(8,128)} %get-tuple-element.50), channel_id=1, source_target_pairs={{0,4},{4,0},{8,12},{12,8},{16,20},{20,16},{24,28},{28,24},{1,5},{5... | collective-permute-start | bytes 3145736 | tf_op jit(solution)/shard_map/ppermute | solution.py:372
  5.9 0.1 collective-permute-start
  6.0 1.3 %broadcast_maximum_fusion = f32[16,128,128]{2,1,0:T(8,128)S(1)} fusion(f32[16,128,128]{2,1,0:T(8,128)} %get-tuple-element.47), kind=kLoop, calls=%fused_computation.28 | loop fusion | flops 262144 | bytes 2097152 | tf_op jit(solution)/shard_map/max | solution.py:501
  7.3 1.1 %collective-permute-done = f32[8,16,128]{2,1,0:T(8,128)S(1)} collective-permute-done((f32[8,16,128]{2,1,0:T(8,128)}, f32[8,16,128]{2,1,0:T(8,128)S(1)}, u32[]{:S(2)}, u32[]{:S(2)}) %collective-permute-start) | collective-permute-done | bytes 65568 | tf_op jit(solution)/shard_map/ppermute | solution.py:372
  8.5 0.4 multiply_convert_fusion
  8.9 0.1 constant_dynamic-update-slice_fusion.9
  8.9 0.1 constant_dynamic-update-slice_fusion.4
  9.1 2.9 %collective-permute-start.2 = (f16[1088,128]{1,0:T(8,128)(2,1)S(1)}, f16[1088,128]{1,0:T(8,128)(2,1)S(1)}, u32[]{:S(2)}, u32[]{:S(2)}) collective-permute-start(f16[1088,128]{1,0:T(8,128)(2,1)S(1)} %get-tuple-element.51), channel_id=1, source_target_pairs={{0,8},{4,12},{8,0},{12,4},{16,24},{20,28},{24,16},{28,20},{1,9},{5... | collective-permute-start | bytes 835592 | tf_op jit(solution)/shard_map/ppermute | solution.py:372
  12.1 1.5 %collective-permute-start.3 = (f16[1088,128]{1,0:T(8,128)(2,1)S(1)}, f16[1088,128]{1,0:T(8,128)(2,1)S(1)}, u32[]{:S(2)}, u32[]{:S(2)}) collective-permute-start(f16[1088,128]{1,0:T(8,128)(2,1)S(1)} %get-tuple-element.52), channel_id=1, source_target_pairs={{0,16},{4,20},{8,24},{12,28},{16,0},{20,4},{24,8},{28,12},{1,17},{... | collective-permute-start | bytes 835592 | tf_op jit(solution)/shard_map/ppermute | solution.py:372
  13.6 9.8 %local.1 = (f32[256,2048]{1,0:T(8,128)}, f32[256,2048]{1,0:T(8,128)}, f32[4,2,64,128]{3,2,1,0:T(8,128)}) custom-call(f32[32]{0:T(128)} %skip_ref, s32[1]{0:T(128)} %bitcast.1.place_ref, bf16[256,2048]{1,0:T(8,128)(2,1)} %x_ref.3, bf16[256,2048]{1,0:T(8,128)(2,1)} %g_ref.3, f32[32,256]{1,0:T(8,128)} %step_blk.1, f32[32,256]{1,0:T(8,128)} %step_blk.1, ...), custom_call_target="tpu_custom_call" | custom-call | flops 2684354560 | bytes 6291456 | tf_op jit(solution)/shard_map/local/pallas_call | solution.py:536
  23.4 3.0 %collective-permute-done.3 = f16[1088,128]{1,0:T(8,128)(2,1)S(1)} collective-permute-done((f16[1088,128]{1,0:T(8,128)(2,1)S(1)}, f16[1088,128]{1,0:T(8,128)(2,1)S(1)}, u32[]{:S(2)}, u32[]{:S(2)}) %collective-permute-start.3) | collective-permute-done | bytes 278560 | tf_op jit(solution)/shard_map/ppermute | solution.py:372
  26.5 0.1 slice.132
  26.6 0.1 slice.137
  26.7 0.4 fusion.5
  27.1 0.1 collective-permute-start.5
  27.2 0.5 collective-permute-start.6
  27.7 0.4 fusion.11
  28.1 1.0 %collective-permute-done.5.other_f.other = f32[16,64,128]{2,1,0:T(8,128)S(1)} collective-permute-done((f32[16,64,128]{2,1,0:T(8,128)S(1)}, f32[16,64,128]{2,1,0:T(8,128)S(1)}, u32[]{:S(2)}, u32[]{:S(2)}) %collective-permute-start.5) | collective-permute-done | bytes 524320 | tf_op jit(solution)/shard_map/ppermute | solution.py:372
  29.1 0.7 %collective-permute-done.6.other_b.other = f32[16,64,128]{2,1,0:T(8,128)S(1)} collective-permute-done((f32[16,64,128]{2,1,0:T(8,128)S(1)}, f32[16,64,128]{2,1,0:T(8,128)S(1)}, u32[]{:S(2)}, u32[]{:S(2)}) %collective-permute-start.6) | collective-permute-done | bytes 524320 | tf_op jit(solution)/shard_map/ppermute | solution.py:372
  29.9 2.4 %grads.1 = f32[4,2,64,128]{3,2,1,0:T(8,128)S(1)} custom-call(s32[1]{0:T(128)} %bitcast.core_ref, s32[1]{0:T(128)} %bitcast.1.place_ref, f32[16,64,128]{2,1,0:T(8,128)S(1)} %get-tuple-element.104.own_f.own, f32[16,64,128]{2,1,0:T(8,128)S(1)} %collective-permute-done.5.other_f.other, f32[16,64,128]{2,1,0:T(8,128)S(1)} %get-tuple-element.103.own_b.own, ...), custom_call_target="tpu_custom_call" | custom-call | tf_op jit(solution)/shard_map/grads/pallas_call | solution.py:603
  32.4 2.7 %collective-permute-start.7 = (f32[2,64,128]{2,1,0:T(8,128)S(1)}, f32[2,64,128]{2,1,0:T(8,128)S(1)}, u32[]{:S(2)}, u32[]{:S(2)}) collective-permute-start(f32[2,64,128]{2,1,0:T(8,128)S(1)} %get-tuple-element.71), channel_id=1, source_target_pairs={{0,2},{1,3},{2,0},{3,1},{4,6},{5,7},{6,4},{7,5},{8,10},{9,11},{10,... | collective-permute-start | bytes 196616 | tf_op jit(solution)/shard_map/ppermute | solution.py:372
  35.1 1.3 %collective-permute-start.8 = (f32[2,64,128]{2,1,0:T(8,128)S(1)}, f32[2,64,128]{2,1,0:T(8,128)S(1)}, u32[]{:S(2)}, u32[]{:S(2)}) collective-permute-start(f32[2,64,128]{2,1,0:T(8,128)S(1)} %get-tuple-element.72), channel_id=1, source_target_pairs={{0,3},{1,2},{2,1},{3,0},{4,7},{5,6},{6,5},{7,4},{8,11},{9,10},{10,... | collective-permute-start | bytes 196616 | tf_op jit(solution)/shard_map/ppermute | solution.py:372
  36.4 0.2 collective-permute-start.9
  36.6 4.5 %mixed.1 = bf16[256,2048]{1,0:T(8,128)(2,1)} custom-call(s32[1]{0:T(128)} %bitcast.core_ref, f32[16,64,128]{2,1,0:T(8,128)} %copy-done.1, f32[16,64,128]{2,1,0:T(8,128)} %copy-done.5, f32[256,2048]{1,0:T(8,128)} %get-tuple-element.75.base_ref, bf16[256,128]{1,0:T(8,128)(2,1)} %get-tuple-element.69.edges_ref, bf16[256,128]{1,0:T(8,128)(2,1)} %proj_ref.2), custom_call_target="tpu_custom_call" | custom-call | flops 268435456 | bytes 4194304 | tf_op jit(solution)/shard_map/mixed/pallas_call | solution.py:623
  41.2 0.3 collective-permute-done.8
  41.5 0.3 collective-permute-done.9
  41.8 2.6 %collective-permute-start.10 = (bf16[2,64,128]{2,1,0:T(8,128)(2,1)S(1)}, bf16[2,64,128]{2,1,0:T(8,128)(2,1)S(1)}, u32[]{:S(2)}, u32[]{:S(2)}) collective-permute-start(bf16[2,64,128]{2,1,0:T(8,128)(2,1)S(1)} %add_convert_fusion), channel_id=1, source_target_pairs={{0,2},{1,3},{2,0},{3,1},{4,6},{5,7},{6,4},{7,5},{8,10},{9,11},{10,... | collective-permute-start | bytes 98312 | tf_op jit(solution)/shard_map/ppermute | solution.py:372
  44.4 1.0 %collective-permute-start.11 = (bf16[2,64,128]{2,1,0:T(8,128)(2,1)S(1)}, bf16[2,64,128]{2,1,0:T(8,128)(2,1)S(1)}, u32[]{:S(2)}, u32[]{:S(2)}) collective-permute-start(bf16[2,64,128]{2,1,0:T(8,128)(2,1)S(1)} %add_convert_fusion), channel_id=1, source_target_pairs={{0,3},{1,2},{2,1},{3,0},{4,7},{5,6},{6,5},{7,4},{8,11},{9,10},{10,... | collective-permute-start | bytes 98312 | tf_op jit(solution)/shard_map/ppermute | solution.py:372
  45.5 0.1 collective-permute-start.12
  45.6 4.6 %grad_inputs.1 = bf16[256,2048]{1,0:T(8,128)(2,1)} custom-call(s32[1]{0:T(128)} %bitcast.core_ref, f32[16,64,128]{2,1,0:T(8,128)} %copy-done, f32[16,64,128]{2,1,0:T(8,128)} %copy-done.4, f32[256,2048]{1,0:T(8,128)} %get-tuple-element.83.base_ref, bf16[256,128]{1,0:T(8,128)(2,1)} %get-tuple-element.69.edges_ref, bf16[256,128]{1,0:T(8,128)(2,1)} %proj_ref.3), custom_call_target="tpu_custom_call" | custom-call | flops 268435456 | bytes 4194304 | tf_op jit(solution)/shard_map/grad_inputs/pallas_call | solution.py:623
  50.3 0.7 %fusion.37 = (bf16[4,1,64,128]{3,2,0,1:T(8,128)(2,1)}, bf16[4,1,64,128]{3,2,0,1:T(8,128)(2,1)}) fusion(bf16[4,2,64,128]{3,2,0,1:T(8,128)(2,1)S(1)} %bitcast_dynamic-update-slice_fusion), kind=kLoop, calls=%fused_computation.100 | loop fusion | bytes 262144 | tf_op jit(solution)/shard_map/slice | solution.py:659
  (44 shorter events, 0.5 us)
Async XLA Ops:
  5.3 1.9 %copy-start.8 = (f32[8,16,128]{2,1,0:T(8,128)S(1)}, f32[8,16,128]{2,1,0:T(8,128)}, u32[]{:S(2)}) copy-start(f32[8,16,128]{2,1,0:T(8,128)} %get-tuple-element.46) | copy-start | bytes 196612
  5.4 3.2 %collective-permute-start.1 = (f32[16,128,128]{2,1,0:T(8,128)}, f32[16,128,128]{2,1,0:T(8,128)S(1)}, u32[]{:S(2)}, u32[]{:S(2)}) collective-permute-start(f32[16,128,128]{2,1,0:T(8,128)} %get-tuple-element.50), channel_id=1, source_target_pairs={{0,4},{4,0},{8,12},{12,8},{16,20},{20,16},{24,28},{28,24},{1,5},{5... | collective-permute-start | bytes 3145736 | tf_op jit(solution)/shard_map/ppermute | solution.py:372
  5.9 2.6 %collective-permute-start = (f32[8,16,128]{2,1,0:T(8,128)}, f32[8,16,128]{2,1,0:T(8,128)S(1)}, u32[]{:S(2)}, u32[]{:S(2)}) collective-permute-start(f32[8,16,128]{2,1,0:T(8,128)} %get-tuple-element.46), channel_id=1, source_target_pairs={{0,4},{4,0},{8,12},{12,8},{16,20},{20,16},{24,28},{28,24},{1,5},{5... | collective-permute-start | bytes 196616 | tf_op jit(solution)/shard_map/ppermute | solution.py:372
  9.1 14.3 %collective-permute-start.2 = (f16[1088,128]{1,0:T(8,128)(2,1)S(1)}, f16[1088,128]{1,0:T(8,128)(2,1)S(1)}, u32[]{:S(2)}, u32[]{:S(2)}) collective-permute-start(f16[1088,128]{1,0:T(8,128)(2,1)S(1)} %get-tuple-element.51), channel_id=1, source_target_pairs={{0,8},{4,12},{8,0},{12,4},{16,24},{20,28},{24,16},{28,20},{1,9},{5... | collective-permute-start | bytes 835592 | tf_op jit(solution)/shard_map/ppermute | solution.py:372
  12.1 14.4 %collective-permute-start.3 = (f16[1088,128]{1,0:T(8,128)(2,1)S(1)}, f16[1088,128]{1,0:T(8,128)(2,1)S(1)}, u32[]{:S(2)}, u32[]{:S(2)}) collective-permute-start(f16[1088,128]{1,0:T(8,128)(2,1)S(1)} %get-tuple-element.52), channel_id=1, source_target_pairs={{0,16},{4,20},{8,24},{12,28},{16,0},{20,4},{24,8},{28,12},{1,17},{... | collective-permute-start | bytes 835592 | tf_op jit(solution)/shard_map/ppermute | solution.py:372
  13.6 12.9 %collective-permute-start.4 = (f16[1088,128]{1,0:T(8,128)(2,1)S(1)}, f16[1088,128]{1,0:T(8,128)(2,1)S(1)}, u32[]{:S(2)}, u32[]{:S(2)}) collective-permute-start(f16[1088,128]{1,0:T(8,128)(2,1)S(1)} %get-tuple-element.52), channel_id=1, source_target_pairs={{0,24},{4,28},{8,16},{12,20},{16,8},{20,12},{24,0},{28,4},{1,25},{... | collective-permute-start | bytes 835592 | tf_op jit(solution)/shard_map/ppermute | solution.py:372
  27.1 2.8 %copy-start.2 = (bf16[256,2048]{1,0:T(8,128)(2,1)S(1)}, bf16[256,2048]{1,0:T(8,128)(2,1)}, u32[]{:S(2)}) copy-start(bf16[256,2048]{1,0:T(8,128)(2,1)} %x_ref.3) | copy-start | bytes 3145732
  27.1 2.8 %copy-start.3 = (bf16[256,2048]{1,0:T(8,128)(2,1)S(1)}, bf16[256,2048]{1,0:T(8,128)(2,1)}, u32[]{:S(2)}) copy-start(bf16[256,2048]{1,0:T(8,128)(2,1)} %g_ref.3) | copy-start | bytes 3145732
  27.1 2.7 %copy-start.6 = (bf16[256,128]{1,0:T(8,128)(2,1)S(1)}, bf16[256,128]{1,0:T(8,128)(2,1)}, u32[]{:S(2)}) copy-start(bf16[256,128]{1,0:T(8,128)(2,1)} %get-tuple-element.69.edges_ref) | copy-start | bytes 196612
  27.1 2.0 %collective-permute-start.5 = (f32[16,64,128]{2,1,0:T(8,128)S(1)}, f32[16,64,128]{2,1,0:T(8,128)S(1)}, u32[]{:S(2)}, u32[]{:S(2)}) collective-permute-start(f32[16,64,128]{2,1,0:T(8,128)S(1)} %get-tuple-element.64), channel_id=1, source_target_pairs={{0,4},{4,0},{8,12},{12,8},{16,20},{20,16},{24,28},{28,24},{1,5},{5... | collective-permute-start | bytes 1572872 | tf_op jit(solution)/shard_map/ppermute | solution.py:372
  27.2 2.6 %collective-permute-start.6 = (f32[16,64,128]{2,1,0:T(8,128)S(1)}, f32[16,64,128]{2,1,0:T(8,128)S(1)}, u32[]{:S(2)}, u32[]{:S(2)}) collective-permute-start(f32[16,64,128]{2,1,0:T(8,128)S(1)} %get-tuple-element.68), channel_id=1, source_target_pairs={{0,4},{4,0},{8,12},{12,8},{16,20},{20,16},{24,28},{28,24},{1,5},{5... | collective-permute-start | bytes 1572872 | tf_op jit(solution)/shard_map/ppermute | solution.py:372
  28.1 4.3 %copy-start = (f32[16,64,128]{2,1,0:T(8,128)}, f32[16,64,128]{2,1,0:T(8,128)S(1)}, u32[]{:S(2)}) copy-start(f32[16,64,128]{2,1,0:T(8,128)S(1)} %get-tuple-element.103.own_b.own) | copy-start | bytes 1572868
  28.1 4.3 %copy-start.1 = (f32[16,64,128]{2,1,0:T(8,128)}, f32[16,64,128]{2,1,0:T(8,128)S(1)}, u32[]{:S(2)}) copy-start(f32[16,64,128]{2,1,0:T(8,128)S(1)} %get-tuple-element.104.own_f.own) | copy-start | bytes 1572868
  29.1 3.2 %copy-start.5 = (f32[16,64,128]{2,1,0:T(8,128)}, f32[16,64,128]{2,1,0:T(8,128)S(1)}, u32[]{:S(2)}) copy-start(f32[16,64,128]{2,1,0:T(8,128)S(1)} %collective-permute-done.5.other_f.other) | copy-start | bytes 1572868
  29.8 2.5 %copy-start.4 = (f32[16,64,128]{2,1,0:T(8,128)}, f32[16,64,128]{2,1,0:T(8,128)S(1)}, u32[]{:S(2)}) copy-start(f32[16,64,128]{2,1,0:T(8,128)S(1)} %collective-permute-done.6.other_b.other) | copy-start | bytes 1572868
  29.9 2.5 %copy-start.7 = (f32[4,2,64,128]{3,2,1,0:T(8,128)S(1)}, f32[4,2,64,128]{3,2,1,0:T(8,128)}, u32[]{:S(2)}) copy-start(f32[4,2,64,128]{3,2,1,0:T(8,128)} %get-tuple-element.70) | copy-start | bytes 786436
  32.4 8.8 %collective-permute-start.7 = (f32[2,64,128]{2,1,0:T(8,128)S(1)}, f32[2,64,128]{2,1,0:T(8,128)S(1)}, u32[]{:S(2)}, u32[]{:S(2)}) collective-permute-start(f32[2,64,128]{2,1,0:T(8,128)S(1)} %get-tuple-element.71), channel_id=1, source_target_pairs={{0,2},{1,3},{2,0},{3,1},{4,6},{5,7},{6,4},{7,5},{8,10},{9,11},{10,... | collective-permute-start | bytes 196616 | tf_op jit(solution)/shard_map/ppermute | solution.py:372
  35.1 6.4 %collective-permute-start.8 = (f32[2,64,128]{2,1,0:T(8,128)S(1)}, f32[2,64,128]{2,1,0:T(8,128)S(1)}, u32[]{:S(2)}, u32[]{:S(2)}) collective-permute-start(f32[2,64,128]{2,1,0:T(8,128)S(1)} %get-tuple-element.72), channel_id=1, source_target_pairs={{0,3},{1,2},{2,1},{3,0},{4,7},{5,6},{6,5},{7,4},{8,11},{9,10},{10,... | collective-permute-start | bytes 196616 | tf_op jit(solution)/shard_map/ppermute | solution.py:372
  36.4 5.4 %collective-permute-start.9 = (f32[2,64,128]{2,1,0:T(8,128)S(1)}, f32[2,64,128]{2,1,0:T(8,128)S(1)}, u32[]{:S(2)}, u32[]{:S(2)}) collective-permute-start(f32[2,64,128]{2,1,0:T(8,128)S(1)} %get-tuple-element.73), channel_id=1, source_target_pairs={{0,1},{1,0},{2,3},{3,2},{4,5},{5,4},{6,7},{7,6},{8,9},{9,8},{10,11... | collective-permute-start | bytes 196616 | tf_op jit(solution)/shard_map/ppermute | solution.py:372
  41.8 8.4 %collective-permute-start.10 = (bf16[2,64,128]{2,1,0:T(8,128)(2,1)S(1)}, bf16[2,64,128]{2,1,0:T(8,128)(2,1)S(1)}, u32[]{:S(2)}, u32[]{:S(2)}) collective-permute-start(bf16[2,64,128]{2,1,0:T(8,128)(2,1)S(1)} %add_convert_fusion), channel_id=1, source_target_pairs={{0,2},{1,3},{2,0},{3,1},{4,6},{5,7},{6,4},{7,5},{8,10},{9,11},{10,... | collective-permute-start | bytes 98312 | tf_op jit(solution)/shard_map/ppermute | solution.py:372
  44.4 5.8 %collective-permute-start.11 = (bf16[2,64,128]{2,1,0:T(8,128)(2,1)S(1)}, bf16[2,64,128]{2,1,0:T(8,128)(2,1)S(1)}, u32[]{:S(2)}, u32[]{:S(2)}) collective-permute-start(bf16[2,64,128]{2,1,0:T(8,128)(2,1)S(1)} %add_convert_fusion), channel_id=1, source_target_pairs={{0,3},{1,2},{2,1},{3,0},{4,7},{5,6},{6,5},{7,4},{8,11},{9,10},{10,... | collective-permute-start | bytes 98312 | tf_op jit(solution)/shard_map/ppermute | solution.py:372
  45.5 4.8 %collective-permute-start.12 = (bf16[2,64,128]{2,1,0:T(8,128)(2,1)S(1)}, bf16[2,64,128]{2,1,0:T(8,128)(2,1)S(1)}, u32[]{:S(2)}, u32[]{:S(2)}) collective-permute-start(bf16[2,64,128]{2,1,0:T(8,128)(2,1)S(1)} %add_convert_fusion), channel_id=1, source_target_pairs={{0,1},{1,0},{2,3},{3,2},{4,5},{5,4},{6,7},{7,6},{8,9},{9,8},{10,11... | collective-permute-start | bytes 98312 | tf_op jit(solution)/shard_map/ppermute | solution.py:372

commit v8 on v7

--- a/solution.py
+++ b/solution.py
@@ -397,16 +397,15 @@
     data = state * jnp.exp2(14.0 - power)[:, None]
     first = lax.reduce_precision(log_decay, 5, 10)
     second = lax.reduce_precision(log_decay - first, 8, 10)
-    third = lax.reduce_precision(log_decay - first - second, 8, 10)
-    rows = [data.reshape(-1, LANES), first, second * STEP, third * STEP**2, power]
+    rows = [data.reshape(-1, LANES), first, second * STEP, power]
     return jnp.concatenate([v.astype(jnp.float16) for v in rows], 0)
 
 
 def decode(coded, chunks):
-    size = coded.shape[0] - 4 * chunks
-    rows = [coded[size + k * chunks : size + (k + 1) * chunks].astype(F32) for k in range(4)]
+    size = coded.shape[0] - 3 * chunks
+    rows = [coded[size + k * chunks : size + (k + 1) * chunks].astype(F32) for k in range(3)]
     state = coded[:size].reshape(chunks, -1, LANES)
-    return state, jnp.exp2(rows[3] - 14.0), jnp.exp(rows[0] + (rows[1] + rows[2] / STEP) / STEP)
+    return state, jnp.exp2(rows[2] - 14.0), jnp.exp(rows[0] + rows[1] / STEP)
 
 
 def chip_place(axis):

time: 51.3 us -> 51.1 us (level)
  no operation moved by 1% of the time
where the time goes in v8:
time: 51.1 us; the launch traced here: 50.7 us
  Pallas kernels  26.1 us (51%)
  starting transfers between devices  13.6 us (27%)
  waiting for transfers between devices  6.37 us (12%)
  other arithmetic  2.77 us (5%)
  local copies, waits for them, and re-layouts  0.96 us (2%)
  between operations  0.93 us (2%)
    ppermute x13, starting transfers between devices, swap_with(): return lax.ppermute(value, axis, [(i, i ^ mask) for i in range(size)])  13.6 us
    pallas_call x1, Pallas kernels, shards(): pl.pallas_call(functools.partial(local_kernel, group, width, masks), grid...  9.84 us
    pallas_call x2, Pallas kernels, finish(): pl.pallas_call(functools.partial(output_kernel, group, width, kind), grid...  9.09 us
    ppermute x13, waiting for transfers between devices, swap_with(): return lax.ppermute(value, axis, [(i, i ^ mask) for i in range(size)])  6.37 us
    pallas_call x1, Pallas kernels, shards(): pl.pallas_call(functools.partial(states_kernel, sgroup, width), grid=(sgr...  4.7 us
    pallas_call x1, Pallas kernels, shards(): pl.pallas_call(functools.partial(grads_kernel, ggroup, width, masks), gri...  2.44 us
    max x1, other arithmetic, shards(): jnp.maximum(mine, least)  1.32 us
  transfers between devices with their start and end apart: 13, of which 6 were waited for; matrix products, arithmetic and copies ran while one was open for 3% of the time, Pallas kernels for 37%

profile of v8, /device:TPU:0, one launch (start us, length us, event | category | flops | bytes accessed | tf_op | source)
XLA Modules:
  0.0 50.7 jit_solution(4364516933568741587)
XLA Ops:
  0.6 4.7 %states.1 = (f32[16,128,128]{2,1,0:T(8,128)}, f32[16,128,128]{2,1,0:T(8,128)}, f32[8,16,128]{2,1,0:T(8,128)}, bf16[256,128]{1,0:T(8,128)(2,1)}) custom-call(s32[1]{0:T(128)} %bitcast.core_ref, bf16[256,2048]{1,0:T(8,128)(2,1)} %x_ref.3, bf16[256,2048]{1,0:T(8,128)(2,1)} %g_ref.3, f32[32,256]{1,0:T(8,128)} %step_blk.1, f32[1,32]{1,0:T(1,128)} %bitcast.89, ...), custom_call_target="tpu_custom_call" | custom-call | tf_op jit(solution)/shard_map/states/pallas_call | solution.py:471
  5.4 0.5 %collective-permute-start.1 = (f32[16,128,128]{2,1,0:T(8,128)}, f32[16,128,128]{2,1,0:T(8,128)S(1)}, u32[]{:S(2)}, u32[]{:S(2)}) collective-permute-start(f32[16,128,128]{2,1,0:T(8,128)} %get-tuple-element.50), channel_id=1, source_target_pairs={{0,4},{4,0},{8,12},{12,8},{16,20},{20,16},{24,28},{28,24},{1,5},{5... | collective-permute-start | bytes 3145736 | tf_op jit(solution)/shard_map/ppermute | solution.py:372
  5.9 0.1 collective-permute-start
  6.0 1.3 %broadcast_maximum_fusion = f32[16,128,128]{2,1,0:T(8,128)S(1)} fusion(f32[16,128,128]{2,1,0:T(8,128)} %get-tuple-element.47), kind=kLoop, calls=%fused_computation.28 | loop fusion | flops 262144 | bytes 2097152 | tf_op jit(solution)/shard_map/max | solution.py:500
  7.3 1.1 %collective-permute-done = f32[8,16,128]{2,1,0:T(8,128)S(1)} collective-permute-done((f32[8,16,128]{2,1,0:T(8,128)}, f32[8,16,128]{2,1,0:T(8,128)S(1)}, u32[]{:S(2)}, u32[]{:S(2)}) %collective-permute-start) | collective-permute-done | bytes 65568 | tf_op jit(solution)/shard_map/ppermute | solution.py:372
  8.5 0.4 multiply_convert_fusion
  8.9 0.2 fusion.13
  9.1 2.9 %collective-permute-start.2 = (f16[1072,128]{1,0:T(8,128)(2,1)S(1)}, f16[1072,128]{1,0:T(8,128)(2,1)S(1)}, u32[]{:S(2)}, u32[]{:S(2)}) collective-permute-start(f16[1072,128]{1,0:T(8,128)(2,1)S(1)} %get-tuple-element.51), channel_id=1, source_target_pairs={{0,8},{4,12},{8,0},{12,4},{16,24},{20,28},{24,16},{28,20},{1,9},{5... | collective-permute-start | bytes 823304 | tf_op jit(solution)/shard_map/ppermute | solution.py:372
  12.0 1.5 %collective-permute-start.3 = (f16[1072,128]{1,0:T(8,128)(2,1)S(1)}, f16[1072,128]{1,0:T(8,128)(2,1)S(1)}, u32[]{:S(2)}, u32[]{:S(2)}) collective-permute-start(f16[1072,128]{1,0:T(8,128)(2,1)S(1)} %get-tuple-element.52), channel_id=1, source_target_pairs={{0,16},{4,20},{8,24},{12,28},{16,0},{20,4},{24,8},{28,12},{1,17},{... | collective-permute-start | bytes 823304 | tf_op jit(solution)/shard_map/ppermute | solution.py:372
  13.6 9.8 %local.1 = (f32[256,2048]{1,0:T(8,128)}, f32[256,2048]{1,0:T(8,128)}, f32[4,2,64,128]{3,2,1,0:T(8,128)}) custom-call(f32[32]{0:T(128)} %skip_ref, s32[1]{0:T(128)} %bitcast.1.place_ref, bf16[256,2048]{1,0:T(8,128)(2,1)} %x_ref.3, bf16[256,2048]{1,0:T(8,128)(2,1)} %g_ref.3, f32[32,256]{1,0:T(8,128)} %step_blk.1, f32[32,256]{1,0:T(8,128)} %step_blk.1, ...), custom_call_target="tpu_custom_call" | custom-call | flops 2684354560 | bytes 6291456 | tf_op jit(solution)/shard_map/local/pallas_call | solution.py:535
  23.4 2.8 %collective-permute-done.3 = f16[1072,128]{1,0:T(8,128)(2,1)S(1)} collective-permute-done((f16[1072,128]{1,0:T(8,128)(2,1)S(1)}, f16[1072,128]{1,0:T(8,128)(2,1)S(1)}, u32[]{:S(2)}, u32[]{:S(2)}) %collective-permute-start.3) | collective-permute-done | bytes 274464 | tf_op jit(solution)/shard_map/ppermute | solution.py:372
  26.3 0.1 slice.115
  26.3 0.1 slice.121
  26.4 0.1 slice.125
  26.5 0.4 fusion.5
  26.9 0.1 collective-permute-start.5
  27.0 0.5 collective-permute-start.6
  27.5 0.4 fusion.11
  27.9 1.0 %collective-permute-done.5.other_f.other = f32[16,64,128]{2,1,0:T(8,128)S(1)} collective-permute-done((f32[16,64,128]{2,1,0:T(8,128)S(1)}, f32[16,64,128]{2,1,0:T(8,128)S(1)}, u32[]{:S(2)}, u32[]{:S(2)}) %collective-permute-start.5) | collective-permute-done | bytes 524320 | tf_op jit(solution)/shard_map/ppermute | solution.py:372
  28.9 0.7 %collective-permute-done.6.other_b.other = f32[16,64,128]{2,1,0:T(8,128)S(1)} collective-permute-done((f32[16,64,128]{2,1,0:T(8,128)S(1)}, f32[16,64,128]{2,1,0:T(8,128)S(1)}, u32[]{:S(2)}, u32[]{:S(2)}) %collective-permute-start.6) | collective-permute-done | bytes 524320 | tf_op jit(solution)/shard_map/ppermute | solution.py:372
  29.7 2.4 %grads.1 = f32[4,2,64,128]{3,2,1,0:T(8,128)S(1)} custom-call(s32[1]{0:T(128)} %bitcast.core_ref, s32[1]{0:T(128)} %bitcast.1.place_ref, f32[16,64,128]{2,1,0:T(8,128)S(1)} %get-tuple-element.102.own_f.own, f32[16,64,128]{2,1,0:T(8,128)S(1)} %collective-permute-done.5.other_f.other, f32[16,64,128]{2,1,0:T(8,128)S(1)} %get-tuple-element.101.own_b.own, ...), custom_call_target="tpu_custom_call" | custom-call | tf_op jit(solution)/shard_map/grads/pallas_call | solution.py:602
  32.2 2.7 %collective-permute-start.7 = (f32[2,64,128]{2,1,0:T(8,128)S(1)}, f32[2,64,128]{2,1,0:T(8,128)S(1)}, u32[]{:S(2)}, u32[]{:S(2)}) collective-permute-start(f32[2,64,128]{2,1,0:T(8,128)S(1)} %get-tuple-element.71), channel_id=1, source_target_pairs={{0,2},{1,3},{2,0},{3,1},{4,6},{5,7},{6,4},{7,5},{8,10},{9,11},{10,... | collective-permute-start | bytes 196616 | tf_op jit(solution)/shard_map/ppermute | solution.py:372
  34.9 1.3 %collective-permute-start.8 = (f32[2,64,128]{2,1,0:T(8,128)S(1)}, f32[2,64,128]{2,1,0:T(8,128)S(1)}, u32[]{:S(2)}, u32[]{:S(2)}) collective-permute-start(f32[2,64,128]{2,1,0:T(8,128)S(1)} %get-tuple-element.72), channel_id=1, source_target_pairs={{0,3},{1,2},{2,1},{3,0},{4,7},{5,6},{6,5},{7,4},{8,11},{9,10},{10,... | collective-permute-start | bytes 196616 | tf_op jit(solution)/shard_map/ppermute | solution.py:372
  36.2 0.2 collective-permute-start.9
  36.4 4.5 %mixed.1 = bf16[256,2048]{1,0:T(8,128)(2,1)} custom-call(s32[1]{0:T(128)} %bitcast.core_ref, f32[16,64,128]{2,1,0:T(8,128)} %copy-done.1, f32[16,64,128]{2,1,0:T(8,128)} %copy-done.5, f32[256,2048]{1,0:T(8,128)} %get-tuple-element.75.base_ref, bf16[256,128]{1,0:T(8,128)(2,1)} %get-tuple-element.69.edges_ref, bf16[256,128]{1,0:T(8,128)(2,1)} %proj_ref.2), custom_call_target="tpu_custom_call" | custom-call | flops 268435456 | bytes 4194304 | tf_op jit(solution)/shard_map/mixed/pallas_call | solution.py:622
  41.0 0.3 collective-permute-done.8
  41.3 0.3 collective-permute-done.9
  41.6 2.6 %collective-permute-start.10 = (bf16[2,64,128]{2,1,0:T(8,128)(2,1)S(1)}, bf16[2,64,128]{2,1,0:T(8,128)(2,1)S(1)}, u32[]{:S(2)}, u32[]{:S(2)}) collective-permute-start(bf16[2,64,128]{2,1,0:T(8,128)(2,1)S(1)} %add_convert_fusion), channel_id=1, source_target_pairs={{0,2},{1,3},{2,0},{3,1},{4,6},{5,7},{6,4},{7,5},{8,10},{9,11},{10,... | collective-permute-start | bytes 98312 | tf_op jit(solution)/shard_map/ppermute | solution.py:372
  44.2 1.0 %collective-permute-start.11 = (bf16[2,64,128]{2,1,0:T(8,128)(2,1)S(1)}, bf16[2,64,128]{2,1,0:T(8,128)(2,1)S(1)}, u32[]{:S(2)}, u32[]{:S(2)}) collective-permute-start(bf16[2,64,128]{2,1,0:T(8,128)(2,1)S(1)} %add_convert_fusion), channel_id=1, source_target_pairs={{0,3},{1,2},{2,1},{3,0},{4,7},{5,6},{6,5},{7,4},{8,11},{9,10},{10,... | collective-permute-start | bytes 98312 | tf_op jit(solution)/shard_map/ppermute | solution.py:372
  45.2 0.2 collective-permute-start.12
  45.4 4.6 %grad_inputs.1 = bf16[256,2048]{1,0:T(8,128)(2,1)} custom-call(s32[1]{0:T(128)} %bitcast.core_ref, f32[16,64,128]{2,1,0:T(8,128)} %copy-done, f32[16,64,128]{2,1,0:T(8,128)} %copy-done.4, f32[256,2048]{1,0:T(8,128)} %get-tuple-element.83.base_ref, bf16[256,128]{1,0:T(8,128)(2,1)} %get-tuple-element.69.edges_ref, bf16[256,128]{1,0:T(8,128)(2,1)} %proj_ref.3), custom_call_target="tpu_custom_call" | custom-call | flops 268435456 | bytes 4194304 | tf_op jit(solution)/shard_map/grad_inputs/pallas_call | solution.py:622
  50.1 0.7 %fusion.39 = (bf16[4,1,64,128]{3,2,0,1:T(8,128)(2,1)}, bf16[4,1,64,128]{3,2,0,1:T(8,128)(2,1)}) fusion(bf16[4,2,64,128]{3,2,0,1:T(8,128)(2,1)S(1)} %bitcast_dynamic-update-slice_fusion), kind=kLoop, calls=%fused_computation.95 | loop fusion | bytes 262144 | tf_op jit(solution)/shard_map/slice | solution.py:658
  (38 shorter events, 0.3 us)
Async XLA Ops:
  5.3 1.9 %copy-start.8 = (f32[8,16,128]{2,1,0:T(8,128)S(1)}, f32[8,16,128]{2,1,0:T(8,128)}, u32[]{:S(2)}) copy-start(f32[8,16,128]{2,1,0:T(8,128)} %get-tuple-element.46) | copy-start | bytes 196612
  5.4 3.2 %collective-permute-start.1 = (f32[16,128,128]{2,1,0:T(8,128)}, f32[16,128,128]{2,1,0:T(8,128)S(1)}, u32[]{:S(2)}, u32[]{:S(2)}) collective-permute-start(f32[16,128,128]{2,1,0:T(8,128)} %get-tuple-element.50), channel_id=1, source_target_pairs={{0,4},{4,0},{8,12},{12,8},{16,20},{20,16},{24,28},{28,24},{1,5},{5... | collective-permute-start | bytes 3145736 | tf_op jit(solution)/shard_map/ppermute | solution.py:372
  5.9 2.6 %collective-permute-start = (f32[8,16,128]{2,1,0:T(8,128)}, f32[8,16,128]{2,1,0:T(8,128)S(1)}, u32[]{:S(2)}, u32[]{:S(2)}) collective-permute-start(f32[8,16,128]{2,1,0:T(8,128)} %get-tuple-element.46), channel_id=1, source_target_pairs={{0,4},{4,0},{8,12},{12,8},{16,20},{20,16},{24,28},{28,24},{1,5},{5... | collective-permute-start | bytes 196616 | tf_op jit(solution)/shard_map/ppermute | solution.py:372
  9.1 14.3 %collective-permute-start.2 = (f16[1072,128]{1,0:T(8,128)(2,1)S(1)}, f16[1072,128]{1,0:T(8,128)(2,1)S(1)}, u32[]{:S(2)}, u32[]{:S(2)}) collective-permute-start(f16[1072,128]{1,0:T(8,128)(2,1)S(1)} %get-tuple-element.51), channel_id=1, source_target_pairs={{0,8},{4,12},{8,0},{12,4},{16,24},{20,28},{24,16},{28,20},{1,9},{5... | collective-permute-start | bytes 823304 | tf_op jit(solution)/shard_map/ppermute | solution.py:372
  12.0 14.2 %collective-permute-start.3 = (f16[1072,128]{1,0:T(8,128)(2,1)S(1)}, f16[1072,128]{1,0:T(8,128)(2,1)S(1)}, u32[]{:S(2)}, u32[]{:S(2)}) collective-permute-start(f16[1072,128]{1,0:T(8,128)(2,1)S(1)} %get-tuple-element.52), channel_id=1, source_target_pairs={{0,16},{4,20},{8,24},{12,28},{16,0},{20,4},{24,8},{28,12},{1,17},{... | collective-permute-start | bytes 823304 | tf_op jit(solution)/shard_map/ppermute | solution.py:372
  13.6 12.7 %collective-permute-start.4 = (f16[1072,128]{1,0:T(8,128)(2,1)S(1)}, f16[1072,128]{1,0:T(8,128)(2,1)S(1)}, u32[]{:S(2)}, u32[]{:S(2)}) collective-permute-start(f16[1072,128]{1,0:T(8,128)(2,1)S(1)} %get-tuple-element.52), channel_id=1, source_target_pairs={{0,24},{4,28},{8,16},{12,20},{16,8},{20,12},{24,0},{28,4},{1,25},{... | collective-permute-start | bytes 823304 | tf_op jit(solution)/shard_map/ppermute | solution.py:372
  26.9 2.8 %copy-start.2 = (bf16[256,2048]{1,0:T(8,128)(2,1)S(1)}, bf16[256,2048]{1,0:T(8,128)(2,1)}, u32[]{:S(2)}) copy-start(bf16[256,2048]{1,0:T(8,128)(2,1)} %x_ref.3) | copy-start | bytes 3145732
  26.9 2.8 %copy-start.3 = (bf16[256,2048]{1,0:T(8,128)(2,1)S(1)}, bf16[256,2048]{1,0:T(8,128)(2,1)}, u32[]{:S(2)}) copy-start(bf16[256,2048]{1,0:T(8,128)(2,1)} %g_ref.3) | copy-start | bytes 3145732
  26.9 2.7 %copy-start.6 = (bf16[256,128]{1,0:T(8,128)(2,1)S(1)}, bf16[256,128]{1,0:T(8,128)(2,1)}, u32[]{:S(2)}) copy-start(bf16[256,128]{1,0:T(8,128)(2,1)} %get-tuple-element.69.edges_ref) | copy-start | bytes 196612
  26.9 2.0 %collective-permute-start.5 = (f32[16,64,128]{2,1,0:T(8,128)S(1)}, f32[16,64,128]{2,1,0:T(8,128)S(1)}, u32[]{:S(2)}, u32[]{:S(2)}) collective-permute-start(f32[16,64,128]{2,1,0:T(8,128)S(1)} %get-tuple-element.64), channel_id=1, source_target_pairs={{0,4},{4,0},{8,12},{12,8},{16,20},{20,16},{24,28},{28,24},{1,5},{5... | collective-permute-start | bytes 1572872 | tf_op jit(solution)/shard_map/ppermute | solution.py:372
  27.0 2.6 %collective-permute-start.6 = (f32[16,64,128]{2,1,0:T(8,128)S(1)}, f32[16,64,128]{2,1,0:T(8,128)S(1)}, u32[]{:S(2)}, u32[]{:S(2)}) collective-permute-start(f32[16,64,128]{2,1,0:T(8,128)S(1)} %get-tuple-element.68), channel_id=1, source_target_pairs={{0,4},{4,0},{8,12},{12,8},{16,20},{20,16},{24,28},{28,24},{1,5},{5... | collective-permute-start | bytes 1572872 | tf_op jit(solution)/shard_map/ppermute | solution.py:372
  27.8 4.3 %copy-start = (f32[16,64,128]{2,1,0:T(8,128)}, f32[16,64,128]{2,1,0:T(8,128)S(1)}, u32[]{:S(2)}) copy-start(f32[16,64,128]{2,1,0:T(8,128)S(1)} %get-tuple-element.101.own_b.own) | copy-start | bytes 1572868
  27.9 4.3 %copy-start.1 = (f32[16,64,128]{2,1,0:T(8,128)}, f32[16,64,128]{2,1,0:T(8,128)S(1)}, u32[]{:S(2)}) copy-start(f32[16,64,128]{2,1,0:T(8,128)S(1)} %get-tuple-element.102.own_f.own) | copy-start | bytes 1572868
  28.9 3.2 %copy-start.5 = (f32[16,64,128]{2,1,0:T(8,128)}, f32[16,64,128]{2,1,0:T(8,128)S(1)}, u32[]{:S(2)}) copy-start(f32[16,64,128]{2,1,0:T(8,128)S(1)} %collective-permute-done.5.other_f.other) | copy-start | bytes 1572868
  29.6 2.5 %copy-start.4 = (f32[16,64,128]{2,1,0:T(8,128)}, f32[16,64,128]{2,1,0:T(8,128)S(1)}, u32[]{:S(2)}) copy-start(f32[16,64,128]{2,1,0:T(8,128)S(1)} %collective-permute-done.6.other_b.other) | copy-start | bytes 1572868
  29.6 2.5 %copy-start.7 = (f32[4,2,64,128]{3,2,1,0:T(8,128)S(1)}, f32[4,2,64,128]{3,2,1,0:T(8,128)}, u32[]{:S(2)}) copy-start(f32[4,2,64,128]{3,2,1,0:T(8,128)} %get-tuple-element.70) | copy-start | bytes 786436
  32.2 8.8 %collective-permute-start.7 = (f32[2,64,128]{2,1,0:T(8,128)S(1)}, f32[2,64,128]{2,1,0:T(8,128)S(1)}, u32[]{:S(2)}, u32[]{:S(2)}) collective-permute-start(f32[2,64,128]{2,1,0:T(8,128)S(1)} %get-tuple-element.71), channel_id=1, source_target_pairs={{0,2},{1,3},{2,0},{3,1},{4,6},{5,7},{6,4},{7,5},{8,10},{9,11},{10,... | collective-permute-start | bytes 196616 | tf_op jit(solution)/shard_map/ppermute | solution.py:372
  34.9 6.4 %collective-permute-start.8 = (f32[2,64,128]{2,1,0:T(8,128)S(1)}, f32[2,64,128]{2,1,0:T(8,128)S(1)}, u32[]{:S(2)}, u32[]{:S(2)}) collective-permute-start(f32[2,64,128]{2,1,0:T(8,128)S(1)} %get-tuple-element.72), channel_id=1, source_target_pairs={{0,3},{1,2},{2,1},{3,0},{4,7},{5,6},{6,5},{7,4},{8,11},{9,10},{10,... | collective-permute-start | bytes 196616 | tf_op jit(solution)/shard_map/ppermute | solution.py:372
  36.2 5.4 %collective-permute-start.9 = (f32[2,64,128]{2,1,0:T(8,128)S(1)}, f32[2,64,128]{2,1,0:T(8,128)S(1)}, u32[]{:S(2)}, u32[]{:S(2)}) collective-permute-start(f32[2,64,128]{2,1,0:T(8,128)S(1)} %get-tuple-element.73), channel_id=1, source_target_pairs={{0,1},{1,0},{2,3},{3,2},{4,5},{5,4},{6,7},{7,6},{8,9},{9,8},{10,11... | collective-permute-start | bytes 196616 | tf_op jit(solution)/shard_map/ppermute | solution.py:372
  41.6 8.4 %collective-permute-start.10 = (bf16[2,64,128]{2,1,0:T(8,128)(2,1)S(1)}, bf16[2,64,128]{2,1,0:T(8,128)(2,1)S(1)}, u32[]{:S(2)}, u32[]{:S(2)}) collective-permute-start(bf16[2,64,128]{2,1,0:T(8,128)(2,1)S(1)} %add_convert_fusion), channel_id=1, source_target_pairs={{0,2},{1,3},{2,0},{3,1},{4,6},{5,7},{6,4},{7,5},{8,10},{9,11},{10,... | collective-permute-start | bytes 98312 | tf_op jit(solution)/shard_map/ppermute | solution.py:372
  44.2 5.8 %collective-permute-start.11 = (bf16[2,64,128]{2,1,0:T(8,128)(2,1)S(1)}, bf16[2,64,128]{2,1,0:T(8,128)(2,1)S(1)}, u32[]{:S(2)}, u32[]{:S(2)}) collective-permute-start(bf16[2,64,128]{2,1,0:T(8,128)(2,1)S(1)} %add_convert_fusion), channel_id=1, source_target_pairs={{0,3},{1,2},{2,1},{3,0},{4,7},{5,6},{6,5},{7,4},{8,11},{9,10},{10,... | collective-permute-start | bytes 98312 | tf_op jit(solution)/shard_map/ppermute | solution.py:372
  45.2 4.8 %collective-permute-start.12 = (bf16[2,64,128]{2,1,0:T(8,128)(2,1)S(1)}, bf16[2,64,128]{2,1,0:T(8,128)(2,1)S(1)}, u32[]{:S(2)}, u32[]{:S(2)}) collective-permute-start(bf16[2,64,128]{2,1,0:T(8,128)(2,1)S(1)} %add_convert_fusion), channel_id=1, source_target_pairs={{0,1},{1,0},{2,3},{3,2},{4,5},{5,4},{6,7},{7,6},{8,9},{9,8},{10,11... | collective-permute-start | bytes 98312 | tf_op jit(solution)/shard_map/ppermute | solution.py:372

commit v9 on v8

--- a/solution.py
+++ b/solution.py
@@ -178,8 +178,7 @@
             swapped = jnp.concatenate([turned[half:], turned[:half]], 0)
             out[...] = jnp.where(swap, swapped, turned).astype(BF16)
 
-    for copy in big(step_id):
-        copy.wait()
+    arriving = big(step_id)
     edges = edges_ref[...]
     spreads = [make(edges.shape[1], step_id * group, width, wide) for make in SPREADS]
     rows = dot(meta[...], spreads[0] + spreads[1], NN)
@@ -187,6 +186,7 @@
         for n in range(META):
             meta_ref[n, pl.ds(step_id * chunks + k, 1)] = rows[n : n + 1, k * LANES : (k + 1) * LANES]
     for kind, (ref, turned) in enumerate(((x_ref, b_t), (g_ref, c_t))):
+        arriving[kind].wait()
         turned = turned[...]
         for lanes in pieces(wide):
             scale = dot(edges, spreads[kind][:, lanes], NN)

time: 51.1 us -> 51.5 us (level)
  no operation moved by 1% of the time
where the time goes in v9:
time: 51.5 us; the launch traced here: 51.2 us
  Pallas kernels  26.5 us (51%)
  starting transfers between devices  13.6 us (26%)
  waiting for transfers between devices  6.36 us (12%)
  other arithmetic  2.77 us (5%)
  local copies, waits for them, and re-layouts  0.96 us (2%)
  between operations  0.93 us (2%)
    ppermute x13, starting transfers between devices, swap_with(): return lax.ppermute(value, axis, [(i, i ^ mask) for i in range(size)])  13.6 us
    pallas_call x1, Pallas kernels, shards(): pl.pallas_call(functools.partial(local_kernel, group, width, masks), grid...  9.84 us
    pallas_call x2, Pallas kernels, finish(): pl.pallas_call(functools.partial(output_kernel, group, width, kind), grid...  9.09 us
    ppermute x13, waiting for transfers between devices, swap_with(): return lax.ppermute(value, axis, [(i, i ^ mask) for i in range(size)])  6.36 us
    pallas_call x1, Pallas kernels, shards(): pl.pallas_call(functools.partial(states_kernel, sgroup, width), grid=(sgr...  5.13 us
    pallas_call x1, Pallas kernels, shards(): pl.pallas_call(functools.partial(grads_kernel, ggroup, width, masks), gri...  2.44 us
    max x1, other arithmetic, shards(): jnp.maximum(mine, least)  1.32 us
  transfers between devices with their start and end apart: 13, of which 6 were waited for; matrix products, arithmetic and copies ran while one was open for 3% of the time, Pallas kernels for 37%

profile of v9, /device:TPU:0, one launch (start us, length us, event | category | flops | bytes accessed | tf_op | source)
XLA Modules:
  0.0 51.2 jit_solution(10029464627404964407)
XLA Ops:
  0.6 5.1 %states.1 = (f32[16,128,128]{2,1,0:T(8,128)}, f32[16,128,128]{2,1,0:T(8,128)}, f32[8,16,128]{2,1,0:T(8,128)}, bf16[256,128]{1,0:T(8,128)(2,1)}) custom-call(s32[1]{0:T(128)} %bitcast.core_ref, bf16[256,2048]{1,0:T(8,128)(2,1)} %x_ref.3, bf16[256,2048]{1,0:T(8,128)(2,1)} %g_ref.3, f32[32,256]{1,0:T(8,128)} %step_blk.1, f32[1,32]{1,0:T(1,128)} %bitcast.89, ...), custom_call_target="tpu_custom_call" | custom-call | tf_op jit(solution)/shard_map/states/pallas_call | solution.py:471
  5.8 0.5 %collective-permute-start.1 = (f32[16,128,128]{2,1,0:T(8,128)}, f32[16,128,128]{2,1,0:T(8,128)S(1)}, u32[]{:S(2)}, u32[]{:S(2)}) collective-permute-start(f32[16,128,128]{2,1,0:T(8,128)} %get-tuple-element.50), channel_id=1, source_target_pairs={{0,4},{4,0},{8,12},{12,8},{16,20},{20,16},{24,28},{28,24},{1,5},{5... | collective-permute-start | bytes 3145736 | tf_op jit(solution)/shard_map/ppermute | solution.py:372
  6.3 0.1 collective-permute-start
  6.4 1.3 %broadcast_maximum_fusion = f32[16,128,128]{2,1,0:T(8,128)S(1)} fusion(f32[16,128,128]{2,1,0:T(8,128)} %get-tuple-element.47), kind=kLoop, calls=%fused_computation.28 | loop fusion | flops 262144 | bytes 2097152 | tf_op jit(solution)/shard_map/max | solution.py:500
  7.7 1.1 %collective-permute-done = f32[8,16,128]{2,1,0:T(8,128)S(1)} collective-permute-done((f32[8,16,128]{2,1,0:T(8,128)}, f32[8,16,128]{2,1,0:T(8,128)S(1)}, u32[]{:S(2)}, u32[]{:S(2)}) %collective-permute-start) | collective-permute-done | bytes 65568 | tf_op jit(solution)/shard_map/ppermute | solution.py:372
  9.0 0.4 multiply_convert_fusion
  9.3 0.2 fusion.13
  9.5 2.9 %collective-permute-start.2 = (f16[1072,128]{1,0:T(8,128)(2,1)S(1)}, f16[1072,128]{1,0:T(8,128)(2,1)S(1)}, u32[]{:S(2)}, u32[]{:S(2)}) collective-permute-start(f16[1072,128]{1,0:T(8,128)(2,1)S(1)} %get-tuple-element.51), channel_id=1, source_target_pairs={{0,8},{4,12},{8,0},{12,4},{16,24},{20,28},{24,16},{28,20},{1,9},{5... | collective-permute-start | bytes 823304 | tf_op jit(solution)/shard_map/ppermute | solution.py:372
  12.5 1.5 %collective-permute-start.3 = (f16[1072,128]{1,0:T(8,128)(2,1)S(1)}, f16[1072,128]{1,0:T(8,128)(2,1)S(1)}, u32[]{:S(2)}, u32[]{:S(2)}) collective-permute-start(f16[1072,128]{1,0:T(8,128)(2,1)S(1)} %get-tuple-element.52), channel_id=1, source_target_pairs={{0,16},{4,20},{8,24},{12,28},{16,0},{20,4},{24,8},{28,12},{1,17},{... | collective-permute-start | bytes 823304 | tf_op jit(solution)/shard_map/ppermute | solution.py:372
  14.0 9.8 %local.1 = (f32[256,2048]{1,0:T(8,128)}, f32[256,2048]{1,0:T(8,128)}, f32[4,2,64,128]{3,2,1,0:T(8,128)}) custom-call(f32[32]{0:T(128)} %skip_ref, s32[1]{0:T(128)} %bitcast.1.place_ref, bf16[256,2048]{1,0:T(8,128)(2,1)} %x_ref.3, bf16[256,2048]{1,0:T(8,128)(2,1)} %g_ref.3, f32[32,256]{1,0:T(8,128)} %step_blk.1, f32[32,256]{1,0:T(8,128)} %step_blk.1, ...), custom_call_target="tpu_custom_call" | custom-call | flops 2684354560 | bytes 6291456 | tf_op jit(solution)/shard_map/local/pallas_call | solution.py:535
  23.9 2.8 %collective-permute-done.3 = f16[1072,128]{1,0:T(8,128)(2,1)S(1)} collective-permute-done((f16[1072,128]{1,0:T(8,128)(2,1)S(1)}, f16[1072,128]{1,0:T(8,128)(2,1)S(1)}, u32[]{:S(2)}, u32[]{:S(2)}) %collective-permute-start.3) | collective-permute-done | bytes 274464 | tf_op jit(solution)/shard_map/ppermute | solution.py:372
  26.7 0.1 slice.115
  26.7 0.1 slice.121
  26.8 0.1 slice.125
  26.9 0.4 fusion.5
  27.3 0.1 collective-permute-start.5
  27.4 0.5 collective-permute-start.6
  27.9 0.4 fusion.11
  28.3 1.0 %collective-permute-done.5.other_f.other = f32[16,64,128]{2,1,0:T(8,128)S(1)} collective-permute-done((f32[16,64,128]{2,1,0:T(8,128)S(1)}, f32[16,64,128]{2,1,0:T(8,128)S(1)}, u32[]{:S(2)}, u32[]{:S(2)}) %collective-permute-start.5) | collective-permute-done | bytes 524320 | tf_op jit(solution)/shard_map/ppermute | solution.py:372
  29.3 0.7 %collective-permute-done.6.other_b.other = f32[16,64,128]{2,1,0:T(8,128)S(1)} collective-permute-done((f32[16,64,128]{2,1,0:T(8,128)S(1)}, f32[16,64,128]{2,1,0:T(8,128)S(1)}, u32[]{:S(2)}, u32[]{:S(2)}) %collective-permute-start.6) | collective-permute-done | bytes 524320 | tf_op jit(solution)/shard_map/ppermute | solution.py:372
  30.1 2.4 %grads.1 = f32[4,2,64,128]{3,2,1,0:T(8,128)S(1)} custom-call(s32[1]{0:T(128)} %bitcast.core_ref, s32[1]{0:T(128)} %bitcast.1.place_ref, f32[16,64,128]{2,1,0:T(8,128)S(1)} %get-tuple-element.102.own_f.own, f32[16,64,128]{2,1,0:T(8,128)S(1)} %collective-permute-done.5.other_f.other, f32[16,64,128]{2,1,0:T(8,128)S(1)} %get-tuple-element.101.own_b.own, ...), custom_call_target="tpu_custom_call" | custom-call | tf_op jit(solution)/shard_map/grads/pallas_call | solution.py:602
  32.6 2.7 %collective-permute-start.7 = (f32[2,64,128]{2,1,0:T(8,128)S(1)}, f32[2,64,128]{2,1,0:T(8,128)S(1)}, u32[]{:S(2)}, u32[]{:S(2)}) collective-permute-start(f32[2,64,128]{2,1,0:T(8,128)S(1)} %get-tuple-element.71), channel_id=1, source_target_pairs={{0,2},{1,3},{2,0},{3,1},{4,6},{5,7},{6,4},{7,5},{8,10},{9,11},{10,... | collective-permute-start | bytes 196616 | tf_op jit(solution)/shard_map/ppermute | solution.py:372
  35.3 1.3 %collective-permute-start.8 = (f32[2,64,128]{2,1,0:T(8,128)S(1)}, f32[2,64,128]{2,1,0:T(8,128)S(1)}, u32[]{:S(2)}, u32[]{:S(2)}) collective-permute-start(f32[2,64,128]{2,1,0:T(8,128)S(1)} %get-tuple-element.72), channel_id=1, source_target_pairs={{0,3},{1,2},{2,1},{3,0},{4,7},{5,6},{6,5},{7,4},{8,11},{9,10},{10,... | collective-permute-start | bytes 196616 | tf_op jit(solution)/shard_map/ppermute | solution.py:372
  36.6 0.2 collective-permute-start.9
  36.9 4.5 %mixed.1 = bf16[256,2048]{1,0:T(8,128)(2,1)} custom-call(s32[1]{0:T(128)} %bitcast.core_ref, f32[16,64,128]{2,1,0:T(8,128)} %copy-done.1, f32[16,64,128]{2,1,0:T(8,128)} %copy-done.5, f32[256,2048]{1,0:T(8,128)} %get-tuple-element.75.base_ref, bf16[256,128]{1,0:T(8,128)(2,1)} %get-tuple-element.69.edges_ref, bf16[256,128]{1,0:T(8,128)(2,1)} %proj_ref.2), custom_call_target="tpu_custom_call" | custom-call | flops 268435456 | bytes 4194304 | tf_op jit(solution)/shard_map/mixed/pallas_call | solution.py:622
  41.4 0.3 collective-permute-done.8
  41.7 0.3 collective-permute-done.9
  42.0 2.6 %collective-permute-start.10 = (bf16[2,64,128]{2,1,0:T(8,128)(2,1)S(1)}, bf16[2,64,128]{2,1,0:T(8,128)(2,1)S(1)}, u32[]{:S(2)}, u32[]{:S(2)}) collective-permute-start(bf16[2,64,128]{2,1,0:T(8,128)(2,1)S(1)} %add_convert_fusion), channel_id=1, source_target_pairs={{0,2},{1,3},{2,0},{3,1},{4,6},{5,7},{6,4},{7,5},{8,10},{9,11},{10,... | collective-permute-start | bytes 98312 | tf_op jit(solution)/shard_map/ppermute | solution.py:372
  44.7 1.0 %collective-permute-start.11 = (bf16[2,64,128]{2,1,0:T(8,128)(2,1)S(1)}, bf16[2,64,128]{2,1,0:T(8,128)(2,1)S(1)}, u32[]{:S(2)}, u32[]{:S(2)}) collective-permute-start(bf16[2,64,128]{2,1,0:T(8,128)(2,1)S(1)} %add_convert_fusion), channel_id=1, source_target_pairs={{0,3},{1,2},{2,1},{3,0},{4,7},{5,6},{6,5},{7,4},{8,11},{9,10},{10,... | collective-permute-start | bytes 98312 | tf_op jit(solution)/shard_map/ppermute | solution.py:372
  45.7 0.2 collective-permute-start.12
  45.9 4.6 %grad_inputs.1 = bf16[256,2048]{1,0:T(8,128)(2,1)} custom-call(s32[1]{0:T(128)} %bitcast.core_ref, f32[16,64,128]{2,1,0:T(8,128)} %copy-done, f32[16,64,128]{2,1,0:T(8,128)} %copy-done.4, f32[256,2048]{1,0:T(8,128)} %get-tuple-element.83.base_ref, bf16[256,128]{1,0:T(8,128)(2,1)} %get-tuple-element.69.edges_ref, bf16[256,128]{1,0:T(8,128)(2,1)} %proj_ref.3), custom_call_target="tpu_custom_call" | custom-call | flops 268435456 | bytes 4194304 | tf_op jit(solution)/shard_map/grad_inputs/pallas_call | solution.py:622
  50.5 0.7 %fusion.39 = (bf16[4,1,64,128]{3,2,0,1:T(8,128)(2,1)}, bf16[4,1,64,128]{3,2,0,1:T(8,128)(2,1)}) fusion(bf16[4,2,64,128]{3,2,0,1:T(8,128)(2,1)S(1)} %bitcast_dynamic-update-slice_fusion), kind=kLoop, calls=%fused_computation.95 | loop fusion | bytes 262144 | tf_op jit(solution)/shard_map/slice | solution.py:658
  (38 shorter events, 0.3 us)
Async XLA Ops:
  5.8 1.9 %copy-start.8 = (f32[8,16,128]{2,1,0:T(8,128)S(1)}, f32[8,16,128]{2,1,0:T(8,128)}, u32[]{:S(2)}) copy-start(f32[8,16,128]{2,1,0:T(8,128)} %get-tuple-element.46) | copy-start | bytes 196612
  5.8 3.2 %collective-permute-start.1 = (f32[16,128,128]{2,1,0:T(8,128)}, f32[16,128,128]{2,1,0:T(8,128)S(1)}, u32[]{:S(2)}, u32[]{:S(2)}) collective-permute-start(f32[16,128,128]{2,1,0:T(8,128)} %get-tuple-element.50), channel_id=1, source_target_pairs={{0,4},{4,0},{8,12},{12,8},{16,20},{20,16},{24,28},{28,24},{1,5},{5... | collective-permute-start | bytes 3145736 | tf_op jit(solution)/shard_map/ppermute | solution.py:372
  6.3 2.6 %collective-permute-start = (f32[8,16,128]{2,1,0:T(8,128)}, f32[8,16,128]{2,1,0:T(8,128)S(1)}, u32[]{:S(2)}, u32[]{:S(2)}) collective-permute-start(f32[8,16,128]{2,1,0:T(8,128)} %get-tuple-element.46), channel_id=1, source_target_pairs={{0,4},{4,0},{8,12},{12,8},{16,20},{20,16},{24,28},{28,24},{1,5},{5... | collective-permute-start | bytes 196616 | tf_op jit(solution)/shard_map/ppermute | solution.py:372
  9.5 14.3 %collective-permute-start.2 = (f16[1072,128]{1,0:T(8,128)(2,1)S(1)}, f16[1072,128]{1,0:T(8,128)(2,1)S(1)}, u32[]{:S(2)}, u32[]{:S(2)}) collective-permute-start(f16[1072,128]{1,0:T(8,128)(2,1)S(1)} %get-tuple-element.51), channel_id=1, source_target_pairs={{0,8},{4,12},{8,0},{12,4},{16,24},{20,28},{24,16},{28,20},{1,9},{5... | collective-permute-start | bytes 823304 | tf_op jit(solution)/shard_map/ppermute | solution.py:372
  12.5 14.2 %collective-permute-start.3 = (f16[1072,128]{1,0:T(8,128)(2,1)S(1)}, f16[1072,128]{1,0:T(8,128)(2,1)S(1)}, u32[]{:S(2)}, u32[]{:S(2)}) collective-permute-start(f16[1072,128]{1,0:T(8,128)(2,1)S(1)} %get-tuple-element.52), channel_id=1, source_target_pairs={{0,16},{4,20},{8,24},{12,28},{16,0},{20,4},{24,8},{28,12},{1,17},{... | collective-permute-start | bytes 823304 | tf_op jit(solution)/shard_map/ppermute | solution.py:372
  14.0 12.7 %collective-permute-start.4 = (f16[1072,128]{1,0:T(8,128)(2,1)S(1)}, f16[1072,128]{1,0:T(8,128)(2,1)S(1)}, u32[]{:S(2)}, u32[]{:S(2)}) collective-permute-start(f16[1072,128]{1,0:T(8,128)(2,1)S(1)} %get-tuple-element.52), channel_id=1, source_target_pairs={{0,24},{4,28},{8,16},{12,20},{16,8},{20,12},{24,0},{28,4},{1,25},{... | collective-permute-start | bytes 823304 | tf_op jit(solution)/shard_map/ppermute | solution.py:372
  27.3 2.8 %copy-start.2 = (bf16[256,2048]{1,0:T(8,128)(2,1)S(1)}, bf16[256,2048]{1,0:T(8,128)(2,1)}, u32[]{:S(2)}) copy-start(bf16[256,2048]{1,0:T(8,128)(2,1)} %x_ref.3) | copy-start | bytes 3145732
  27.3 2.8 %copy-start.3 = (bf16[256,2048]{1,0:T(8,128)(2,1)S(1)}, bf16[256,2048]{1,0:T(8,128)(2,1)}, u32[]{:S(2)}) copy-start(bf16[256,2048]{1,0:T(8,128)(2,1)} %g_ref.3) | copy-start | bytes 3145732
  27.3 2.7 %copy-start.6 = (bf16[256,128]{1,0:T(8,128)(2,1)S(1)}, bf16[256,128]{1,0:T(8,128)(2,1)}, u32[]{:S(2)}) copy-start(bf16[256,128]{1,0:T(8,128)(2,1)} %get-tuple-element.69.edges_ref) | copy-start | bytes 196612
  27.3 2.0 %collective-permute-start.5 = (f32[16,64,128]{2,1,0:T(8,128)S(1)}, f32[16,64,128]{2,1,0:T(8,128)S(1)}, u32[]{:S(2)}, u32[]{:S(2)}) collective-permute-start(f32[16,64,128]{2,1,0:T(8,128)S(1)} %get-tuple-element.64), channel_id=1, source_target_pairs={{0,4},{4,0},{8,12},{12,8},{16,20},{20,16},{24,28},{28,24},{1,5},{5... | collective-permute-start | bytes 1572872 | tf_op jit(solution)/shard_map/ppermute | solution.py:372
  27.4 2.6 %collective-permute-start.6 = (f32[16,64,128]{2,1,0:T(8,128)S(1)}, f32[16,64,128]{2,1,0:T(8,128)S(1)}, u32[]{:S(2)}, u32[]{:S(2)}) collective-permute-start(f32[16,64,128]{2,1,0:T(8,128)S(1)} %get-tuple-element.68), channel_id=1, source_target_pairs={{0,4},{4,0},{8,12},{12,8},{16,20},{20,16},{24,28},{28,24},{1,5},{5... | collective-permute-start | bytes 1572872 | tf_op jit(solution)/shard_map/ppermute | solution.py:372
  28.3 4.3 %copy-start = (f32[16,64,128]{2,1,0:T(8,128)}, f32[16,64,128]{2,1,0:T(8,128)S(1)}, u32[]{:S(2)}) copy-start(f32[16,64,128]{2,1,0:T(8,128)S(1)} %get-tuple-element.101.own_b.own) | copy-start | bytes 1572868
  28.3 4.3 %copy-start.1 = (f32[16,64,128]{2,1,0:T(8,128)}, f32[16,64,128]{2,1,0:T(8,128)S(1)}, u32[]{:S(2)}) copy-start(f32[16,64,128]{2,1,0:T(8,128)S(1)} %get-tuple-element.102.own_f.own) | copy-start | bytes 1572868
  29.3 3.2 %copy-start.5 = (f32[16,64,128]{2,1,0:T(8,128)}, f32[16,64,128]{2,1,0:T(8,128)S(1)}, u32[]{:S(2)}) copy-start(f32[16,64,128]{2,1,0:T(8,128)S(1)} %collective-permute-done.5.other_f.other) | copy-start | bytes 1572868
  30.1 2.5 %copy-start.4 = (f32[16,64,128]{2,1,0:T(8,128)}, f32[16,64,128]{2,1,0:T(8,128)S(1)}, u32[]{:S(2)}) copy-start(f32[16,64,128]{2,1,0:T(8,128)S(1)} %collective-permute-done.6.other_b.other) | copy-start | bytes 1572868
  30.1 2.5 %copy-start.7 = (f32[4,2,64,128]{3,2,1,0:T(8,128)S(1)}, f32[4,2,64,128]{3,2,1,0:T(8,128)}, u32[]{:S(2)}) copy-start(f32[4,2,64,128]{3,2,1,0:T(8,128)} %get-tuple-element.70) | copy-start | bytes 786436
  32.6 8.8 %collective-permute-start.7 = (f32[2,64,128]{2,1,0:T(8,128)S(1)}, f32[2,64,128]{2,1,0:T(8,128)S(1)}, u32[]{:S(2)}, u32[]{:S(2)}) collective-permute-start(f32[2,64,128]{2,1,0:T(8,128)S(1)} %get-tuple-element.71), channel_id=1, source_target_pairs={{0,2},{1,3},{2,0},{3,1},{4,6},{5,7},{6,4},{7,5},{8,10},{9,11},{10,... | collective-permute-start | bytes 196616 | tf_op jit(solution)/shard_map/ppermute | solution.py:372
  35.3 6.4 %collective-permute-start.8 = (f32[2,64,128]{2,1,0:T(8,128)S(1)}, f32[2,64,128]{2,1,0:T(8,128)S(1)}, u32[]{:S(2)}, u32[]{:S(2)}) collective-permute-start(f32[2,64,128]{2,1,0:T(8,128)S(1)} %get-tuple-element.72), channel_id=1, source_target_pairs={{0,3},{1,2},{2,1},{3,0},{4,7},{5,6},{6,5},{7,4},{8,11},{9,10},{10,... | collective-permute-start | bytes 196616 | tf_op jit(solution)/shard_map/ppermute | solution.py:372
  36.6 5.4 %collective-permute-start.9 = (f32[2,64,128]{2,1,0:T(8,128)S(1)}, f32[2,64,128]{2,1,0:T(8,128)S(1)}, u32[]{:S(2)}, u32[]{:S(2)}) collective-permute-start(f32[2,64,128]{2,1,0:T(8,128)S(1)} %get-tuple-element.73), channel_id=1, source_target_pairs={{0,1},{1,0},{2,3},{3,2},{4,5},{5,4},{6,7},{7,6},{8,9},{9,8},{10,11... | collective-permute-start | bytes 196616 | tf_op jit(solution)/shard_map/ppermute | solution.py:372
  42.0 8.4 %collective-permute-start.10 = (bf16[2,64,128]{2,1,0:T(8,128)(2,1)S(1)}, bf16[2,64,128]{2,1,0:T(8,128)(2,1)S(1)}, u32[]{:S(2)}, u32[]{:S(2)}) collective-permute-start(bf16[2,64,128]{2,1,0:T(8,128)(2,1)S(1)} %add_convert_fusion), channel_id=1, source_target_pairs={{0,2},{1,3},{2,0},{3,1},{4,6},{5,7},{6,4},{7,5},{8,10},{9,11},{10,... | collective-permute-start | bytes 98312 | tf_op jit(solution)/shard_map/ppermute | solution.py:372
  44.7 5.8 %collective-permute-start.11 = (bf16[2,64,128]{2,1,0:T(8,128)(2,1)S(1)}, bf16[2,64,128]{2,1,0:T(8,128)(2,1)S(1)}, u32[]{:S(2)}, u32[]{:S(2)}) collective-permute-start(bf16[2,64,128]{2,1,0:T(8,128)(2,1)S(1)} %add_convert_fusion), channel_id=1, source_target_pairs={{0,3},{1,2},{2,1},{3,0},{4,7},{5,6},{6,5},{7,4},{8,11},{9,10},{10,... | collective-permute-start | bytes 98312 | tf_op jit(solution)/shard_map/ppermute | solution.py:372
  45.7 4.8 %collective-permute-start.12 = (bf16[2,64,128]{2,1,0:T(8,128)(2,1)S(1)}, bf16[2,64,128]{2,1,0:T(8,128)(2,1)S(1)}, u32[]{:S(2)}, u32[]{:S(2)}) collective-permute-start(bf16[2,64,128]{2,1,0:T(8,128)(2,1)S(1)} %add_convert_fusion), channel_id=1, source_target_pairs={{0,1},{1,0},{2,3},{3,2},{4,5},{5,4},{6,7},{7,6},{8,9},{9,8},{10,11... | collective-permute-start | bytes 98312 | tf_op jit(solution)/shard_map/ppermute | solution.py:372

commit v10 on v8

--- a/solution.py
+++ b/solution.py
@@ -16,7 +16,7 @@
 BOUND = 6.0 * 1.796875
 STEP = 1024.0
 META = 8
-STATES_VMEM, LOCAL_VMEM, GRADS_VMEM, OUTPUT_VMEM = 62, 60, 48, 60
+STATES_VMEM, LOCAL_VMEM, GRADS_VMEM, OUTPUT_VMEM = 62, 60, 48, 40
 
 NN = (((1,), (0,)), ((), ()))
 NT = (((1,), (1,)), ((), ()))

time: 51.1 us -> 50.8 us (level)
  Pallas kernels: 26.1 us -> 22.4 us
  waiting for transfers between devices: 6.37 us -> 8.39 us
  local copies, waits for them, and re-layouts: 0.96 us -> 2.54 us
    pallas_call x2, Pallas kernels: 9.09 us -> 5.36 us  [finish(): pl.pallas_call(functools.partial(output_kernel, group, width, kind), grid...]
    ppermute x13, waiting for transfers between devices: 6.37 us -> 8.39 us  [swap_with(): return lax.ppermute(value, axis, [(i, i ^ mask) for i in range(size)])]
    unnamed x18, local copies, waits for them, and re-layouts: 0.05 us -> 1.64 us
  transfers between devices with their start and end apart: 13 -> 13, of which waited for: 6 -> 7; matrix products, arithmetic and copies ran while one was open for 3% -> 3% of each run, Pallas kernels for 37% -> 30%
where the time goes in v10:
time: 50.8 us; the launch traced here: 50.6 us
  Pallas kernels  22.4 us (44%)
  starting transfers between devices  13.6 us (27%)
  waiting for transfers between devices  8.39 us (17%)
  other arithmetic  2.77 us (5%)
  local copies, waits for them, and re-layouts  2.54 us (5%)
  between operations  0.89 us (2%)
    ppermute x13, starting transfers between devices, swap_with(): return lax.ppermute(value, axis, [(i, i ^ mask) for i in range(size)])  13.6 us
    pallas_call x1, Pallas kernels, shards(): pl.pallas_call(functools.partial(local_kernel, group, width, masks), grid...  9.9 us
    ppermute x13, waiting for transfers between devices, swap_with(): return lax.ppermute(value, axis, [(i, i ^ mask) for i in range(size)])  8.39 us
    pallas_call x2, Pallas kernels, finish(): pl.pallas_call(functools.partial(output_kernel, group, width, kind), grid...  5.36 us
    pallas_call x1, Pallas kernels, shards(): pl.pallas_call(functools.partial(states_kernel, sgroup, width), grid=(sgr...  4.7 us
    pallas_call x1, Pallas kernels, shards(): pl.pallas_call(functools.partial(grads_kernel, ggroup, width, masks), gri...  2.44 us
    unnamed x18, local copies, waits for them, and re-layouts  1.64 us
    max x1, other arithmetic, shards(): jnp.maximum(mine, least)  1.32 us
  transfers between devices with their start and end apart: 13, of which 7 were waited for; matrix products, arithmetic and copies ran while one was open for 3% of the time, Pallas kernels for 30%

profile of v10, /device:TPU:0, one launch (start us, length us, event | category | flops | bytes accessed | tf_op | source)
XLA Modules:
  0.0 50.6 jit_solution(10004966885515653278)
XLA Ops:
  0.6 4.7 %states.1 = (f32[16,128,128]{2,1,0:T(8,128)}, f32[16,128,128]{2,1,0:T(8,128)}, f32[8,16,128]{2,1,0:T(8,128)}, bf16[256,128]{1,0:T(8,128)(2,1)}) custom-call(s32[1]{0:T(128)} %bitcast.core_ref, bf16[256,2048]{1,0:T(8,128)(2,1)} %x_ref.3, bf16[256,2048]{1,0:T(8,128)(2,1)} %g_ref.3, f32[32,256]{1,0:T(8,128)} %step_blk.1, f32[1,32]{1,0:T(1,128)} %bitcast.89, ...), custom_call_target="tpu_custom_call" | custom-call | tf_op jit(solution)/shard_map/states/pallas_call | solution.py:471
  5.4 0.5 %collective-permute-start.1 = (f32[16,128,128]{2,1,0:T(8,128)}, f32[16,128,128]{2,1,0:T(8,128)S(1)}, u32[]{:S(2)}, u32[]{:S(2)}) collective-permute-start(f32[16,128,128]{2,1,0:T(8,128)} %get-tuple-element.50), channel_id=1, source_target_pairs={{0,4},{4,0},{8,12},{12,8},{16,20},{20,16},{24,28},{28,24},{1,5},{5... | collective-permute-start | bytes 3145736 | tf_op jit(solution)/shard_map/ppermute | solution.py:372
  5.9 0.1 collective-permute-start
  6.0 1.3 %broadcast_maximum_fusion = f32[16,128,128]{2,1,0:T(8,128)S(1)} fusion(f32[16,128,128]{2,1,0:T(8,128)} %get-tuple-element.47), kind=kLoop, calls=%fused_computation.28 | loop fusion | flops 262144 | bytes 2097152 | tf_op jit(solution)/shard_map/max | solution.py:500
  7.3 1.1 %collective-permute-done = f32[8,16,128]{2,1,0:T(8,128)S(1)} collective-permute-done((f32[8,16,128]{2,1,0:T(8,128)}, f32[8,16,128]{2,1,0:T(8,128)S(1)}, u32[]{:S(2)}, u32[]{:S(2)}) %collective-permute-start) | collective-permute-done | bytes 65568 | tf_op jit(solution)/shard_map/ppermute | solution.py:372
  8.5 0.4 multiply_convert_fusion
  8.9 0.2 fusion.13
  9.1 2.9 %collective-permute-start.2 = (f16[1072,128]{1,0:T(8,128)(2,1)S(1)}, f16[1072,128]{1,0:T(8,128)(2,1)S(1)}, u32[]{:S(2)}, u32[]{:S(2)}) collective-permute-start(f16[1072,128]{1,0:T(8,128)(2,1)S(1)} %get-tuple-element.51), channel_id=1, source_target_pairs={{0,8},{4,12},{8,0},{12,4},{16,24},{20,28},{24,16},{28,20},{1,9},{5... | collective-permute-start | bytes 823304 | tf_op jit(solution)/shard_map/ppermute | solution.py:372
  12.0 1.5 %collective-permute-start.3 = (f16[1072,128]{1,0:T(8,128)(2,1)S(1)}, f16[1072,128]{1,0:T(8,128)(2,1)S(1)}, u32[]{:S(2)}, u32[]{:S(2)}) collective-permute-start(f16[1072,128]{1,0:T(8,128)(2,1)S(1)} %get-tuple-element.52), channel_id=1, source_target_pairs={{0,16},{4,20},{8,24},{12,28},{16,0},{20,4},{24,8},{28,12},{1,17},{... | collective-permute-start | bytes 823304 | tf_op jit(solution)/shard_map/ppermute | solution.py:372
  13.6 9.9 %local.1 = (f32[256,2048]{1,0:T(8,128)}, f32[256,2048]{1,0:T(8,128)}, f32[4,2,64,128]{3,2,1,0:T(8,128)}) custom-call(f32[32]{0:T(128)} %skip_ref, s32[1]{0:T(128)} %bitcast.1.place_ref, bf16[256,2048]{1,0:T(8,128)(2,1)} %x_ref.3, bf16[256,2048]{1,0:T(8,128)(2,1)} %g_ref.3, f32[32,256]{1,0:T(8,128)} %step_blk.1, f32[32,256]{1,0:T(8,128)} %step_blk.1, ...), custom_call_target="tpu_custom_call" | custom-call | flops 2684354560 | bytes 6291456 | tf_op jit(solution)/shard_map/local/pallas_call | solution.py:535
  23.5 2.8 %collective-permute-done.3 = f16[1072,128]{1,0:T(8,128)(2,1)S(1)} collective-permute-done((f16[1072,128]{1,0:T(8,128)(2,1)S(1)}, f16[1072,128]{1,0:T(8,128)(2,1)S(1)}, u32[]{:S(2)}, u32[]{:S(2)}) %collective-permute-start.3) | collective-permute-done | bytes 274464 | tf_op jit(solution)/shard_map/ppermute | solution.py:372
  26.3 0.1 slice.121
  26.5 0.4 fusion.5
  26.9 0.1 collective-permute-start.5
  27.0 0.5 collective-permute-start.6
  27.5 0.4 fusion.11
  27.8 1.0 %collective-permute-done.5.other_f.other = f32[16,64,128]{2,1,0:T(8,128)S(1)} collective-permute-done((f32[16,64,128]{2,1,0:T(8,128)S(1)}, f32[16,64,128]{2,1,0:T(8,128)S(1)}, u32[]{:S(2)}, u32[]{:S(2)}) %collective-permute-start.5) | collective-permute-done | bytes 524320 | tf_op jit(solution)/shard_map/ppermute | solution.py:372
  28.9 0.7 %collective-permute-done.6.other_b.other = f32[16,64,128]{2,1,0:T(8,128)S(1)} collective-permute-done((f32[16,64,128]{2,1,0:T(8,128)S(1)}, f32[16,64,128]{2,1,0:T(8,128)S(1)}, u32[]{:S(2)}, u32[]{:S(2)}) %collective-permute-start.6) | collective-permute-done | bytes 524320 | tf_op jit(solution)/shard_map/ppermute | solution.py:372
  29.7 2.4 %grads.1 = f32[4,2,64,128]{3,2,1,0:T(8,128)S(1)} custom-call(s32[1]{0:T(128)} %bitcast.core_ref, s32[1]{0:T(128)} %bitcast.1.place_ref, f32[16,64,128]{2,1,0:T(8,128)S(1)} %get-tuple-element.102.own_f.own, f32[16,64,128]{2,1,0:T(8,128)S(1)} %collective-permute-done.5.other_f.other, f32[16,64,128]{2,1,0:T(8,128)S(1)} %get-tuple-element.101.own_b.own, ...), custom_call_target="tpu_custom_call" | custom-call | tf_op jit(solution)/shard_map/grads/pallas_call | solution.py:602
  32.2 2.7 %collective-permute-start.7 = (f32[2,64,128]{2,1,0:T(8,128)S(1)}, f32[2,64,128]{2,1,0:T(8,128)S(1)}, u32[]{:S(2)}, u32[]{:S(2)}) collective-permute-start(f32[2,64,128]{2,1,0:T(8,128)S(1)} %get-tuple-element.71), channel_id=1, source_target_pairs={{0,2},{1,3},{2,0},{3,1},{4,6},{5,7},{6,4},{7,5},{8,10},{9,11},{10,... | collective-permute-start | bytes 196616 | tf_op jit(solution)/shard_map/ppermute | solution.py:372
  34.8 1.3 %collective-permute-start.8 = (f32[2,64,128]{2,1,0:T(8,128)S(1)}, f32[2,64,128]{2,1,0:T(8,128)S(1)}, u32[]{:S(2)}, u32[]{:S(2)}) collective-permute-start(f32[2,64,128]{2,1,0:T(8,128)S(1)} %get-tuple-element.72), channel_id=1, source_target_pairs={{0,3},{1,2},{2,1},{3,0},{4,7},{5,6},{6,5},{7,4},{8,11},{9,10},{10,... | collective-permute-start | bytes 196616 | tf_op jit(solution)/shard_map/ppermute | solution.py:372
  36.2 0.2 collective-permute-start.9
  36.4 1.6 %copy-done.3 = f32[256,2048]{1,0:T(8,128)S(1)} copy-done((f32[256,2048]{1,0:T(8,128)S(1)}, f32[256,2048]{1,0:T(8,128)}, u32[]{:S(2)}) %copy-start.3) | copy-done | bytes 2097176
  38.0 2.7 %mixed.1 = bf16[256,2048]{1,0:T(8,128)(2,1)} custom-call(s32[1]{0:T(128)} %bitcast.core_ref, f32[16,64,128]{2,1,0:T(8,128)S(1)} %get-tuple-element.102.own_f.own, f32[16,64,128]{2,1,0:T(8,128)S(1)} %collective-permute-done.5.other_f.other, f32[256,2048]{1,0:T(8,128)S(1)} %copy-done.3, bf16[256,128]{1,0:T(8,128)(2,1)S(1)} %copy-done.4, ...), custom_call_target="tpu_custom_call" | custom-call | flops 268435456 | bytes 4194304 | tf_op jit(solution)/shard_map/mixed/pallas_call | solution.py:622
  40.7 0.5 %collective-permute-done.8 = f32[2,64,128]{2,1,0:T(8,128)S(1)} collective-permute-done((f32[2,64,128]{2,1,0:T(8,128)S(1)}, f32[2,64,128]{2,1,0:T(8,128)S(1)}, u32[]{:S(2)}, u32[]{:S(2)}) %collective-permute-start.8) | collective-permute-done | bytes 65568 | tf_op jit(solution)/shard_map/ppermute | solution.py:372
  41.2 0.3 collective-permute-done.9
  41.6 2.6 %collective-permute-start.10 = (bf16[2,64,128]{2,1,0:T(8,128)(2,1)S(1)}, bf16[2,64,128]{2,1,0:T(8,128)(2,1)S(1)}, u32[]{:S(2)}, u32[]{:S(2)}) collective-permute-start(bf16[2,64,128]{2,1,0:T(8,128)(2,1)S(1)} %add_convert_fusion), channel_id=1, source_target_pairs={{0,2},{1,3},{2,0},{3,1},{4,6},{5,7},{6,4},{7,5},{8,10},{9,11},{10,... | collective-permute-start | bytes 98312 | tf_op jit(solution)/shard_map/ppermute | solution.py:372
  44.2 0.7 %collective-permute-start.11 = (bf16[2,64,128]{2,1,0:T(8,128)(2,1)S(1)}, bf16[2,64,128]{2,1,0:T(8,128)(2,1)S(1)}, u32[]{:S(2)}, u32[]{:S(2)}) collective-permute-start(bf16[2,64,128]{2,1,0:T(8,128)(2,1)S(1)} %add_convert_fusion), channel_id=1, source_target_pairs={{0,3},{1,2},{2,1},{3,0},{4,7},{5,6},{6,5},{7,4},{8,11},{9,10},{10,... | collective-permute-start | bytes 98312 | tf_op jit(solution)/shard_map/ppermute | solution.py:372
  44.9 0.4 collective-permute-start.12
  45.4 2.7 %grad_inputs.1 = bf16[256,2048]{1,0:T(8,128)(2,1)} custom-call(s32[1]{0:T(128)} %bitcast.core_ref, f32[16,64,128]{2,1,0:T(8,128)S(1)} %get-tuple-element.101.own_b.own, f32[16,64,128]{2,1,0:T(8,128)S(1)} %collective-permute-done.6.other_b.other, f32[256,2048]{1,0:T(8,128)S(1)} %copy-done.2, bf16[256,128]{1,0:T(8,128)(2,1)S(1)} %copy-done.4, ...), custom_call_target="tpu_custom_call" | custom-call | flops 268435456 | bytes 4194304 | tf_op jit(solution)/shard_map/grad_inputs/pallas_call | solution.py:622
  48.1 1.8 %collective-permute-done.11 = bf16[2,64,128]{2,1,0:T(8,128)(2,1)S(1)} collective-permute-done((bf16[2,64,128]{2,1,0:T(8,128)(2,1)S(1)}, bf16[2,64,128]{2,1,0:T(8,128)(2,1)S(1)}, u32[]{:S(2)}, u32[]{:S(2)}) %collective-permute-start.11) | collective-permute-done | bytes 32800 | tf_op jit(solution)/shard_map/ppermute | solution.py:372
  50.0 0.7 %fusion.39 = (bf16[4,1,64,128]{3,2,0,1:T(8,128)(2,1)}, bf16[4,1,64,128]{3,2,0,1:T(8,128)(2,1)}) fusion(bf16[4,2,64,128]{3,2,0,1:T(8,128)(2,1)S(1)} %bitcast_dynamic-update-slice_fusion), kind=kLoop, calls=%fused_computation.95 | loop fusion | bytes 262144 | tf_op jit(solution)/shard_map/slice | solution.py:658
  (38 shorter events, 0.4 us)
Async XLA Ops:
  5.3 1.9 %copy-start.8 = (f32[8,16,128]{2,1,0:T(8,128)S(1)}, f32[8,16,128]{2,1,0:T(8,128)}, u32[]{:S(2)}) copy-start(f32[8,16,128]{2,1,0:T(8,128)} %get-tuple-element.46) | copy-start | bytes 196612
  5.4 3.2 %collective-permute-start.1 = (f32[16,128,128]{2,1,0:T(8,128)}, f32[16,128,128]{2,1,0:T(8,128)S(1)}, u32[]{:S(2)}, u32[]{:S(2)}) collective-permute-start(f32[16,128,128]{2,1,0:T(8,128)} %get-tuple-element.50), channel_id=1, source_target_pairs={{0,4},{4,0},{8,12},{12,8},{16,20},{20,16},{24,28},{28,24},{1,5},{5... | collective-permute-start | bytes 3145736 | tf_op jit(solution)/shard_map/ppermute | solution.py:372
  5.9 2.6 %collective-permute-start = (f32[8,16,128]{2,1,0:T(8,128)}, f32[8,16,128]{2,1,0:T(8,128)S(1)}, u32[]{:S(2)}, u32[]{:S(2)}) collective-permute-start(f32[8,16,128]{2,1,0:T(8,128)} %get-tuple-element.46), channel_id=1, source_target_pairs={{0,4},{4,0},{8,12},{12,8},{16,20},{20,16},{24,28},{28,24},{1,5},{5... | collective-permute-start | bytes 196616 | tf_op jit(solution)/shard_map/ppermute | solution.py:372
  9.1 14.4 %collective-permute-start.2 = (f16[1072,128]{1,0:T(8,128)(2,1)S(1)}, f16[1072,128]{1,0:T(8,128)(2,1)S(1)}, u32[]{:S(2)}, u32[]{:S(2)}) collective-permute-start(f16[1072,128]{1,0:T(8,128)(2,1)S(1)} %get-tuple-element.51), channel_id=1, source_target_pairs={{0,8},{4,12},{8,0},{12,4},{16,24},{20,28},{24,16},{28,20},{1,9},{5... | collective-permute-start | bytes 823304 | tf_op jit(solution)/shard_map/ppermute | solution.py:372
  12.0 14.2 %collective-permute-start.3 = (f16[1072,128]{1,0:T(8,128)(2,1)S(1)}, f16[1072,128]{1,0:T(8,128)(2,1)S(1)}, u32[]{:S(2)}, u32[]{:S(2)}) collective-permute-start(f16[1072,128]{1,0:T(8,128)(2,1)S(1)} %get-tuple-element.52), channel_id=1, source_target_pairs={{0,16},{4,20},{8,24},{12,28},{16,0},{20,4},{24,8},{28,12},{1,17},{... | collective-permute-start | bytes 823304 | tf_op jit(solution)/shard_map/ppermute | solution.py:372
  13.6 12.7 %collective-permute-start.4 = (f16[1072,128]{1,0:T(8,128)(2,1)S(1)}, f16[1072,128]{1,0:T(8,128)(2,1)S(1)}, u32[]{:S(2)}, u32[]{:S(2)}) collective-permute-start(f16[1072,128]{1,0:T(8,128)(2,1)S(1)} %get-tuple-element.52), channel_id=1, source_target_pairs={{0,24},{4,28},{8,16},{12,20},{16,8},{20,12},{24,0},{28,4},{1,25},{... | collective-permute-start | bytes 823304 | tf_op jit(solution)/shard_map/ppermute | solution.py:372
  26.9 2.8 %copy-start = (bf16[256,2048]{1,0:T(8,128)(2,1)S(1)}, bf16[256,2048]{1,0:T(8,128)(2,1)}, u32[]{:S(2)}) copy-start(bf16[256,2048]{1,0:T(8,128)(2,1)} %x_ref.3) | copy-start | bytes 3145732
  26.9 2.8 %copy-start.1 = (bf16[256,2048]{1,0:T(8,128)(2,1)S(1)}, bf16[256,2048]{1,0:T(8,128)(2,1)}, u32[]{:S(2)}) copy-start(bf16[256,2048]{1,0:T(8,128)(2,1)} %g_ref.3) | copy-start | bytes 3145732
  26.9 2.7 %copy-start.4 = (bf16[256,128]{1,0:T(8,128)(2,1)S(1)}, bf16[256,128]{1,0:T(8,128)(2,1)}, u32[]{:S(2)}) copy-start(bf16[256,128]{1,0:T(8,128)(2,1)} %get-tuple-element.69.edges_ref) | copy-start | bytes 196612
  26.9 2.0 %collective-permute-start.5 = (f32[16,64,128]{2,1,0:T(8,128)S(1)}, f32[16,64,128]{2,1,0:T(8,128)S(1)}, u32[]{:S(2)}, u32[]{:S(2)}) collective-permute-start(f32[16,64,128]{2,1,0:T(8,128)S(1)} %get-tuple-element.64), channel_id=1, source_target_pairs={{0,4},{4,0},{8,12},{12,8},{16,20},{20,16},{24,28},{28,24},{1,5},{5... | collective-permute-start | bytes 1572872 | tf_op jit(solution)/shard_map/ppermute | solution.py:372
  27.0 2.6 %collective-permute-start.6 = (f32[16,64,128]{2,1,0:T(8,128)S(1)}, f32[16,64,128]{2,1,0:T(8,128)S(1)}, u32[]{:S(2)}, u32[]{:S(2)}) collective-permute-start(f32[16,64,128]{2,1,0:T(8,128)S(1)} %get-tuple-element.68), channel_id=1, source_target_pairs={{0,4},{4,0},{8,12},{12,8},{16,20},{20,16},{24,28},{28,24},{1,5},{5... | collective-permute-start | bytes 1572872 | tf_op jit(solution)/shard_map/ppermute | solution.py:372
  29.6 2.5 %copy-start.7 = (f32[4,2,64,128]{3,2,1,0:T(8,128)S(1)}, f32[4,2,64,128]{3,2,1,0:T(8,128)}, u32[]{:S(2)}) copy-start(f32[4,2,64,128]{3,2,1,0:T(8,128)} %get-tuple-element.70) | copy-start | bytes 786436
  29.7 6.7 %copy-start.5 = (bf16[256,128]{1,0:T(8,128)(2,1)S(1)}, bf16[256,128]{1,0:T(8,128)(2,1)}, u32[]{:S(2)}) copy-start(bf16[256,128]{1,0:T(8,128)(2,1)} %proj_ref.2) | copy-start | bytes 196612
  32.2 8.5 %collective-permute-start.7 = (f32[2,64,128]{2,1,0:T(8,128)S(1)}, f32[2,64,128]{2,1,0:T(8,128)S(1)}, u32[]{:S(2)}, u32[]{:S(2)}) collective-permute-start(f32[2,64,128]{2,1,0:T(8,128)S(1)} %get-tuple-element.71), channel_id=1, source_target_pairs={{0,2},{1,3},{2,0},{3,1},{4,6},{5,7},{6,4},{7,5},{8,10},{9,11},{10,... | collective-permute-start | bytes 196616 | tf_op jit(solution)/shard_map/ppermute | solution.py:372
  34.8 6.4 %collective-permute-start.8 = (f32[2,64,128]{2,1,0:T(8,128)S(1)}, f32[2,64,128]{2,1,0:T(8,128)S(1)}, u32[]{:S(2)}, u32[]{:S(2)}) collective-permute-start(f32[2,64,128]{2,1,0:T(8,128)S(1)} %get-tuple-element.72), channel_id=1, source_target_pairs={{0,3},{1,2},{2,1},{3,0},{4,7},{5,6},{6,5},{7,4},{8,11},{9,10},{10,... | collective-permute-start | bytes 196616 | tf_op jit(solution)/shard_map/ppermute | solution.py:372
  36.2 5.4 %collective-permute-start.9 = (f32[2,64,128]{2,1,0:T(8,128)S(1)}, f32[2,64,128]{2,1,0:T(8,128)S(1)}, u32[]{:S(2)}, u32[]{:S(2)}) collective-permute-start(f32[2,64,128]{2,1,0:T(8,128)S(1)} %get-tuple-element.73), channel_id=1, source_target_pairs={{0,1},{1,0},{2,3},{3,2},{4,5},{5,4},{6,7},{7,6},{8,9},{9,8},{10,11... | collective-permute-start | bytes 196616 | tf_op jit(solution)/shard_map/ppermute | solution.py:372
  36.4 1.6 %copy-start.3 = (f32[256,2048]{1,0:T(8,128)S(1)}, f32[256,2048]{1,0:T(8,128)}, u32[]{:S(2)}) copy-start(f32[256,2048]{1,0:T(8,128)} %get-tuple-element.75.base_ref) | copy-start | bytes 6291460
  38.0 7.4 %copy-start.2 = (f32[256,2048]{1,0:T(8,128)S(1)}, f32[256,2048]{1,0:T(8,128)}, u32[]{:S(2)}) copy-start(f32[256,2048]{1,0:T(8,128)} %get-tuple-element.83.base_ref) | copy-start | bytes 6291460
  38.0 7.4 %copy-start.6 = (bf16[256,128]{1,0:T(8,128)(2,1)S(1)}, bf16[256,128]{1,0:T(8,128)(2,1)}, u32[]{:S(2)}) copy-start(bf16[256,128]{1,0:T(8,128)(2,1)} %proj_ref.3) | copy-start | bytes 196612
  41.6 6.5 %collective-permute-start.10 = (bf16[2,64,128]{2,1,0:T(8,128)(2,1)S(1)}, bf16[2,64,128]{2,1,0:T(8,128)(2,1)S(1)}, u32[]{:S(2)}, u32[]{:S(2)}) collective-permute-start(bf16[2,64,128]{2,1,0:T(8,128)(2,1)S(1)} %add_convert_fusion), channel_id=1, source_target_pairs={{0,2},{1,3},{2,0},{3,1},{4,6},{5,7},{6,4},{7,5},{8,10},{9,11},{10,... | collective-permute-start | bytes 98312 | tf_op jit(solution)/shard_map/ppermute | solution.py:372
  44.2 5.7 %collective-permute-start.11 = (bf16[2,64,128]{2,1,0:T(8,128)(2,1)S(1)}, bf16[2,64,128]{2,1,0:T(8,128)(2,1)S(1)}, u32[]{:S(2)}, u32[]{:S(2)}) collective-permute-start(bf16[2,64,128]{2,1,0:T(8,128)(2,1)S(1)} %add_convert_fusion), channel_id=1, source_target_pairs={{0,3},{1,2},{2,1},{3,0},{4,7},{5,6},{6,5},{7,4},{8,11},{9,10},{10,... | collective-permute-start | bytes 98312 | tf_op jit(solution)/shard_map/ppermute | solution.py:372
  44.9 5.0 %collective-permute-start.12 = (bf16[2,64,128]{2,1,0:T(8,128)(2,1)S(1)}, bf16[2,64,128]{2,1,0:T(8,128)(2,1)S(1)}, u32[]{:S(2)}, u32[]{:S(2)}) collective-permute-start(bf16[2,64,128]{2,1,0:T(8,128)(2,1)S(1)} %add_convert_fusion), channel_id=1, source_target_pairs={{0,1},{1,0},{2,3},{3,2},{4,5},{5,4},{6,7},{7,6},{8,9},{9,8},{10,11... | collective-permute-start | bytes 98312 | tf_op jit(solution)/shard_map/ppermute | solution.py:372
